TPU v7x, 32 devices: a whole 2x2x4 slice. The times are simulated.
32 devices in a mesh: dp: 4 (over x, core), expert: 8 (over z, y).
Axes of the slice: x: 2, y: 2, z: 4, core: 2. Of those that a mesh axis runs over, the one named last changes fastest.
Arguments:
- grad_partials: bfloat16 [4, 7168, 8192], P('dp', None, 'expert'), may hold values from -6 to 6
- master_weights: float32 [7168, 8192], P('dp', 'expert'), may hold values from -0.3125 to 0.3125
- first_moment: float32 [7168, 8192], P('dp', 'expert'), may hold values from -2 to 2
- second_moment: float32 [7168, 8192], P('dp', 'expert'), may hold values from 0.02 to 0.5
- resident_weights: bfloat16 [7168, 16384], P('dp', 'expert'), may hold values from -0.6 to 0.6
- token_tiles: bfloat16 [8192, 7168], P('expert', 'dp'), may hold values from -6 to 6
- owner_expert: int32 [8], replicated, may hold values from 0 to 3, as said below
- live_rows: int32 [8], P('expert'), may hold values from 256 to 1024, as said below
Outputs:
- updated_master: float32 [7168, 8192], P('dp', 'expert')
- projected: bfloat16 [8192, 2048], P('expert', 'dp')
Inputs may be any that keep to these rules, and one draw needn't show every extreme that they name: `owner_expert`: each owner hosts one of the 4 experts; every expert is hosted by at least one owner, some by several. The first live_rows[o] of owner o's rows are live; some owner has all 1024 rows live.
All inputs are finite; a program needn't handle non-finite values.
Results may differ from a plain program's by a relative error of at most 0.035.
Values may be sent and summed in bfloat16 or wider, within the bound.
No kernel may reach another device: no remote copies, remote signals or barrier semaphores. Data moves between devices by JAX's collectives and lax.ppermute only.
A program may use at most 192 MiB of HBM per device.

v0:
```python
import jax
import jax.numpy as jnp
from jax import lax
from jax.experimental import pallas as pl
from jax.experimental.pallas import tpu as pltpu
from jax.sharding import PartitionSpec as P


EXPERTS = 4
QB = 128

beta_first = 0.9
beta_second = 0.95
learn_rate = 0.02
decay_rate = 0.1
adam_epsilon = 1e-08
scale_epsilon = 1e-06
quant_range = 448.0
grid_step = 8.0
bias_first = 1.0 - 0.9**20
bias_second = 1.0 - 0.95**20

ROW_PARTS = 2
TILE = 1024
UNROLL = 7
ADAM_SPLIT = 1
SUM_VMEM = 50 << 20
PICK_VMEM = 16 << 20
ADAM_VMEM = 58 << 20
SERVE_VMEM = 50 << 20


def adamw(gradient, master_weights, first_moment, second_moment):
    moment_one = beta_first * first_moment + (1.0 - beta_first) * gradient
    moment_two = beta_second * second_moment + (1.0 - beta_second) * gradient * gradient
    update = (moment_one * (1.0 / bias_first)) / (
        jnp.sqrt(moment_two * (1.0 / bias_second)) + adam_epsilon
    )
    return master_weights - learn_rate * (update + decay_rate * master_weights)


def params(limit):
    return pltpu.CompilerParams(vmem_limit_bytes=limit)


def total(refs):
    value = refs[0].astype(jnp.float32)
    for ref in refs[1:]:
        value = value + ref.astype(jnp.float32)
    return value


def slab_sum(grad, table, relative, received, rows, part_rows, part, cols, width):
    n_out = len(relative)
    skip = relative[1] - relative[0] if n_out > 1 else 0
    n_cols = len(cols)
    block = part_rows
    step = rows // block
    n_rows = part_rows // block

    def kernel(tab, *refs):
        grads, recs, out = refs[:n_cols], refs[n_cols:-1], refs[-1]
        for k in range(n_cols):
            span = slice(k * width, (k + 1) * width)
            values = [grads[k][...]] + [rec[0, :, span] for rec in recs]
            out[0, :, span] = total(values).astype(out.dtype)

    def grad_map(k):
        at = cols[k] // width
        return lambda i, r, tab: (tab[relative[0] + i * skip] * step + part * n_rows + r, at)

    def rec_map(stride, offset, first):
        return lambda i, r, tab: (first + i * stride, offset * n_rows + r, 0)

    in_specs = [pl.BlockSpec((block, width), grad_map(k)) for k in range(n_cols)]
    in_specs += [
        pl.BlockSpec((1, block, n_cols * width), rec_map(stride, offset, first))
        for (_, offset, first, stride) in received
    ]
    moved = n_out * part_rows * n_cols * width * 2
    return pl.pallas_call(
        kernel,
        grid_spec=pltpu.PrefetchScalarGridSpec(
            num_scalar_prefetch=1,
            grid=(n_out, n_rows),
            in_specs=in_specs,
            out_specs=pl.BlockSpec((1, block, n_cols * width), lambda i, r, tab: (i, r, 0)),
        ),
        out_shape=jax.ShapeDtypeStruct((n_out, part_rows, n_cols * width), jnp.bfloat16),
        compiler_params=params(SUM_VMEM),
        cost_estimate=pl.CostEstimate(
            flops=moved, bytes_accessed=moved * (2 + len(received)), transcendentals=0
        ),
        name="slab_sum",
    )(table, *([grad] * n_cols), *[item[0] for item in received])


def adam_part(grad, table, received, state, out, rows, part_rows, part, cols, width):
    n_cols = len(cols)
    block = part_rows // ADAM_SPLIT if part_rows % (ADAM_SPLIT * 16) == 0 else part_rows
    step = rows // block
    n_rows = part_rows // block
    base = cols[0] // width
    stride = (cols[1] - cols[0]) // width if n_cols > 1 else 0
    n_rec = len(received)

    def kernel(tab, grad_ref, *refs):
        recs = refs[:n_rec]
        master, first, second = refs[n_rec : n_rec + 3]
        new_ref, delta_ref = refs[-2:]
        gradient = total([grad_ref[...]] + [rec[0] for rec in recs])
        old = master[...]
        new = adamw(gradient, old, first[...], second[...])
        new_ref[...] = new
        delta_ref[...] = (new - old).astype(delta_ref.dtype)

    def state_map(r, k, tab):
        return (part * n_rows + r, base + k * stride)

    state_spec = pl.BlockSpec((block, width), state_map)
    in_specs = [
        pl.BlockSpec(
            (block, width), lambda r, k, tab: (tab[0] * step + part * n_rows + r, base + k * stride)
        )
    ]

    def rec_map(offset):
        return lambda r, k, tab: (0, offset * n_rows + r, k)

    in_specs += [pl.BlockSpec((1, block, width), rec_map(offset)) for (_, offset) in received]
    in_specs += [state_spec] * 3
    operands = [table, grad, *[item[0] for item in received], *state]
    aliases = {}
    if out is not None:
        in_specs.append(pl.BlockSpec(memory_space=pl.ANY))
        aliases = {len(operands): 0}
        operands.append(out)
    count = part_rows * n_cols * width
    return pl.pallas_call(
        kernel,
        grid_spec=pltpu.PrefetchScalarGridSpec(
            num_scalar_prefetch=1,
            grid=(n_rows, n_cols),
            in_specs=in_specs,
            out_specs=(
                state_spec,
                pl.BlockSpec((block, width), lambda r, k, tab: (r, k)),
            ),
        ),
        out_shape=(
            jax.ShapeDtypeStruct(state[0].shape, jnp.float32),
            jax.ShapeDtypeStruct((part_rows, n_cols * width), jnp.bfloat16),
        ),
        input_output_aliases=aliases,
        compiler_params=params(ADAM_VMEM),
        cost_estimate=pl.CostEstimate(
            flops=30 * count, bytes_accessed=(20 + 2 * n_rec) * count, transcendentals=2 * count
        ),
        name="adam_part",
    )(*operands)


def pick(table, code_of, options):
    shape = options[0].shape

    def kernel(tab, *refs):
        out, sem = refs[-2:]
        code = code_of(tab)
        for k in range(len(options)):

            @pl.when(code == k)
            def _():
                copy = pltpu.make_async_copy(refs[k], out, sem)
                copy.start()
                copy.wait()

    return pl.pallas_call(
        kernel,
        grid_spec=pltpu.PrefetchScalarGridSpec(
            num_scalar_prefetch=1,
            grid=(1,),
            in_specs=[pl.BlockSpec(memory_space=pl.ANY)] * len(options),
            out_specs=pl.BlockSpec(shape, lambda i, tab: (0, 0)),
            scratch_shapes=[pltpu.SemaphoreType.DMA],
        ),
        out_shape=jax.ShapeDtypeStruct(shape, options[0].dtype),
        compiler_params=params(PICK_VMEM),
        cost_estimate=pl.CostEstimate(
            flops=0, bytes_accessed=4 * shape[0] * shape[1], transcendentals=0
        ),
        name="pick",
    )(table, *options)


def serve_piece(tokens, resident, parts, code_of, table, places, stride, shift, width):
    rows_total, depth = tokens.shape
    n_parts = len(parts)
    n_options = len(parts[0])
    part_rows, part_cols = parts[0][0].shape
    n_cols = part_cols // width
    tile = TILE if rows_total % TILE == 0 else rows_total

    def kernel(tab, tok, *refs):
        residents = refs[:n_cols]
        options = refs[n_cols : n_cols + n_parts * n_options]
        out, weight, delta, sems = refs[-4:]
        code = code_of(tab)
        for k in range(n_options):

            @pl.when(code == k)
            def _():
                copies = [
                    pltpu.make_async_copy(options[h * n_options + k], delta.at[h], sems.at[h])
                    for h in range(n_parts)
                ]
                for copy in copies:
                    copy.start()
                for copy in copies:
                    copy.wait()

        starts = [
            pl.multiple_of(lax.rem(tab[places[k]], n_cols) * width, width) for k in range(n_cols)
        ]
        for h in range(n_parts):

            @pl.loop(0, part_rows // QB, unroll=UNROLL)
            def _(b):
                at = pl.multiple_of(h * part_rows + b * QB, QB)
                near = pl.multiple_of(b * QB, QB)
                for k in range(n_cols):
                    for c in range(width // QB):
                        span = slice(c * QB, (c + 1) * QB)
                        change = delta[h, pl.ds(near, QB), pl.ds(starts[k] + c * QB, QB)]
                        value = residents[k][pl.ds(at, QB), span].astype(
                            jnp.float32
                        ) + change.astype(jnp.float32)
                        largest = jnp.max(jnp.abs(value), axis=(0, 1), keepdims=True)
                        scale = (largest + scale_epsilon) / quant_range
                        level = jnp.floor(value * (1.0 / (scale * grid_step)) + 0.5)
                        weight[pl.ds(at, QB), k * width + c * QB : k * width + (c + 1) * QB] = (
                            level * (scale * grid_step)
                        ).astype(jnp.bfloat16)

        @pl.loop(0, rows_total // tile)
        def _(m):
            at = pl.multiple_of(m * tile, tile)
            product = jnp.dot(
                tok[pl.ds(at, tile), :], weight[...], preferred_element_type=jnp.float32
            )
            for k in range(n_cols):
                out[k, pl.ds(at, tile), :] = product[:, k * width : (k + 1) * width].astype(
                    jnp.bfloat16
                )

    def res_map(k):
        return lambda i, tab: (0, tab[places[k]] * stride + shift)

    in_specs = [pl.BlockSpec((rows_total, depth), lambda i, tab: (0, 0))]
    in_specs += [pl.BlockSpec((depth, width), res_map(k)) for k in range(n_cols)]
    in_specs += [pl.BlockSpec(memory_space=pl.ANY)] * (n_parts * n_options)
    operands = [tokens] + [resident] * n_cols + [option for part in parts for option in part]
    return pl.pallas_call(
        kernel,
        grid_spec=pltpu.PrefetchScalarGridSpec(
            num_scalar_prefetch=1,
            grid=(1,),
            in_specs=in_specs,
            out_specs=pl.BlockSpec((n_cols, rows_total, width), lambda i, tab: (0, 0, 0)),
            scratch_shapes=[
                pltpu.VMEM((depth, n_cols * width), jnp.bfloat16),
                pltpu.VMEM((n_parts, part_rows, part_cols), jnp.bfloat16),
                pltpu.SemaphoreType.DMA((n_parts,)),
            ],
        ),
        out_shape=jax.ShapeDtypeStruct((n_cols, rows_total, width), jnp.bfloat16),
        compiler_params=params(SERVE_VMEM),
        cost_estimate=pl.CostEstimate(
            flops=2 * rows_total * depth * n_cols * width,
            bytes_accessed=2 * depth * (rows_total + 2 * n_cols * width),
            transcendentals=0,
        ),
        name="serve_piece",
    )(table, *operands)


def make_table(me, own, owner_expert, n_dp, group, n_cols, two_slots):
    place_at = n_dp
    code_at = place_at + group * n_cols
    flag_at = code_at + group
    last = EXPERTS - 1

    def kernel(here, hosts, out):
        me = here[0]
        plane = lax.div(here[1], group)
        lane = lax.rem(here[1], group)
        for r in range(n_dp):
            out[r] = jnp.bitwise_xor(me, r)
        for s in range(group):
            piece = lax.rem(lane + group - s, group)
            for k in range(n_cols):
                column = jnp.bitwise_xor(jnp.bitwise_and(me, n_cols - 1), k)
                out[place_at + s * n_cols + k] = piece * n_cols + column
        outer = jnp.where(plane < EXPERTS // 2, 0, last)
        inner = jnp.where(plane < EXPERTS // 2, 1, last - 1)
        near = jnp.int32(0)
        far = jnp.int32(0)
        for j in range(group):
            host = hosts[outer * group + j]
            near = jnp.where(host == inner, 1, near)
            far = jnp.where(host == last - outer, 1, far)
        at_end = jnp.where(plane == outer, 1, 0)
        for s in range(group):
            expert = hosts[plane * group + lax.rem(lane + s, group)]
            if two_slots:
                first = jnp.where(near == 1, inner, last - inner)
                code_end = jnp.where(expert == first, 2, 3)
                code_mid = jnp.where(expert == outer, 1, jnp.where(expert == last - plane, 4, 5))
                code = jnp.where(at_end == 1, code_end, code_mid)
            else:
                code = jnp.where(expert < plane, plane - expert, last + expert - plane)
            out[code_at + s] = jnp.where(expert == plane, 0, code)
        out[flag_at] = near
        out[flag_at + 1] = far
        out[flag_at + 2] = at_end
        out[flag_at + 3] = jnp.where(lane == lax.div(me, 2), 1, 0)

    table = pl.pallas_call(
        kernel,
        in_specs=[pl.BlockSpec(memory_space=pltpu.SMEM)] * 2,
        out_specs=pl.BlockSpec(memory_space=pltpu.SMEM),
        out_shape=jax.ShapeDtypeStruct((flag_at + 4,), jnp.int32),
        name="make_table",
    )(jnp.stack([me, own]).astype(jnp.int32), owner_expert)
    return table, place_at, code_at, flag_at


def body(
    grad_partials,
    master_weights,
    first_moment,
    second_moment,
    resident_weights,
    token_tiles,
    owner_expert,
    live_rows,
):
    n_dp = lax.axis_size("dp")
    n_expert = lax.axis_size("expert")
    group = n_expert // EXPERTS
    me = lax.axis_index("dp")
    own = lax.axis_index("expert")
    lane = own % group
    levels = n_dp.bit_length() - 1
    assert 1 << levels == n_dp and EXPERTS * group == n_expert

    rows, piece_cols = master_weights.shape
    owner_cols = resident_weights.shape[1]
    dp_cols = owner_cols // n_dp
    n_cols = piece_cols // dp_cols
    assert n_cols in (1, 2) and n_cols * dp_cols == piece_cols
    width = QB
    n_chunks = dp_cols // width
    parts = ROW_PARTS if rows % (ROW_PARTS * QB) == 0 else 1
    part_rows = rows // parts
    grad = grad_partials.reshape(n_dp * rows, piece_cols)
    state = (master_weights, first_moment, second_moment)

    two_slots = EXPERTS == 4 and group == 2
    table, place_at, code_at, flag_at = make_table(
        me, own, owner_expert, n_dp, group, n_cols, two_slots
    )

    def flip(value, level):
        pairs = [(i, i ^ (1 << level)) for i in range(n_dp)]
        return lax.ppermute(value, "dp", pairs)

    def along(value, moves):
        pairs = [(a * group + j, b * group + j) for (a, b) in moves for j in range(group)]
        return lax.ppermute(value, "expert", pairs)

    columns = [[k * dp_cols + c * width for k in range(n_cols)] for c in range(n_chunks)]
    updated_master = None
    delta = [[None] * n_chunks for _ in range(parts)]

    def relative(level):
        return [(1 << level) + i * (2 << level) for i in range(n_dp >> (level + 1))]

    core_recs = []
    for c in range(n_chunks):
        send = slab_sum(grad, table, relative(0), [], rows, rows, 0, columns[c], width)
        core_recs.append(flip(send, 0))
    for c in range(n_chunks):
        for h in range(parts):
            received = [(core_recs[c], h)]
            for level in range(1, levels):
                feed = []
                for j, (array, offset) in enumerate(received):
                    feed.append((array, offset, (1 << level) >> (j + 1), (2 << level) >> (j + 1)))
                send = slab_sum(
                    grad, table, relative(level), feed, rows, part_rows, h, columns[c], width
                )
                received.append((flip(send, level), 0))
            updated_master, delta[h][c] = adam_part(
                grad,
                table,
                received,
                state,
                updated_master,
                rows,
                part_rows,
                h,
                columns[c],
                width,
            )

    last = EXPERTS - 1

    def at(index):
        return lambda tab: tab[index]

    def full_line(pieces):
        found = []
        for piece in pieces:
            options = [piece]
            for side in range(2):
                value = piece
                for k in range(1, EXPERTS):
                    moves = [(p, p + 1) for p in range(k - 1, last)]
                    if side:
                        moves = [(last - a, last - b) for a, b in moves]
                    value = along(value, moves)
                    options.append(value)
            found.append(options)
        return found

    def slotted_line(pieces):
        sides = [(0, 1), (1, 0), (2, 3), (3, 2)]
        middle = [(1, 2), (2, 1)]
        count = len(pieces)
        side, center = [], []

        def odd_code(tab):
            return 1 - tab[flag_at]

        def even_code(tab):
            return jnp.where(tab[flag_at + 2] == 1, 2, tab[flag_at + 1])

        def last_code(tab):
            return tab[flag_at + 1]

        for t in range(2 * count + 1):
            c = t // 2
            if t == 0:
                value = pieces[0]
            else:
                if t % 2:
                    value = pick(table, odd_code, [pieces[c], center[2 * c]])
                elif c < count:
                    value = pick(table, even_code, [center[t - 2], center[t - 1], pieces[c]])
                else:
                    value = pick(table, last_code, [center[t - 2], center[t - 1]])
            side.append(along(value, sides))
            if t < 2 * count:
                center.append(along(side[t - 1] if t % 2 else pieces[c], middle))
        return [
            [pieces[c], *side[2 * c : 2 * c + 3], *center[2 * c : 2 * c + 2]] for c in range(count)
        ]

    if two_slots:
        options = [slotted_line(delta[h]) for h in range(parts)]
    else:
        options = [full_line(delta[h]) for h in range(parts)]

    moved = [[[None] * parts for _ in range(n_chunks)] for _ in range(group)]
    for c in range(n_chunks):
        for h in range(parts):
            for s in range(1, group):
                value = pick(table, at(code_at + s), options[h][c])
                pairs = [
                    (e * group + j, e * group + (j + s) % group)
                    for e in range(EXPERTS)
                    for j in range(group)
                ]
                moved[s][c][h] = lax.ppermute(value, "expert", pairs)

    sums = []
    parity = (me % 2).astype(jnp.int32)
    for c in range(n_chunks):
        products = []
        for s in range(group):
            if s == 0:
                sources, code_of = [options[h][c] for h in range(parts)], at(code_at)
            else:
                sources, code_of = [[moved[s][c][h]] for h in range(parts)], lambda tab: 0
            products.append(
                serve_piece(
                    token_tiles,
                    resident_weights,
                    sources,
                    code_of,
                    table,
                    [place_at + s * n_cols + k for k in range(n_cols)],
                    n_chunks,
                    c,
                    width,
                )
            )
        if n_dp == 4 and group == 2:
            stacked = jnp.stack([product[1] for product in products])
            crossed = flip(stacked, 0)
            kept = [
                products[s][0].astype(jnp.float32) + crossed[s].astype(jnp.float32)
                for s in range(2)
            ]
            straight = table[flag_at + 3] == 1
            other = jnp.where(straight, kept[1], kept[0]).astype(jnp.bfloat16)
            held = jnp.where(straight, kept[0], kept[1])
            crossed = flip(other, 1)
            sums.append(held + crossed.astype(jnp.float32))
        else:
            buffer = jnp.zeros((n_dp,) + products[0].shape[1:], jnp.bfloat16)
            for s in range(group):
                piece = (lane - s) % group
                for k in range(n_cols):
                    column = piece * n_cols + ((k ^ parity) if n_cols == 2 else 0)
                    buffer = lax.dynamic_update_index_in_dim(
                        buffer, products[s][k], jnp.bitwise_xor(column, me), 0
                    )
            for level in range(levels):
                got = flip(buffer[1::2], level).astype(jnp.float32)
                buffer = (buffer[0::2].astype(jnp.float32) + got).astype(
                    jnp.bfloat16 if level < levels - 1 else jnp.float32
                )
            sums.append(buffer[0])
    summed = jnp.concatenate(sums, axis=1)
    row_index = lax.broadcasted_iota(jnp.int32, summed.shape, 0)
    projected = jnp.where(row_index < live_rows[0], summed, jnp.float32(0.0)).astype(jnp.bfloat16)
    return (updated_master, projected)


def solution(mesh):
    placed = (
        P("dp", None, "expert"),
        P("dp", "expert"),
        P("dp", "expert"),
        P("dp", "expert"),
        P("dp", "expert"),
        P("expert", "dp"),
        P(),
        P("expert"),
    )

    return jax.shard_map(
        body,
        mesh=mesh,
        in_specs=placed,
        out_specs=(P("dp", "expert"), P("expert", "dp")),
        check_vma=False,
    )
```

profile of v0, /device:TPU:0, one launch (start us, length us, event | category | flops | bytes accessed | tf_op | source)
XLA Modules:
  0.0 328.5 jit_solution(14820382184795323850)
XLA Ops:
  3.1 2.2 slab_sum.21
  5.9 2.2 slab_sum.18
  8.2 3.2 slab_sum.15
  11.9 1.8 slab_sum.23
  13.7 2.6 collective-permute-start.11
  16.2 3.1 slab_sum.12
  19.6 1.7 slab_sum.22
  21.7 2.6 slab_sum.20
  24.3 1.7 collective-permute-start.8
  26.0 2.5 slab_sum.19
  30.4 4.2 %adam_part.8 = (f32[1792,1024]{1,0:T(8,128)}, bf16[896,256]{1,0:T(8,128)(2,1)}) custom-call(s32[14]{0:T(128)} %make_table.1.tab, bf16[7168,1024]{1,0:T(8,128)(2,1)} %bitcast.38, bf16[2,1792,256]{2,1,0:T(8,128)(2,1)} %copy-done.3, bf16[1,896,256]{2,1,0:T(8,128)(2,1)} %copy-done.54, f32[1792,1024]{1,0:T(8,128)} %refs_2_.15, f32[1792,1024]{1,0:T(8,128)} %refs_3_.15, ...), custom_call_target="tpu_custom_call" | custom-call | flops 6881280 | bytes 5505024 | tf_op jit(solution)/shard_map/adam_part/pallas_call | solution.py:139
  34.6 2.9 collective-permute-done.10.refs_1_
  37.6 4.4 %adam_part.9 = (f32[1792,1024]{1,0:T(8,128)}, bf16[896,256]{1,0:T(8,128)(2,1)}) custom-call(s32[14]{0:T(128)} %make_table.1.tab, bf16[7168,1024]{1,0:T(8,128)(2,1)} %bitcast.39, bf16[2,1792,256]{2,1,0:T(8,128)(2,1)} %copy-done.3, bf16[1,896,256]{2,1,0:T(8,128)(2,1)} %collective-permute-done.10.refs_1_, ...), custom_call_target="tpu_custom_call", output_to_operand_aliasing={{0}: (7, {})} | custom-call | flops 6881280 | bytes 5505024 | tf_op jit(solution)/shard_map/adam_part/pallas_call | solution.py:139
  41.9 2.1 collective-permute-start.17
  44.0 3.4 %collective-permute-done.8.refs_1_ = bf16[1,896,256]{2,1,0:T(8,128)(2,1)} collective-permute-done((bf16[1,896,256]{2,1,0:T(8,128)(2,1)}, bf16[1,896,256]{2,1,0:T(8,128)(2,1)}, u32[]{:S(2)}, u32[]{:S(2)}) %collective-permute-start.8) | collective-permute-done | bytes 458784 | tf_op jit(solution)/shard_map/ppermute | solution.py:375
  48.1 8.8 %collective-permute-done.7.refs_1_ = bf16[1,896,256]{2,1,0:T(8,128)(2,1)S(1)} collective-permute-done((bf16[1,896,256]{2,1,0:T(8,128)(2,1)}, bf16[1,896,256]{2,1,0:T(8,128)(2,1)S(1)}, u32[]{:S(2)}, u32[]{:S(2)}) %collective-permute-start.7) | collective-permute-done | bytes 458784 | tf_op jit(solution)/shard_map/ppermute | solution.py:375
  56.9 1.8 collective-permute-start.12
  60.2 9.2 %collective-permute-done.12.refs_3_.refs_1_ = bf16[896,256]{1,0:T(8,128)(2,1)} collective-permute-done((bf16[896,256]{1,0:T(8,128)(2,1)S(1)}, bf16[896,256]{1,0:T(8,128)(2,1)}, u32[]{:S(2)}, u32[]{:S(2)}) %collective-permute-start.12) | collective-permute-done | bytes 458784 | tf_op jit(solution)/shard_map/ppermute | solution.py:379
  70.8 4.2 %adam_part.10 = (f32[1792,1024]{1,0:T(8,128)}, bf16[896,256]{1,0:T(8,128)(2,1)}) custom-call(s32[14]{0:T(128)} %make_table.1.tab, bf16[7168,1024]{1,0:T(8,128)(2,1)} %bitcast.40, bf16[2,1792,256]{2,1,0:T(8,128)(2,1)} %copy-done.2, bf16[1,896,256]{2,1,0:T(8,128)(2,1)} %collective-permute-done.8.refs_1_, ...), custom_call_target="tpu_custom_call", output_to_operand_aliasing={{0}: (7, {})} | custom-call | flops 6881280 | bytes 5505024 | tf_op jit(solution)/shard_map/adam_part/pallas_call | solution.py:139
  75.1 4.3 %adam_part.11 = (f32[1792,1024]{1,0:T(8,128)}, bf16[896,256]{1,0:T(8,128)(2,1)}) custom-call(s32[14]{0:T(128)} %make_table.1.tab, bf16[7168,1024]{1,0:T(8,128)(2,1)} %bitcast.41, bf16[2,1792,256]{2,1,0:T(8,128)(2,1)} %copy-done.2, bf16[1,896,256]{2,1,0:T(8,128)(2,1)} %copy-done.52, f32[1792,1024]{1,0:T(8,128)} %refs_2_.15, ...), custom_call_target="tpu_custom_call", output_to_operand_aliasing={{0}: (7, {})} | custom-call | flops 6881280 | bytes 5505024 | tf_op jit(solution)/shard_map/adam_part/pallas_call | solution.py:139
  82.1 3.6 %collective-permute-start.21 = (bf16[896,256]{1,0:T(8,128)(2,1)S(1)}, bf16[896,256]{1,0:T(8,128)(2,1)S(1)}, u32[]{:S(2)}, u32[]{:S(2)}) collective-permute-start(bf16[896,256]{1,0:T(8,128)(2,1)S(1)} %pick.27), channel_id=1, source_target_pairs={{0,2},{1,3},{2,0},{3,1},{4,6},{5,7},{6,4},{7,5},{8,10},{9,11},{10,... | collective-permute-start | bytes 1376264 | tf_op jit(solution)/shard_map/ppermute | solution.py:379
  85.7 1.8 slab_sum.17
  89.9 4.6 %collective-permute-start.16 = (bf16[896,256]{1,0:T(8,128)(2,1)S(1)}, bf16[896,256]{1,0:T(8,128)(2,1)}, u32[]{:S(2)}, u32[]{:S(2)}) collective-permute-start(bf16[896,256]{1,0:T(8,128)(2,1)S(1)} %pick.25), channel_id=1, source_target_pairs={{0,2},{1,3},{2,0},{3,1},{4,6},{5,7},{6,4},{7,5},{8,10},{9,11},{10,... | collective-permute-start | bytes 1376264 | tf_op jit(solution)/shard_map/ppermute | solution.py:379
  94.5 1.7 slab_sum.16
  99.9 4.8 %collective-permute-done.16.refs_5_.refs_3_.refs_1_ = bf16[896,256]{1,0:T(8,128)(2,1)} collective-permute-done((bf16[896,256]{1,0:T(8,128)(2,1)S(1)}, bf16[896,256]{1,0:T(8,128)(2,1)}, u32[]{:S(2)}, u32[]{:S(2)}) %collective-permute-start.16) | collective-permute-done | bytes 458784 | tf_op jit(solution)/shard_map/ppermute | solution.py:379
  106.2 2.5 slab_sum.14
  110.2 2.5 slab_sum.13
  113.3 4.2 %adam_part.12 = (f32[1792,1024]{1,0:T(8,128)}, bf16[896,256]{1,0:T(8,128)(2,1)}) custom-call(s32[14]{0:T(128)} %make_table.1.tab, bf16[7168,1024]{1,0:T(8,128)(2,1)} %bitcast.50, bf16[2,1792,256]{2,1,0:T(8,128)(2,1)} %copy-done.1, bf16[1,896,256]{2,1,0:T(8,128)(2,1)} %copy-done.51, f32[1792,1024]{1,0:T(8,128)} %refs_2_.15, ...), custom_call_target="tpu_custom_call", output_to_operand_aliasing={{0}: (7, {})} | custom-call | flops 6881280 | bytes 5505024 | tf_op jit(solution)/shard_map/adam_part/pallas_call | solution.py:139
  117.5 4.4 %adam_part.13 = (f32[1792,1024]{1,0:T(8,128)}, bf16[896,256]{1,0:T(8,128)(2,1)}) custom-call(s32[14]{0:T(128)} %make_table.1.tab, bf16[7168,1024]{1,0:T(8,128)(2,1)} %bitcast.51, bf16[2,1792,256]{2,1,0:T(8,128)(2,1)} %copy-done.1, bf16[1,896,256]{2,1,0:T(8,128)(2,1)} %copy-done.53, f32[1792,1024]{1,0:T(8,128)} %refs_2_.15, ...), custom_call_target="tpu_custom_call", output_to_operand_aliasing={{0}: (7, {})} | custom-call | flops 6881280 | bytes 5505024 | tf_op jit(solution)/shard_map/adam_part/pallas_call | solution.py:139
  124.6 8.1 %collective-permute-start.33 = (bf16[896,256]{1,0:T(8,128)(2,1)S(1)}, bf16[896,256]{1,0:T(8,128)(2,1)S(1)}, u32[]{:S(2)}, u32[]{:S(2)}) collective-permute-start(bf16[896,256]{1,0:T(8,128)(2,1)S(1)} %pick.33), channel_id=1, source_target_pairs={{0,2},{1,3},{2,0},{3,1},{4,6},{5,7},{6,4},{7,5},{8,10},{9,11},{10,... | collective-permute-start | bytes 1376264 | tf_op jit(solution)/shard_map/ppermute | solution.py:379
  134.4 1.6 pick.31
  136.1 8.4 %collective-permute-start.29 = (bf16[896,256]{1,0:T(8,128)(2,1)}, bf16[896,256]{1,0:T(8,128)(2,1)}, u32[]{:S(2)}, u32[]{:S(2)}) collective-permute-start(bf16[896,256]{1,0:T(8,128)(2,1)} %pick.31), channel_id=1, source_target_pairs={{0,2},{1,3},{2,0},{3,1},{4,6},{5,7},{6,4},{7,5},{8,10},{9,11},{10,... | collective-permute-start | bytes 1376264 | tf_op jit(solution)/shard_map/ppermute | solution.py:379
  146.2 2.0 collective-permute-start.14
  150.3 4.2 %adam_part.14 = (f32[1792,1024]{1,0:T(8,128)}, bf16[896,256]{1,0:T(8,128)(2,1)}) custom-call(s32[14]{0:T(128)} %make_table.1.tab, bf16[7168,1024]{1,0:T(8,128)(2,1)} %bitcast.52, bf16[2,1792,256]{2,1,0:T(8,128)(2,1)} %copy-done, bf16[1,896,256]{2,1,0:T(8,128)(2,1)} %collective-permute-done.2.refs_1_, ...), custom_call_target="tpu_custom_call", output_to_operand_aliasing={{0}: (7, {})} | custom-call | flops 6881280 | bytes 5505024 | tf_op jit(solution)/shard_map/adam_part/pallas_call | solution.py:139
  154.6 4.3 %adam_part.15 = (f32[1792,1024]{1,0:T(8,128)}, bf16[896,256]{1,0:T(8,128)(2,1)}) custom-call(s32[14]{0:T(128)} %make_table.1.tab, bf16[7168,1024]{1,0:T(8,128)(2,1)} %bitcast.53, bf16[2,1792,256]{2,1,0:T(8,128)(2,1)} %copy-done, bf16[1,896,256]{2,1,0:T(8,128)(2,1)} %collective-permute-done.1.refs_1_, ...), custom_call_target="tpu_custom_call", output_to_operand_aliasing={{0}: (7, {})} | custom-call | flops 6881280 | bytes 5505024 | tf_op jit(solution)/shard_map/adam_part/pallas_call | solution.py:139
  159.7 5.6 %collective-permute-done.19.refs_10_.refs_2_ = bf16[896,256]{1,0:T(8,128)(2,1)} collective-permute-done((bf16[896,256]{1,0:T(8,128)(2,1)}, bf16[896,256]{1,0:T(8,128)(2,1)}, u32[]{:S(2)}, u32[]{:S(2)}) %collective-permute-start.19) | collective-permute-done | bytes 458784 | tf_op jit(solution)/shard_map/ppermute | solution.py:379
  166.0 4.2 %collective-permute-done.14.refs_4_.refs_2_ = bf16[896,256]{1,0:T(8,128)(2,1)} collective-permute-done((bf16[896,256]{1,0:T(8,128)(2,1)}, bf16[896,256]{1,0:T(8,128)(2,1)}, u32[]{:S(2)}, u32[]{:S(2)}) %collective-permute-start.14) | collective-permute-done | bytes 458784 | tf_op jit(solution)/shard_map/ppermute | solution.py:379
  174.8 3.1 collective-permute-start.23
  178.8 6.1 %collective-permute-start.45 = (bf16[896,256]{1,0:T(8,128)(2,1)S(1)}, bf16[896,256]{1,0:T(8,128)(2,1)S(1)}, u32[]{:S(2)}, u32[]{:S(2)}) collective-permute-start(bf16[896,256]{1,0:T(8,128)(2,1)S(1)} %pick.39), channel_id=1, source_target_pairs={{0,2},{1,3},{2,0},{3,1},{4,6},{5,7},{6,4},{7,5},{8,10},{9,11},{10,... | collective-permute-start | bytes 1376264 | tf_op jit(solution)/shard_map/ppermute | solution.py:379
  185.8 9.0 %collective-permute-start.41 = (bf16[896,256]{1,0:T(8,128)(2,1)S(1)}, bf16[896,256]{1,0:T(8,128)(2,1)S(1)}, u32[]{:S(2)}, u32[]{:S(2)}) collective-permute-start(bf16[896,256]{1,0:T(8,128)(2,1)S(1)} %pick.37), channel_id=1, source_target_pairs={{0,2},{1,3},{2,0},{3,1},{4,6},{5,7},{6,4},{7,5},{8,10},{9,11},{10,... | collective-permute-start | bytes 1376264 | tf_op jit(solution)/shard_map/ppermute | solution.py:379
  194.7 1.6 pick.32
  196.4 4.9 %collective-permute-start.31 = (bf16[896,256]{1,0:T(8,128)(2,1)}, bf16[896,256]{1,0:T(8,128)(2,1)S(1)}, u32[]{:S(2)}, u32[]{:S(2)}) collective-permute-start(bf16[896,256]{1,0:T(8,128)(2,1)} %pick.32), channel_id=1, source_target_pairs={{0,2},{1,3},{2,0},{3,1},{4,6},{5,7},{6,4},{7,5},{8,10},{9,11},{10,... | collective-permute-start | bytes 1376264 | tf_op jit(solution)/shard_map/ppermute | solution.py:379
  204.6 2.0 collective-permute-start.43
  206.6 6.3 %serve_piece.8 = bf16[2,1024,128]{2,1,0:T(8,128)(2,1)} custom-call(s32[14]{0:T(128)S(1)} %copy-done.42, bf16[1024,1792]{1,0:T(8,128)(2,1)} %tok.15, bf16[1792,2048]{1,0:T(8,128)(2,1)} %refs_1_.15, bf16[1792,2048]{1,0:T(8,128)(2,1)} %refs_1_.15, bf16[896,256]{1,0:T(8,128)(2,1)S(1)} %copy-done.25, bf16[896,256]{1,0:T(8,128)(2,1)} %collective-permute-done.12.refs_3_.refs_1_, ...), custom_call_target="tpu_custom_call" | custom-call | flops 939524096 | bytes 5505024 | tf_op jit(solution)/shard_map/serve_piece/pallas_call | solution.py:262
  214.5 4.9 %serve_piece.9 = bf16[2,1024,128]{2,1,0:T(8,128)(2,1)S(1)} custom-call(s32[14]{0:T(128)S(1)} %copy-done.42, bf16[1024,1792]{1,0:T(8,128)(2,1)} %tok.15, bf16[1792,2048]{1,0:T(8,128)(2,1)} %refs_1_.15, bf16[1792,2048]{1,0:T(8,128)(2,1)} %refs_1_.15, bf16[896,256]{1,0:T(8,128)(2,1)S(1)} %collective-permute-done.22.refs_2_, ...), custom_call_target="tpu_custom_call" | custom-call | flops 939524096 | bytes 5505024 | tf_op jit(solution)/shard_map/serve_piece/pallas_call | solution.py:262
  221.3 1.7 collective-permute-done.27.refs_4_.refs_2_
  223.0 2.9 collective-permute-start.39
  225.9 6.9 %collective-permute-done.43.refs_10_.refs_2_ = bf16[896,256]{1,0:T(8,128)(2,1)S(1)} collective-permute-done((bf16[896,256]{1,0:T(8,128)(2,1)}, bf16[896,256]{1,0:T(8,128)(2,1)S(1)}, u32[]{:S(2)}, u32[]{:S(2)}) %collective-permute-start.43) | collective-permute-done | bytes 458784 | tf_op jit(solution)/shard_map/ppermute | solution.py:379
  232.8 2.3 collective-permute-start.55
  235.1 1.6 pick.35
  236.8 1.7 pick.34
  242.8 1.6 pick.45
  245.7 6.8 %collective-permute-done.55.refs_10_.refs_2_ = bf16[896,256]{1,0:T(8,128)(2,1)S(1)} collective-permute-done((bf16[896,256]{1,0:T(8,128)(2,1)S(1)}, bf16[896,256]{1,0:T(8,128)(2,1)S(1)}, u32[]{:S(2)}, u32[]{:S(2)}) %collective-permute-start.55) | collective-permute-done | bytes 458784 | tf_op jit(solution)/shard_map/ppermute | solution.py:379
  252.5 2.3 collective-permute-start.57
  256.2 6.4 %serve_piece.10 = bf16[2,1024,128]{2,1,0:T(8,128)(2,1)} custom-call(s32[14]{0:T(128)S(1)} %copy-done.42, bf16[1024,1792]{1,0:T(8,128)(2,1)} %tok.15, bf16[1792,2048]{1,0:T(8,128)(2,1)} %refs_1_.15, bf16[1792,2048]{1,0:T(8,128)(2,1)} %refs_1_.15, bf16[896,256]{1,0:T(8,128)(2,1)S(1)} %copy-done.5, ...), custom_call_target="tpu_custom_call" | custom-call | flops 939524096 | bytes 5505024 | tf_op jit(solution)/shard_map/serve_piece/pallas_call | solution.py:262
  267.4 5.5 %serve_piece.11 = bf16[2,1024,128]{2,1,0:T(8,128)(2,1)S(1)} custom-call(s32[14]{0:T(128)S(1)} %copy-done.42, bf16[1024,1792]{1,0:T(8,128)(2,1)} %tok.15, bf16[1792,2048]{1,0:T(8,128)(2,1)} %refs_1_.15, bf16[1792,2048]{1,0:T(8,128)(2,1)} %refs_1_.15, bf16[896,256]{1,0:T(8,128)(2,1)} %collective-permute-done.34.refs_2_, ...), custom_call_target="tpu_custom_call" | custom-call | flops 939524096 | bytes 5505024 | tf_op jit(solution)/shard_map/serve_piece/pallas_call | solution.py:262
  275.3 4.5 %collective-permute-done.53.refs_5_.refs_3_ = bf16[896,256]{1,0:T(8,128)(2,1)S(1)} collective-permute-done((bf16[896,256]{1,0:T(8,128)(2,1)S(1)}, bf16[896,256]{1,0:T(8,128)(2,1)S(1)}, u32[]{:S(2)}, u32[]{:S(2)}) %collective-permute-start.53) | collective-permute-done | bytes 458784 | tf_op jit(solution)/shard_map/ppermute | solution.py:379
  282.4 6.4 %serve_piece.12 = bf16[2,1024,128]{2,1,0:T(8,128)(2,1)} custom-call(s32[14]{0:T(128)S(1)} %copy-done.42, bf16[1024,1792]{1,0:T(8,128)(2,1)} %tok.15, bf16[1792,2048]{1,0:T(8,128)(2,1)} %refs_1_.15, bf16[1792,2048]{1,0:T(8,128)(2,1)} %refs_1_.15, bf16[896,256]{1,0:T(8,128)(2,1)S(1)} %copy-done.8, ...), custom_call_target="tpu_custom_call" | custom-call | flops 939524096 | bytes 5505024 | tf_op jit(solution)/shard_map/serve_piece/pallas_call | solution.py:262
  288.9 4.9 %serve_piece.13 = bf16[2,1024,128]{2,1,0:T(8,128)(2,1)S(1)} custom-call(s32[14]{0:T(128)S(1)} %copy-done.42, bf16[1024,1792]{1,0:T(8,128)(2,1)} %tok.15, bf16[1792,2048]{1,0:T(8,128)(2,1)} %refs_1_.15, bf16[1792,2048]{1,0:T(8,128)(2,1)} %refs_1_.15, bf16[896,256]{1,0:T(8,128)(2,1)S(1)} %collective-permute-done.46.refs_2_, ...), custom_call_target="tpu_custom_call" | custom-call | flops 939524096 | bytes 5505024 | tf_op jit(solution)/shard_map/serve_piece/pallas_call | solution.py:262
  294.5 6.4 %serve_piece.14 = bf16[2,1024,128]{2,1,0:T(8,128)(2,1)} custom-call(s32[14]{0:T(128)S(1)} %copy-done.42, bf16[1024,1792]{1,0:T(8,128)(2,1)} %tok.15, bf16[1792,2048]{1,0:T(8,128)(2,1)} %refs_1_.15, bf16[1792,2048]{1,0:T(8,128)(2,1)} %refs_1_.15, bf16[896,256]{1,0:T(8,128)(2,1)S(1)} %copy-done.13, ...), custom_call_target="tpu_custom_call" | custom-call | flops 939524096 | bytes 5505024 | tf_op jit(solution)/shard_map/serve_piece/pallas_call | solution.py:262
  301.6 4.9 %serve_piece.15 = bf16[2,1024,128]{2,1,0:T(8,128)(2,1)S(1)} custom-call(s32[14]{0:T(128)S(1)} %copy-done.42, bf16[1024,1792]{1,0:T(8,128)(2,1)} %tok.15, bf16[1792,2048]{1,0:T(8,128)(2,1)} %refs_1_.15, bf16[1792,2048]{1,0:T(8,128)(2,1)} %refs_1_.15, bf16[896,256]{1,0:T(8,128)(2,1)S(1)} %collective-permute-done.58.refs_2_, ...), custom_call_target="tpu_custom_call" | custom-call | flops 939524096 | bytes 5505024 | tf_op jit(solution)/shard_map/serve_piece/pallas_call | solution.py:262
  310.7 6.2 %collective-permute-done.37 = bf16[1024,128]{1,0:T(8,128)(2,1)S(1)} collective-permute-done((bf16[1024,128]{1,0:T(8,128)(2,1)S(1)}, bf16[1024,128]{1,0:T(8,128)(2,1)S(1)}, u32[]{:S(2)}, u32[]{:S(2)}) %collective-permute-start.37) | collective-permute-done | bytes 262176 | tf_op jit(solution)/shard_map/ppermute | solution.py:375
  317.1 5.4 %collective-permute-done.49 = bf16[1024,128]{1,0:T(8,128)(2,1)S(1)} collective-permute-done((bf16[1024,128]{1,0:T(8,128)(2,1)S(1)}, bf16[1024,128]{1,0:T(8,128)(2,1)S(1)}, u32[]{:S(2)}, u32[]{:S(2)}) %collective-permute-start.49) | collective-permute-done | bytes 262176 | tf_op jit(solution)/shard_map/ppermute | solution.py:375
  322.7 4.3 %collective-permute-done.61 = bf16[1024,128]{1,0:T(8,128)(2,1)S(1)} collective-permute-done((bf16[1024,128]{1,0:T(8,128)(2,1)S(1)}, bf16[1024,128]{1,0:T(8,128)(2,1)S(1)}, u32[]{:S(2)}, u32[]{:S(2)}) %collective-permute-start.61) | collective-permute-done | bytes 262176 | tf_op jit(solution)/shard_map/ppermute | solution.py:375
  (251 shorter events, 67.0 us)
Async XLA Ops:
  5.3 6.6 %collective-permute-start.9 = (bf16[2,1792,256]{2,1,0:T(8,128)(2,1)S(1)}, bf16[2,1792,256]{2,1,0:T(8,128)(2,1)S(1)}, u32[]{:S(2)}, u32[]{:S(2)}) collective-permute-start(bf16[2,1792,256]{2,1,0:T(8,128)(2,1)S(1)} %slab_sum.21), channel_id=1, source_target_pairs={{0,8},{8,0},{16,24},{24,16},{1,9},{9,1},{17,25},{25,17},{2,10},{10... | collective-permute-start | bytes 5505032 | tf_op jit(solution)/shard_map/ppermute | solution.py:375
  8.1 13.6 %collective-permute-start.6 = (bf16[2,1792,256]{2,1,0:T(8,128)(2,1)S(1)}, bf16[2,1792,256]{2,1,0:T(8,128)(2,1)S(1)}, u32[]{:S(2)}, u32[]{:S(2)}) collective-permute-start(bf16[2,1792,256]{2,1,0:T(8,128)(2,1)S(1)} %slab_sum.18), channel_id=1, source_target_pairs={{0,8},{8,0},{16,24},{24,16},{1,9},{9,1},{17,25},{25,17},{2,10},{10... | collective-permute-start | bytes 5505032 | tf_op jit(solution)/shard_map/ppermute | solution.py:375
  11.4 74.3 %collective-permute-start.3 = (bf16[2,1792,256]{2,1,0:T(8,128)(2,1)}, bf16[2,1792,256]{2,1,0:T(8,128)(2,1)S(1)}, u32[]{:S(2)}, u32[]{:S(2)}) collective-permute-start(bf16[2,1792,256]{2,1,0:T(8,128)(2,1)} %slab_sum.15), channel_id=1, source_target_pairs={{0,8},{8,0},{16,24},{24,16},{1,9},{9,1},{17,25},{25,17},{2,10},{10... | collective-permute-start | bytes 5505032 | tf_op jit(solution)/shard_map/ppermute | solution.py:375
  13.7 14.8 %collective-permute-start.11 = (bf16[1,896,256]{2,1,0:T(8,128)(2,1)S(1)}, bf16[1,896,256]{2,1,0:T(8,128)(2,1)S(1)}, u32[]{:S(2)}, u32[]{:S(2)}) collective-permute-start(bf16[1,896,256]{2,1,0:T(8,128)(2,1)S(1)} %slab_sum.23), channel_id=1, source_target_pairs={{0,16},{8,24},{16,0},{24,8},{1,17},{9,25},{17,1},{25,9},{2,18},{10... | collective-permute-start | bytes 1376264 | tf_op jit(solution)/shard_map/ppermute | solution.py:375
  19.4 78.4 %collective-permute-start = (bf16[2,1792,256]{2,1,0:T(8,128)(2,1)}, bf16[2,1792,256]{2,1,0:T(8,128)(2,1)S(1)}, u32[]{:S(2)}, u32[]{:S(2)}) collective-permute-start(bf16[2,1792,256]{2,1,0:T(8,128)(2,1)} %slab_sum.12), channel_id=1, source_target_pairs={{0,8},{8,0},{16,24},{24,16},{1,9},{9,1},{17,25},{25,17},{2,10},{10... | collective-permute-start | bytes 5505032 | tf_op jit(solution)/shard_map/ppermute | solution.py:375
  21.3 16.2 %collective-permute-start.10 = (bf16[1,896,256]{2,1,0:T(8,128)(2,1)S(1)}, bf16[1,896,256]{2,1,0:T(8,128)(2,1)}, u32[]{:S(2)}, u32[]{:S(2)}) collective-permute-start(bf16[1,896,256]{2,1,0:T(8,128)(2,1)S(1)} %slab_sum.22), channel_id=1, source_target_pairs={{0,16},{8,24},{16,0},{24,8},{1,17},{9,25},{17,1},{25,9},{2,18},{10... | collective-permute-start | bytes 1376264 | tf_op jit(solution)/shard_map/ppermute | solution.py:375
  24.3 23.1 %collective-permute-start.8 = (bf16[1,896,256]{2,1,0:T(8,128)(2,1)}, bf16[1,896,256]{2,1,0:T(8,128)(2,1)}, u32[]{:S(2)}, u32[]{:S(2)}) collective-permute-start(bf16[1,896,256]{2,1,0:T(8,128)(2,1)} %slab_sum.20), channel_id=1, source_target_pairs={{0,16},{8,24},{16,0},{24,8},{1,17},{9,25},{17,1},{25,9},{2,18},{10... | collective-permute-start | bytes 1376264 | tf_op jit(solution)/shard_map/ppermute | solution.py:375
  29.3 27.6 %collective-permute-start.7 = (bf16[1,896,256]{2,1,0:T(8,128)(2,1)}, bf16[1,896,256]{2,1,0:T(8,128)(2,1)S(1)}, u32[]{:S(2)}, u32[]{:S(2)}) collective-permute-start(bf16[1,896,256]{2,1,0:T(8,128)(2,1)} %slab_sum.19), channel_id=1, source_target_pairs={{0,16},{8,24},{16,0},{24,8},{1,17},{9,25},{17,1},{25,9},{2,18},{10... | collective-permute-start | bytes 1376264 | tf_op jit(solution)/shard_map/ppermute | solution.py:375
  41.9 16.8 %collective-permute-start.17 = (bf16[896,256]{1,0:T(8,128)(2,1)}, bf16[896,256]{1,0:T(8,128)(2,1)S(1)}, u32[]{:S(2)}, u32[]{:S(2)}) collective-permute-start(bf16[896,256]{1,0:T(8,128)(2,1)} %get-tuple-element.28.refs_0_.refs_8_), channel_id=1, source_target_pairs={{0,2},{1,3},{2,0},{3,1},{4,6},{5,7},{6,4},{7,5},{8,10},{9,11},{10,... | collective-permute-start | bytes 1376264 | tf_op jit(solution)/shard_map/ppermute | solution.py:379
  47.4 12.1 %collective-permute-start.18 = (bf16[896,256]{1,0:T(8,128)(2,1)}, bf16[896,256]{1,0:T(8,128)(2,1)S(1)}, u32[]{:S(2)}, u32[]{:S(2)}) collective-permute-start(bf16[896,256]{1,0:T(8,128)(2,1)} %get-tuple-element.28.refs_0_.refs_8_), channel_id=1, source_target_pairs={{2,4},{3,5},{4,2},{5,3},{10,12},{11,13},{12,10},{13,11},{18,20},{1... | collective-permute-start | bytes 1376264 | tf_op jit(solution)/shard_map/ppermute | solution.py:379
  56.9 12.4 %collective-permute-start.12 = (bf16[896,256]{1,0:T(8,128)(2,1)S(1)}, bf16[896,256]{1,0:T(8,128)(2,1)}, u32[]{:S(2)}, u32[]{:S(2)}) collective-permute-start(bf16[896,256]{1,0:T(8,128)(2,1)S(1)} %copy-done.23), channel_id=1, source_target_pairs={{0,2},{1,3},{2,0},{3,1},{4,6},{5,7},{6,4},{7,5},{8,10},{9,11},{10,... | collective-permute-start | bytes 1376264 | tf_op jit(solution)/shard_map/ppermute | solution.py:379
  58.8 20.7 %collective-permute-start.20 = (bf16[896,256]{1,0:T(8,128)(2,1)S(1)}, bf16[896,256]{1,0:T(8,128)(2,1)S(1)}, u32[]{:S(2)}, u32[]{:S(2)}) collective-permute-start(bf16[896,256]{1,0:T(8,128)(2,1)S(1)} %collective-permute-done.17.refs_9_.refs_1_), channel_id=1, source_target_pairs={{2,4},{3,5},{4,2},{5,3},{10,12},{11,13},{12,10},{13,11},{18,20},{1... | collective-permute-start | bytes 1376264 | tf_op jit(solution)/shard_map/ppermute | solution.py:379
  59.5 29.6 %collective-permute-start.13 = (bf16[896,256]{1,0:T(8,128)(2,1)S(1)}, bf16[896,256]{1,0:T(8,128)(2,1)S(1)}, u32[]{:S(2)}, u32[]{:S(2)}) collective-permute-start(bf16[896,256]{1,0:T(8,128)(2,1)S(1)} %copy-done.23), channel_id=1, source_target_pairs={{2,4},{3,5},{4,2},{5,3},{10,12},{11,13},{12,10},{13,11},{18,20},{1... | collective-permute-start | bytes 1376264 | tf_op jit(solution)/shard_map/ppermute | solution.py:379
  69.4 19.7 %collective-permute-start.15 = (bf16[896,256]{1,0:T(8,128)(2,1)}, bf16[896,256]{1,0:T(8,128)(2,1)}, u32[]{:S(2)}, u32[]{:S(2)}) collective-permute-start(bf16[896,256]{1,0:T(8,128)(2,1)} %collective-permute-done.12.refs_3_.refs_1_), channel_id=1, source_target_pairs={{2,4},{3,5},{4,2},{5,3},{10,12},{11,13},{12,10},{13,11},{18,20},{1... | collective-permute-start | bytes 1376264 | tf_op jit(solution)/shard_map/ppermute | solution.py:379
  82.1 16.4 %collective-permute-start.21 = (bf16[896,256]{1,0:T(8,128)(2,1)S(1)}, bf16[896,256]{1,0:T(8,128)(2,1)S(1)}, u32[]{:S(2)}, u32[]{:S(2)}) collective-permute-start(bf16[896,256]{1,0:T(8,128)(2,1)S(1)} %pick.27), channel_id=1, source_target_pairs={{0,2},{1,3},{2,0},{3,1},{4,6},{5,7},{6,4},{7,5},{8,10},{9,11},{10,... | collective-permute-start | bytes 1376264 | tf_op jit(solution)/shard_map/ppermute | solution.py:379
  87.5 11.7 %collective-permute-start.5 = (bf16[1,896,256]{2,1,0:T(8,128)(2,1)S(1)}, bf16[1,896,256]{2,1,0:T(8,128)(2,1)S(1)}, u32[]{:S(2)}, u32[]{:S(2)}) collective-permute-start(bf16[1,896,256]{2,1,0:T(8,128)(2,1)S(1)} %slab_sum.17), channel_id=1, source_target_pairs={{0,16},{8,24},{16,0},{24,8},{1,17},{9,25},{17,1},{25,9},{2,18},{10... | collective-permute-start | bytes 1376264 | tf_op jit(solution)/shard_map/ppermute | solution.py:375
  89.9 14.9 %collective-permute-start.16 = (bf16[896,256]{1,0:T(8,128)(2,1)S(1)}, bf16[896,256]{1,0:T(8,128)(2,1)}, u32[]{:S(2)}, u32[]{:S(2)}) collective-permute-start(bf16[896,256]{1,0:T(8,128)(2,1)S(1)} %pick.25), channel_id=1, source_target_pairs={{0,2},{1,3},{2,0},{3,1},{4,6},{5,7},{6,4},{7,5},{8,10},{9,11},{10,... | collective-permute-start | bytes 1376264 | tf_op jit(solution)/shard_map/ppermute | solution.py:379
  96.3 12.5 %collective-permute-start.4 = (bf16[1,896,256]{2,1,0:T(8,128)(2,1)S(1)}, bf16[1,896,256]{2,1,0:T(8,128)(2,1)S(1)}, u32[]{:S(2)}, u32[]{:S(2)}) collective-permute-start(bf16[1,896,256]{2,1,0:T(8,128)(2,1)S(1)} %slab_sum.16), channel_id=1, source_target_pairs={{0,16},{8,24},{16,0},{24,8},{1,17},{9,25},{17,1},{25,9},{2,18},{10... | collective-permute-start | bytes 1376264 | tf_op jit(solution)/shard_map/ppermute | solution.py:375
  97.8 14.9 %collective-permute-start.30 = (bf16[896,256]{1,0:T(8,128)(2,1)S(1)}, bf16[896,256]{1,0:T(8,128)(2,1)S(1)}, u32[]{:S(2)}, u32[]{:S(2)}) collective-permute-start(bf16[896,256]{1,0:T(8,128)(2,1)S(1)} %copy-done.7), channel_id=1, source_target_pairs={{2,4},{3,5},{4,2},{5,3},{10,12},{11,13},{12,10},{13,11},{18,20},{1... | collective-permute-start | bytes 1376264 | tf_op jit(solution)/shard_map/ppermute | solution.py:379
  98.5 23.4 %collective-permute-start.32 = (bf16[896,256]{1,0:T(8,128)(2,1)S(1)}, bf16[896,256]{1,0:T(8,128)(2,1)S(1)}, u32[]{:S(2)}, u32[]{:S(2)}) collective-permute-start(bf16[896,256]{1,0:T(8,128)(2,1)S(1)} %collective-permute-done.21.refs_11_.refs_3_.refs_9_.refs_1_), channel_id=1, source_target_pairs={{2,4},{3,5},{4,2},{5,3},{10,12},{11,13},{12,10},{13,11},{18,20},{1... | collective-permute-start | bytes 1376264 | tf_op jit(solution)/shard_map/ppermute | solution.py:379
  99.2 25.4 %collective-permute-start.26 = (bf16[896,256]{1,0:T(8,128)(2,1)S(1)}, bf16[896,256]{1,0:T(8,128)(2,1)S(1)}, u32[]{:S(2)}, u32[]{:S(2)}) collective-permute-start(bf16[896,256]{1,0:T(8,128)(2,1)S(1)} %copy-done.5), channel_id=1, source_target_pairs={{2,4},{3,5},{4,2},{5,3},{10,12},{11,13},{12,10},{13,11},{18,20},{1... | collective-permute-start | bytes 1376264 | tf_op jit(solution)/shard_map/ppermute | solution.py:379
  104.8 29.6 %collective-permute-start.28 = (bf16[896,256]{1,0:T(8,128)(2,1)}, bf16[896,256]{1,0:T(8,128)(2,1)}, u32[]{:S(2)}, u32[]{:S(2)}) collective-permute-start(bf16[896,256]{1,0:T(8,128)(2,1)} %collective-permute-done.16.refs_5_.refs_3_.refs_1_), channel_id=1, source_target_pairs={{2,4},{3,5},{4,2},{5,3},{10,12},{11,13},{12,10},{13,11},{18,20},{1... | collective-permute-start | bytes 1376264 | tf_op jit(solution)/shard_map/ppermute | solution.py:379
  108.7 35.7 %collective-permute-start.2 = (bf16[1,896,256]{2,1,0:T(8,128)(2,1)}, bf16[1,896,256]{2,1,0:T(8,128)(2,1)}, u32[]{:S(2)}, u32[]{:S(2)}) collective-permute-start(bf16[1,896,256]{2,1,0:T(8,128)(2,1)} %slab_sum.14), channel_id=1, source_target_pairs={{0,16},{8,24},{16,0},{24,8},{1,17},{9,25},{17,1},{25,9},{2,18},{10... | collective-permute-start | bytes 1376264 | tf_op jit(solution)/shard_map/ppermute | solution.py:375
  112.7 122.4 %copy-start.12 = (bf16[896,256]{1,0:T(8,128)(2,1)}, bf16[896,256]{1,0:T(8,128)(2,1)S(1)}, u32[]{:S(2)}) copy-start(bf16[896,256]{1,0:T(8,128)(2,1)S(1)} %collective-permute-done.30.refs_1_.refs_0_.refs_12_.refs_4_) | copy-start | bytes 1376260
  112.7 33.4 %collective-permute-start.1 = (bf16[1,896,256]{2,1,0:T(8,128)(2,1)}, bf16[1,896,256]{2,1,0:T(8,128)(2,1)}, u32[]{:S(2)}, u32[]{:S(2)}) collective-permute-start(bf16[1,896,256]{2,1,0:T(8,128)(2,1)} %slab_sum.13), channel_id=1, source_target_pairs={{0,16},{8,24},{16,0},{24,8},{1,17},{9,25},{17,1},{25,9},{2,18},{10... | collective-permute-start | bytes 1376264 | tf_op jit(solution)/shard_map/ppermute | solution.py:375
  121.9 26.2 %collective-permute-start.42 = (bf16[896,256]{1,0:T(8,128)(2,1)}, bf16[896,256]{1,0:T(8,128)(2,1)S(1)}, u32[]{:S(2)}, u32[]{:S(2)}) collective-permute-start(bf16[896,256]{1,0:T(8,128)(2,1)} %get-tuple-element.31.refs_2_.refs_0_.refs_8_), channel_id=1, source_target_pairs={{2,4},{3,5},{4,2},{5,3},{10,12},{11,13},{12,10},{13,11},{18,20},{1... | collective-permute-start | bytes 1376264 | tf_op jit(solution)/shard_map/ppermute | solution.py:379
  124.6 24.2 %collective-permute-start.33 = (bf16[896,256]{1,0:T(8,128)(2,1)S(1)}, bf16[896,256]{1,0:T(8,128)(2,1)S(1)}, u32[]{:S(2)}, u32[]{:S(2)}) collective-permute-start(bf16[896,256]{1,0:T(8,128)(2,1)S(1)} %pick.33), channel_id=1, source_target_pairs={{0,2},{1,3},{2,0},{3,1},{4,6},{5,7},{6,4},{7,5},{8,10},{9,11},{10,... | collective-permute-start | bytes 1376264 | tf_op jit(solution)/shard_map/ppermute | solution.py:379
  136.1 22.8 %collective-permute-start.29 = (bf16[896,256]{1,0:T(8,128)(2,1)}, bf16[896,256]{1,0:T(8,128)(2,1)}, u32[]{:S(2)}, u32[]{:S(2)}) collective-permute-start(bf16[896,256]{1,0:T(8,128)(2,1)} %pick.31), channel_id=1, source_target_pairs={{0,2},{1,3},{2,0},{3,1},{4,6},{5,7},{6,4},{7,5},{8,10},{9,11},{10,... | collective-permute-start | bytes 1376264 | tf_op jit(solution)/shard_map/ppermute | solution.py:379
  144.4 20.9 %collective-permute-start.19 = (bf16[896,256]{1,0:T(8,128)(2,1)}, bf16[896,256]{1,0:T(8,128)(2,1)}, u32[]{:S(2)}, u32[]{:S(2)}) collective-permute-start(bf16[896,256]{1,0:T(8,128)(2,1)} %pick.26), channel_id=1, source_target_pairs={{0,2},{1,3},{2,0},{3,1},{4,6},{5,7},{6,4},{7,5},{8,10},{9,11},{10,... | collective-permute-start | bytes 1376264 | tf_op jit(solution)/shard_map/ppermute | solution.py:379
  146.2 24.1 %collective-permute-start.14 = (bf16[896,256]{1,0:T(8,128)(2,1)}, bf16[896,256]{1,0:T(8,128)(2,1)}, u32[]{:S(2)}, u32[]{:S(2)}) collective-permute-start(bf16[896,256]{1,0:T(8,128)(2,1)} %pick.24), channel_id=1, source_target_pairs={{0,2},{1,3},{2,0},{3,1},{4,6},{5,7},{6,4},{7,5},{8,10},{9,11},{10,... | collective-permute-start | bytes 1376264 | tf_op jit(solution)/shard_map/ppermute | solution.py:379
  148.2 114.5 %copy-start.11 = (bf16[896,256]{1,0:T(8,128)(2,1)}, bf16[896,256]{1,0:T(8,128)(2,1)S(1)}, u32[]{:S(2)}) copy-start(bf16[896,256]{1,0:T(8,128)(2,1)S(1)} %collective-permute-done.42.refs_1_.refs_0_.refs_12_.refs_4_) | copy-start | bytes 1376260
  148.2 26.6 %collective-permute-start.38 = (bf16[896,256]{1,0:T(8,128)(2,1)S(1)}, bf16[896,256]{1,0:T(8,128)(2,1)S(1)}, u32[]{:S(2)}, u32[]{:S(2)}) collective-permute-start(bf16[896,256]{1,0:T(8,128)(2,1)S(1)} %copy-done.8), channel_id=1, source_target_pairs={{2,4},{3,5},{4,2},{5,3},{10,12},{11,13},{12,10},{13,11},{18,20},{1... | collective-permute-start | bytes 1376264 | tf_op jit(solution)/shard_map/ppermute | solution.py:379
  148.9 28.9 %collective-permute-start.44 = (bf16[896,256]{1,0:T(8,128)(2,1)S(1)}, bf16[896,256]{1,0:T(8,128)(2,1)}, u32[]{:S(2)}, u32[]{:S(2)}) collective-permute-start(bf16[896,256]{1,0:T(8,128)(2,1)S(1)} %collective-permute-done.33.refs_11_.refs_3_.refs_9_.refs_1_), channel_id=1, source_target_pairs={{2,4},{3,5},{4,2},{5,3},{10,12},{11,13},{12,10},{13,11},{18,20},{1... | collective-permute-start | bytes 1376264 | tf_op jit(solution)/shard_map/ppermute | solution.py:379
  158.9 19.9 %collective-permute-start.40 = (bf16[896,256]{1,0:T(8,128)(2,1)}, bf16[896,256]{1,0:T(8,128)(2,1)S(1)}, u32[]{:S(2)}, u32[]{:S(2)}) collective-permute-start(bf16[896,256]{1,0:T(8,128)(2,1)} %collective-permute-done.29.refs_5_.refs_3_.refs_1_), channel_id=1, source_target_pairs={{2,4},{3,5},{4,2},{5,3},{10,12},{11,13},{12,10},{13,11},{18,20},{1... | collective-permute-start | bytes 1376264 | tf_op jit(solution)/shard_map/ppermute | solution.py:379
  165.4 20.4 %collective-permute-start.54 = (bf16[896,256]{1,0:T(8,128)(2,1)}, bf16[896,256]{1,0:T(8,128)(2,1)S(1)}, u32[]{:S(2)}, u32[]{:S(2)}) collective-permute-start(bf16[896,256]{1,0:T(8,128)(2,1)} %get-tuple-element.33.refs_2_.refs_0_.refs_8_), channel_id=1, source_target_pairs={{2,4},{3,5},{4,2},{5,3},{10,12},{11,13},{12,10},{13,11},{18,20},{1... | collective-permute-start | bytes 1376264 | tf_op jit(solution)/shard_map/ppermute | solution.py:379
  170.3 26.1 %collective-permute-start.50 = (bf16[896,256]{1,0:T(8,128)(2,1)S(1)}, bf16[896,256]{1,0:T(8,128)(2,1)S(1)}, u32[]{:S(2)}, u32[]{:S(2)}) collective-permute-start(bf16[896,256]{1,0:T(8,128)(2,1)S(1)} %copy-done.13), channel_id=1, source_target_pairs={{2,4},{3,5},{4,2},{5,3},{10,12},{11,13},{12,10},{13,11},{18,20},{1... | collective-permute-start | bytes 1376264 | tf_op jit(solution)/shard_map/ppermute | solution.py:379
  174.8 29.7 %collective-permute-start.23 = (bf16[896,256]{1,0:T(8,128)(2,1)S(1)}, bf16[896,256]{1,0:T(8,128)(2,1)S(1)}, u32[]{:S(2)}, u32[]{:S(2)}) collective-permute-start(bf16[896,256]{1,0:T(8,128)(2,1)S(1)} %pick.29), channel_id=1, source_target_pairs={{0,1},{1,0},{2,3},{3,2},{4,5},{5,4},{6,7},{7,6},{8,9},{9,8},{10,11... | collective-permute-start | bytes 1376264 | tf_op jit(solution)/shard_map/ppermute | solution.py:484
  177.8 26.7 %collective-permute-start.22 = (bf16[896,256]{1,0:T(8,128)(2,1)S(1)}, bf16[896,256]{1,0:T(8,128)(2,1)S(1)}, u32[]{:S(2)}, u32[]{:S(2)}) collective-permute-start(bf16[896,256]{1,0:T(8,128)(2,1)S(1)} %pick.28), channel_id=1, source_target_pairs={{0,1},{1,0},{2,3},{3,2},{4,5},{5,4},{6,7},{7,6},{8,9},{9,8},{10,11... | collective-permute-start | bytes 1376264 | tf_op jit(solution)/shard_map/ppermute | solution.py:484
  178.8 34.1 %collective-permute-start.45 = (bf16[896,256]{1,0:T(8,128)(2,1)S(1)}, bf16[896,256]{1,0:T(8,128)(2,1)S(1)}, u32[]{:S(2)}, u32[]{:S(2)}) collective-permute-start(bf16[896,256]{1,0:T(8,128)(2,1)S(1)} %pick.39), channel_id=1, source_target_pairs={{0,2},{1,3},{2,0},{3,1},{4,6},{5,7},{6,4},{7,5},{8,10},{9,11},{10,... | collective-permute-start | bytes 1376264 | tf_op jit(solution)/shard_map/ppermute | solution.py:379
  185.8 28.0 %collective-permute-start.41 = (bf16[896,256]{1,0:T(8,128)(2,1)S(1)}, bf16[896,256]{1,0:T(8,128)(2,1)S(1)}, u32[]{:S(2)}, u32[]{:S(2)}) collective-permute-start(bf16[896,256]{1,0:T(8,128)(2,1)S(1)} %pick.37), channel_id=1, source_target_pairs={{0,2},{1,3},{2,0},{3,1},{4,6},{5,7},{6,4},{7,5},{8,10},{9,11},{10,... | collective-permute-start | bytes 1376264 | tf_op jit(solution)/shard_map/ppermute | solution.py:379
  196.4 23.1 %collective-permute-start.31 = (bf16[896,256]{1,0:T(8,128)(2,1)}, bf16[896,256]{1,0:T(8,128)(2,1)S(1)}, u32[]{:S(2)}, u32[]{:S(2)}) collective-permute-start(bf16[896,256]{1,0:T(8,128)(2,1)} %pick.32), channel_id=1, source_target_pairs={{0,2},{1,3},{2,0},{3,1},{4,6},{5,7},{6,4},{7,5},{8,10},{9,11},{10,... | collective-permute-start | bytes 1376264 | tf_op jit(solution)/shard_map/ppermute | solution.py:379
  204.5 18.5 %collective-permute-start.27 = (bf16[896,256]{1,0:T(8,128)(2,1)}, bf16[896,256]{1,0:T(8,128)(2,1)S(1)}, u32[]{:S(2)}, u32[]{:S(2)}) collective-permute-start(bf16[896,256]{1,0:T(8,128)(2,1)} %pick.30), channel_id=1, source_target_pairs={{0,2},{1,3},{2,0},{3,1},{4,6},{5,7},{6,4},{7,5},{8,10},{9,11},{10,... | collective-permute-start | bytes 1376264 | tf_op jit(solution)/shard_map/ppermute | solution.py:379
  204.6 28.2 %collective-permute-start.43 = (bf16[896,256]{1,0:T(8,128)(2,1)}, bf16[896,256]{1,0:T(8,128)(2,1)S(1)}, u32[]{:S(2)}, u32[]{:S(2)}) collective-permute-start(bf16[896,256]{1,0:T(8,128)(2,1)} %pick.38), channel_id=1, source_target_pairs={{0,2},{1,3},{2,0},{3,1},{4,6},{5,7},{6,4},{7,5},{8,10},{9,11},{10,... | collective-permute-start | bytes 1376264 | tf_op jit(solution)/shard_map/ppermute | solution.py:379
  212.9 25.5 %collective-permute-start.56 = (bf16[896,256]{1,0:T(8,128)(2,1)S(1)}, bf16[896,256]{1,0:T(8,128)(2,1)S(1)}, u32[]{:S(2)}, u32[]{:S(2)}) collective-permute-start(bf16[896,256]{1,0:T(8,128)(2,1)S(1)} %collective-permute-done.45.refs_11_.refs_3_.refs_9_.refs_1_), channel_id=1, source_target_pairs={{2,4},{3,5},{4,2},{5,3},{10,12},{11,13},{12,10},{13,11},{18,20},{1... | collective-permute-start | bytes 1376264 | tf_op jit(solution)/shard_map/ppermute | solution.py:379
  213.8 26.3 %collective-permute-start.52 = (bf16[896,256]{1,0:T(8,128)(2,1)S(1)}, bf16[896,256]{1,0:T(8,128)(2,1)S(1)}, u32[]{:S(2)}, u32[]{:S(2)}) collective-permute-start(bf16[896,256]{1,0:T(8,128)(2,1)S(1)} %collective-permute-done.41.refs_5_.refs_3_.refs_1_), channel_id=1, source_target_pairs={{2,4},{3,5},{4,2},{5,3},{10,12},{11,13},{12,10},{13,11},{18,20},{1... | collective-permute-start | bytes 1376264 | tf_op jit(solution)/shard_map/ppermute | solution.py:379
  219.5 35.3 %collective-permute-start.24 = (bf16[2,1024,128]{2,1,0:T(8,128)(2,1)S(1)}, bf16[2,1024,128]{2,1,0:T(8,128)(2,1)S(1)}, u32[]{:S(2)}, u32[]{:S(2)}) collective-permute-start(bf16[2,1024,128]{2,1,0:T(8,128)(2,1)S(1)} %pad_maximum_fusion), channel_id=1, source_target_pairs={{0,8},{8,0},{16,24},{24,16},{1,9},{9,1},{17,25},{25,17},{2,10},{10... | collective-permute-start | bytes 1572872 | tf_op jit(solution)/shard_map/ppermute | solution.py:375
  223.0 22.3 %collective-permute-start.39 = (bf16[896,256]{1,0:T(8,128)(2,1)S(1)}, bf16[896,256]{1,0:T(8,128)(2,1)S(1)}, u32[]{:S(2)}, u32[]{:S(2)}) collective-permute-start(bf16[896,256]{1,0:T(8,128)(2,1)S(1)} %pick.36), channel_id=1, source_target_pairs={{0,2},{1,3},{2,0},{3,1},{4,6},{5,7},{6,4},{7,5},{8,10},{9,11},{10,... | collective-permute-start | bytes 1376264 | tf_op jit(solution)/shard_map/ppermute | solution.py:379
  232.8 19.7 %collective-permute-start.55 = (bf16[896,256]{1,0:T(8,128)(2,1)S(1)}, bf16[896,256]{1,0:T(8,128)(2,1)S(1)}, u32[]{:S(2)}, u32[]{:S(2)}) collective-permute-start(bf16[896,256]{1,0:T(8,128)(2,1)S(1)} %pick.44), channel_id=1, source_target_pairs={{0,2},{1,3},{2,0},{3,1},{4,6},{5,7},{6,4},{7,5},{8,10},{9,11},{10,... | collective-permute-start | bytes 1376264 | tf_op jit(solution)/shard_map/ppermute | solution.py:379
  238.4 26.0 %collective-permute-start.35 = (bf16[896,256]{1,0:T(8,128)(2,1)}, bf16[896,256]{1,0:T(8,128)(2,1)}, u32[]{:S(2)}, u32[]{:S(2)}) collective-permute-start(bf16[896,256]{1,0:T(8,128)(2,1)} %pick.35), channel_id=1, source_target_pairs={{0,1},{1,0},{2,3},{3,2},{4,5},{5,4},{6,7},{7,6},{8,9},{9,8},{10,11... | collective-permute-start | bytes 1376264 | tf_op jit(solution)/shard_map/ppermute | solution.py:484
  240.0 25.2 %collective-permute-start.34 = (bf16[896,256]{1,0:T(8,128)(2,1)}, bf16[896,256]{1,0:T(8,128)(2,1)}, u32[]{:S(2)}, u32[]{:S(2)}) collective-permute-start(bf16[896,256]{1,0:T(8,128)(2,1)} %pick.34), channel_id=1, source_target_pairs={{0,1},{1,0},{2,3},{3,2},{4,5},{5,4},{6,7},{7,6},{8,9},{9,8},{10,11... | collective-permute-start | bytes 1376264 | tf_op jit(solution)/shard_map/ppermute | solution.py:484
  245.3 29.2 %collective-permute-start.51 = (bf16[896,256]{1,0:T(8,128)(2,1)}, bf16[896,256]{1,0:T(8,128)(2,1)S(1)}, u32[]{:S(2)}, u32[]{:S(2)}) collective-permute-start(bf16[896,256]{1,0:T(8,128)(2,1)} %pick.42), channel_id=1, source_target_pairs={{0,2},{1,3},{2,0},{3,1},{4,6},{5,7},{6,4},{7,5},{8,10},{9,11},{10,... | collective-permute-start | bytes 1376264 | tf_op jit(solution)/shard_map/ppermute | solution.py:379
  252.5 20.5 %collective-permute-start.57 = (bf16[896,256]{1,0:T(8,128)(2,1)}, bf16[896,256]{1,0:T(8,128)(2,1)S(1)}, u32[]{:S(2)}, u32[]{:S(2)}) collective-permute-start(bf16[896,256]{1,0:T(8,128)(2,1)} %pick.45), channel_id=1, source_target_pairs={{0,2},{1,3},{2,0},{3,1},{4,6},{5,7},{6,4},{7,5},{8,10},{9,11},{10,... | collective-permute-start | bytes 1376264 | tf_op jit(solution)/shard_map/ppermute | solution.py:379
  254.8 25.1 %collective-permute-start.53 = (bf16[896,256]{1,0:T(8,128)(2,1)S(1)}, bf16[896,256]{1,0:T(8,128)(2,1)S(1)}, u32[]{:S(2)}, u32[]{:S(2)}) collective-permute-start(bf16[896,256]{1,0:T(8,128)(2,1)S(1)} %pick.43), channel_id=1, source_target_pairs={{0,2},{1,3},{2,0},{3,1},{4,6},{5,7},{6,4},{7,5},{8,10},{9,11},{10,... | collective-permute-start | bytes 1376264 | tf_op jit(solution)/shard_map/ppermute | solution.py:379
  264.4 24.4 %collective-permute-start.47 = (bf16[896,256]{1,0:T(8,128)(2,1)S(1)}, bf16[896,256]{1,0:T(8,128)(2,1)S(1)}, u32[]{:S(2)}, u32[]{:S(2)}) collective-permute-start(bf16[896,256]{1,0:T(8,128)(2,1)S(1)} %pick.41), channel_id=1, source_target_pairs={{0,1},{1,0},{2,3},{3,2},{4,5},{5,4},{6,7},{7,6},{8,9},{9,8},{10,11... | collective-permute-start | bytes 1376264 | tf_op jit(solution)/shard_map/ppermute | solution.py:484
  265.3 23.6 %collective-permute-start.46 = (bf16[896,256]{1,0:T(8,128)(2,1)S(1)}, bf16[896,256]{1,0:T(8,128)(2,1)S(1)}, u32[]{:S(2)}, u32[]{:S(2)}) collective-permute-start(bf16[896,256]{1,0:T(8,128)(2,1)S(1)} %pick.40), channel_id=1, source_target_pairs={{0,1},{1,0},{2,3},{3,2},{4,5},{5,4},{6,7},{7,6},{8,9},{9,8},{10,11... | collective-permute-start | bytes 1376264 | tf_op jit(solution)/shard_map/ppermute | solution.py:484
  272.9 33.7 %collective-permute-start.25 = (bf16[1024,128]{1,0:T(8,128)(2,1)}, bf16[1024,128]{1,0:T(8,128)(2,1)S(1)}, u32[]{:S(2)}, u32[]{:S(2)}) collective-permute-start(bf16[1024,128]{1,0:T(8,128)(2,1)} %fusion.1), channel_id=1, source_target_pairs={{0,16},{8,24},{16,0},{24,8},{1,17},{9,25},{17,1},{25,9},{2,18},{10... | collective-permute-start | bytes 786440 | tf_op jit(solution)/shard_map/ppermute | solution.py:375
  274.4 26.5 %collective-permute-start.59 = (bf16[896,256]{1,0:T(8,128)(2,1)S(1)}, bf16[896,256]{1,0:T(8,128)(2,1)S(1)}, u32[]{:S(2)}, u32[]{:S(2)}) collective-permute-start(bf16[896,256]{1,0:T(8,128)(2,1)S(1)} %pick.47), channel_id=1, source_target_pairs={{0,1},{1,0},{2,3},{3,2},{4,5},{5,4},{6,7},{7,6},{8,9},{9,8},{10,11... | collective-permute-start | bytes 1376264 | tf_op jit(solution)/shard_map/ppermute | solution.py:484
  280.7 20.8 %collective-permute-start.58 = (bf16[896,256]{1,0:T(8,128)(2,1)S(1)}, bf16[896,256]{1,0:T(8,128)(2,1)S(1)}, u32[]{:S(2)}, u32[]{:S(2)}) collective-permute-start(bf16[896,256]{1,0:T(8,128)(2,1)S(1)} %pick.46), channel_id=1, source_target_pairs={{0,1},{1,0},{2,3},{3,2},{4,5},{5,4},{6,7},{7,6},{8,9},{9,8},{10,11... | collective-permute-start | bytes 1376264 | tf_op jit(solution)/shard_map/ppermute | solution.py:484
  288.8 18.0 %collective-permute-start.36 = (bf16[2,1024,128]{2,1,0:T(8,128)(2,1)S(1)}, bf16[2,1024,128]{2,1,0:T(8,128)(2,1)S(1)}, u32[]{:S(2)}, u32[]{:S(2)}) collective-permute-start(bf16[2,1024,128]{2,1,0:T(8,128)(2,1)S(1)} %pad_maximum_fusion.1), channel_id=1, source_target_pairs={{0,8},{8,0},{16,24},{24,16},{1,9},{9,1},{17,25},{25,17},{2,10},{10... | collective-permute-start | bytes 1572872 | tf_op jit(solution)/shard_map/ppermute | solution.py:375
  293.9 14.3 %collective-permute-start.48 = (bf16[2,1024,128]{2,1,0:T(8,128)(2,1)S(1)}, bf16[2,1024,128]{2,1,0:T(8,128)(2,1)S(1)}, u32[]{:S(2)}, u32[]{:S(2)}) collective-permute-start(bf16[2,1024,128]{2,1,0:T(8,128)(2,1)S(1)} %pad_maximum_fusion.2), channel_id=1, source_target_pairs={{0,8},{8,0},{16,24},{24,16},{1,9},{9,1},{17,25},{25,17},{2,10},{10... | collective-permute-start | bytes 1572872 | tf_op jit(solution)/shard_map/ppermute | solution.py:375
  306.6 3.4 %collective-permute-start.60 = (bf16[2,1024,128]{2,1,0:T(8,128)(2,1)S(1)}, bf16[2,1024,128]{2,1,0:T(8,128)(2,1)S(1)}, u32[]{:S(2)}, u32[]{:S(2)}) collective-permute-start(bf16[2,1024,128]{2,1,0:T(8,128)(2,1)S(1)} %pad_maximum_fusion.3), channel_id=1, source_target_pairs={{0,8},{8,0},{16,24},{24,16},{1,9},{9,1},{17,25},{25,17},{2,10},{10... | collective-permute-start | bytes 1572872 | tf_op jit(solution)/shard_map/ppermute | solution.py:375
  307.6 9.2 %collective-permute-start.37 = (bf16[1024,128]{1,0:T(8,128)(2,1)S(1)}, bf16[1024,128]{1,0:T(8,128)(2,1)S(1)}, u32[]{:S(2)}, u32[]{:S(2)}) collective-permute-start(bf16[1024,128]{1,0:T(8,128)(2,1)S(1)} %fusion.2), channel_id=1, source_target_pairs={{0,16},{8,24},{16,0},{24,8},{1,17},{9,25},{17,1},{25,9},{2,18},{10... | collective-permute-start | bytes 786440 | tf_op jit(solution)/shard_map/ppermute | solution.py:375
  308.4 14.1 %collective-permute-start.49 = (bf16[1024,128]{1,0:T(8,128)(2,1)S(1)}, bf16[1024,128]{1,0:T(8,128)(2,1)S(1)}, u32[]{:S(2)}, u32[]{:S(2)}) collective-permute-start(bf16[1024,128]{1,0:T(8,128)(2,1)S(1)} %fusion.3), channel_id=1, source_target_pairs={{0,16},{8,24},{16,0},{24,8},{1,17},{9,25},{17,1},{25,9},{2,18},{10... | collective-permute-start | bytes 786440 | tf_op jit(solution)/shard_map/ppermute | solution.py:375
  310.1 16.9 %collective-permute-start.61 = (bf16[1024,128]{1,0:T(8,128)(2,1)S(1)}, bf16[1024,128]{1,0:T(8,128)(2,1)S(1)}, u32[]{:S(2)}, u32[]{:S(2)}) collective-permute-start(bf16[1024,128]{1,0:T(8,128)(2,1)S(1)} %fusion.4), channel_id=1, source_target_pairs={{0,16},{8,24},{16,0},{24,8},{1,17},{9,25},{17,1},{25,9},{2,18},{10... | collective-permute-start | bytes 786440 | tf_op jit(solution)/shard_map/ppermute | solution.py:375
  (57 other events, 827.8 us)
where the time goes:
time: 330 us; the launch traced here: 329 us
  Pallas kernels  137 us (42%)
  starting transfers between devices  101 us (31%)
  waiting for transfers between devices  75.7 us (23%)
  local copies, waits for them, and re-layouts  7.84 us (2%)
  other arithmetic  4.14 us (1%)
    ppermute x34, starting transfers between devices, along(): return lax.ppermute(value, 'expert', pairs)  74.4 us
    pallas_call x8, Pallas kernels, serve_piece(): pl.pallas_call(kernel, grid_spec=pltpu.PrefetchScalarGridSpec(num_scalar_...  45.7 us
    ppermute x34, waiting for transfers between devices, along(): return lax.ppermute(value, 'expert', pairs)  43.9 us
    pallas_call x8, Pallas kernels, adam_part(): pl.pallas_call(kernel, grid_spec=pltpu.PrefetchScalarGridSpec(num_scalar_...  34.3 us
    ppermute x20, waiting for transfers between devices, flip(): return lax.ppermute(value, 'dp', pairs)  31.1 us
    pallas_call x24, Pallas kernels, pick(): pl.pallas_call(kernel, grid_spec=pltpu.PrefetchScalarGridSpec(num_scalar_...  27.9 us
    pallas_call x12, Pallas kernels, slab_sum(): pl.pallas_call(kernel, grid_spec=pltpu.PrefetchScalarGridSpec(num_scalar_...  27.9 us
    ppermute x20, starting transfers between devices, flip(): return lax.ppermute(value, 'dp', pairs)  16.5 us
  transfers between devices with their start and end apart: 62, of which 15 were waited for; matrix products, arithmetic and copies ran while one was open for 1% of the time, Pallas kernels for 41%

commit v1 on v0

v1 whole, which is shorter than its diff:
```python
import jax
import jax.numpy as jnp
from jax import lax
from jax.experimental import pallas as pl
from jax.experimental.pallas import tpu as pltpu
from jax.sharding import PartitionSpec as P


EXPERTS = 4
QB = 128

beta_first = 0.9
beta_second = 0.95
learn_rate = 0.02
decay_rate = 0.1
adam_epsilon = 1e-08
scale_epsilon = 1e-06
quant_range = 448.0
grid_step = 8.0
bias_first = 1.0 - 0.9**20
bias_second = 1.0 - 0.95**20

ROW_PARTS = 2
TILE = 1024
UNROLL = 7
SUM_VMEM = 50 << 20
PICK_VMEM = 16 << 20
ADAM_VMEM = 57 << 20
SERVE_VMEM = 50 << 20


def adamw(gradient, master_weights, first_moment, second_moment):
    moment_one = beta_first * first_moment + (1.0 - beta_first) * gradient
    moment_two = beta_second * second_moment + (1.0 - beta_second) * gradient * gradient
    update = (moment_one * (1.0 / bias_first)) / (
        jnp.sqrt(moment_two * (1.0 / bias_second)) + adam_epsilon
    )
    return master_weights - learn_rate * (update + decay_rate * master_weights)


def params(limit):
    return pltpu.CompilerParams(vmem_limit_bytes=limit)


def total(refs):
    value = refs[0].astype(jnp.float32)
    for ref in refs[1:]:
        value = value + ref.astype(jnp.float32)
    return value


def slab_sum(grad, table, relative, received, rows, part_rows, part, cols, width):
    n_out = len(relative)
    skip = relative[1] - relative[0] if n_out > 1 else 0
    n_cols = len(cols)
    block = part_rows
    step = rows // block
    n_rows = part_rows // block

    def kernel(tab, *refs):
        grads, recs, out = refs[:n_cols], refs[n_cols:-1], refs[-1]
        for k in range(n_cols):
            span = slice(k * width, (k + 1) * width)
            values = [grads[k][...]] + [rec[0, :, span] for rec in recs]
            out[0, :, span] = total(values).astype(out.dtype)

    def grad_map(k):
        at = cols[k] // width
        return lambda i, r, tab: (jnp.bitwise_xor(tab[0], relative[0] + i * skip) * step + part * n_rows + r, at)

    def rec_map(stride, offset, first):
        return lambda i, r, tab: (first + i * stride, offset * n_rows + r, 0)

    in_specs = [pl.BlockSpec((block, width), grad_map(k)) for k in range(n_cols)]
    in_specs += [
        pl.BlockSpec((1, block, n_cols * width), rec_map(stride, offset, first))
        for (_, offset, first, stride) in received
    ]
    moved = n_out * part_rows * n_cols * width * 2
    return pl.pallas_call(
        kernel,
        grid_spec=pltpu.PrefetchScalarGridSpec(
            num_scalar_prefetch=1,
            grid=(n_out, n_rows),
            in_specs=in_specs,
            out_specs=pl.BlockSpec((1, block, n_cols * width), lambda i, r, tab: (i, r, 0)),
        ),
        out_shape=jax.ShapeDtypeStruct((n_out, part_rows, n_cols * width), jnp.bfloat16),
        compiler_params=params(SUM_VMEM),
        cost_estimate=pl.CostEstimate(
            flops=moved, bytes_accessed=moved * (2 + len(received)), transcendentals=0
        ),
        name="slab_sum",
    )(table, *([grad] * n_cols), *[item[0] for item in received])


def adam_parts(grad, table, received, state, out, rows, part_rows, parts, cols, width):
    n_cols = len(cols)
    block = part_rows
    step = rows // block
    n_parts = len(parts)
    first_part = parts[0]
    base = cols[0] // width
    stride = (cols[1] - cols[0]) // width if n_cols > 1 else 0
    n_rec = len(received)

    def kernel(tab, grad_ref, *refs):
        recs = refs[:n_rec]
        master, first, second = refs[n_rec : n_rec + 3]
        new_ref = refs[-1 - n_parts]
        deltas = refs[-n_parts:]
        gradient = total([grad_ref[...]] + [rec[0] for rec in recs])
        old = master[...]
        new = adamw(gradient, old, first[...], second[...])
        new_ref[...] = new
        change = (new - old).astype(jnp.bfloat16)
        if n_parts == 1:
            deltas[0][...] = change
        else:
            for h in range(n_parts):

                @pl.when(pl.program_id(0) == h)
                def _():
                    deltas[h][...] = change

    def state_map(r, k, tab):
        return (first_part + r, base + k * stride)

    state_spec = pl.BlockSpec((block, width), state_map)
    in_specs = [
        pl.BlockSpec((block, width), lambda r, k, tab: (tab[0] * step + first_part + r, base + k * stride))
    ]

    def rec_map(offset):
        return lambda r, k, tab: (0, offset + r, k)

    def delta_map(h):
        return lambda r, k, tab: (0, jnp.where(r == h, k, jnp.where(r < h, 0, n_cols - 1)))

    in_specs += [pl.BlockSpec((1, block, width), rec_map(offset)) for (_, offset) in received]
    in_specs += [state_spec] * 3
    operands = [table, grad, *[item[0] for item in received], *state]
    aliases = {}
    if out is not None:
        in_specs.append(pl.BlockSpec(memory_space=pl.ANY))
        aliases = {len(operands): 0}
        operands.append(out)
    count = n_parts * part_rows * n_cols * width
    result = pl.pallas_call(
        kernel,
        grid_spec=pltpu.PrefetchScalarGridSpec(
            num_scalar_prefetch=1,
            grid=(n_parts, n_cols),
            in_specs=in_specs,
            out_specs=(
                state_spec,
                *[pl.BlockSpec((block, width), delta_map(h)) for h in range(n_parts)],
            ),
        ),
        out_shape=(
            jax.ShapeDtypeStruct(state[0].shape, jnp.float32),
            *[jax.ShapeDtypeStruct((part_rows, n_cols * width), jnp.bfloat16)] * n_parts,
        ),
        input_output_aliases=aliases,
        compiler_params=params(ADAM_VMEM),
        cost_estimate=pl.CostEstimate(
            flops=30 * count, bytes_accessed=(20 + 2 * n_rec) * count, transcendentals=2 * count
        ),
        name="adam_parts",
    )(*operands)
    return result[0], result[1:]


def pick(table, code_of, parts):
    part_rows, cols = parts[0][0].shape
    n_parts, n_options = len(parts), len(parts[0])
    shape = (n_parts * part_rows, cols)

    def kernel(tab, *refs):
        out, sems = refs[-2:]
        code = code_of(tab)
        for k in range(n_options):

            @pl.when(code == k)
            def _():
                copies = [
                    pltpu.make_async_copy(
                        refs[h * n_options + k], out.at[pl.ds(h * part_rows, part_rows)], sems.at[h]
                    )
                    for h in range(n_parts)
                ]
                for copy in copies:
                    copy.start()
                for copy in copies:
                    copy.wait()

    return pl.pallas_call(
        kernel,
        grid_spec=pltpu.PrefetchScalarGridSpec(
            num_scalar_prefetch=1,
            grid=(1,),
            in_specs=[pl.BlockSpec(memory_space=pl.ANY)] * (n_parts * n_options),
            out_specs=pl.BlockSpec(shape, lambda i, tab: (0, 0)),
            scratch_shapes=[pltpu.SemaphoreType.DMA((n_parts,))],
        ),
        out_shape=jax.ShapeDtypeStruct(shape, parts[0][0].dtype),
        compiler_params=params(PICK_VMEM),
        cost_estimate=pl.CostEstimate(
            flops=0, bytes_accessed=4 * shape[0] * shape[1], transcendentals=0
        ),
        name="pick",
    )(table, *[option for options in parts for option in options])


def serve(tokens, resident, pieces, table, part_rows, stride, shift, width):
    rows_total, depth = tokens.shape
    n_pieces = len(pieces)
    n_parts = len(pieces[0][0])
    part_cols = pieces[0][0][0][0][0].shape[1]
    n_cols = part_cols // width
    tile = TILE if rows_total % TILE == 0 else rows_total
    counts = [len(parts[0]) for parts, _, _ in pieces]

    def kernel(tab, tokens_ref, resident_ref, *refs):
        outs = refs[-7 - n_cols : -7]
        tok, held, weight, delta, sems, held_sems, tok_sem = refs[-7:]
        at_ref = 0

        def fetch_resident(s, k):
            column = (tab[pieces[s][2][k]] * stride + shift) * width
            return pltpu.make_async_copy(
                resident_ref.at[:, pl.ds(pl.multiple_of(column, width), width)],
                held.at[s, k],
                held_sems.at[s, k],
            )

        fetch_tokens = pltpu.make_async_copy(tokens_ref, tok, tok_sem)

        def fetch(s, h, ref):
            return pltpu.make_async_copy(ref, delta.at[s, h], sems.at[s, h])

        for s, (parts, code_of, _) in enumerate(pieces):
            code = code_of(tab)
            for k in range(counts[s]):
                chosen = [
                    refs[at_ref + h * counts[s] + k].at[pl.ds(parts[h][k][1], part_rows)]
                    for h in range(n_parts)
                ]

                @pl.when(code == k)
                def _():
                    for h in range(n_parts):
                        fetch(s, h, chosen[h]).start()

            at_ref += n_parts * counts[s]
            for k in range(n_cols):
                fetch_resident(s, k).start()
        fetch_tokens.start()
        for s, (_, _, places) in enumerate(pieces):
            starts = [
                pl.multiple_of(lax.rem(tab[places[k]], n_cols) * width, width)
                for k in range(n_cols)
            ]
            for k in range(n_cols):
                fetch_resident(s, k).wait()
            for h in range(n_parts):
                fetch(s, h, delta.at[s, h]).wait()

                @pl.loop(0, part_rows // QB, unroll=UNROLL)
                def _(b):
                    at = pl.multiple_of(h * part_rows + b * QB, QB)
                    near = pl.multiple_of(b * QB, QB)
                    for k in range(n_cols):
                        for c in range(width // QB):
                            span = slice(c * QB, (c + 1) * QB)
                            change = delta[s, h, pl.ds(near, QB), pl.ds(starts[k] + c * QB, QB)]
                            value = held[s, k, pl.ds(at, QB), span].astype(
                                jnp.float32
                            ) + change.astype(jnp.float32)
                            largest = jnp.max(jnp.abs(value), axis=(0, 1), keepdims=True)
                            scale = (largest + scale_epsilon) / quant_range
                            level = jnp.floor(value * (1.0 / (scale * grid_step)) + 0.5)
                            column = (s * n_cols + k) * width + c * QB
                            weight[pl.ds(at, QB), column : column + QB] = (
                                level * (scale * grid_step)
                            ).astype(jnp.bfloat16)

        fetch_tokens.wait()

        @pl.loop(0, rows_total // tile)
        def _(m):
            at = pl.multiple_of(m * tile, tile)
            product = jnp.dot(
                tok[pl.ds(at, tile), :], weight[...], preferred_element_type=jnp.float32
            )
            for s in range(n_pieces):
                for k in range(n_cols):
                    column = (s * n_cols + k) * width
                    outs[k][s, pl.ds(at, tile), :] = product[:, column : column + width].astype(
                        jnp.bfloat16
                    )

    in_specs = [pl.BlockSpec(memory_space=pl.ANY)] * 2
    operands = [tokens, resident]
    for parts, _, _ in pieces:
        for options in parts:
            in_specs += [pl.BlockSpec(memory_space=pl.ANY)] * len(options)
            operands += [array for array, _ in options]
    out_spec = pl.BlockSpec((n_pieces, rows_total, width), lambda i, tab: (0, 0, 0))
    out_shape = jax.ShapeDtypeStruct((n_pieces, rows_total, width), jnp.bfloat16)
    return pl.pallas_call(
        kernel,
        grid_spec=pltpu.PrefetchScalarGridSpec(
            num_scalar_prefetch=1,
            grid=(1,),
            in_specs=in_specs,
            out_specs=(out_spec,) * n_cols,
            scratch_shapes=[
                pltpu.VMEM((rows_total, depth), jnp.bfloat16),
                pltpu.VMEM((n_pieces, n_cols, depth, width), jnp.bfloat16),
                pltpu.VMEM((depth, n_pieces * n_cols * width), jnp.bfloat16),
                pltpu.VMEM((n_pieces, n_parts, part_rows, part_cols), jnp.bfloat16),
                pltpu.SemaphoreType.DMA((n_pieces, n_parts)),
                pltpu.SemaphoreType.DMA((n_pieces, n_cols)),
                pltpu.SemaphoreType.DMA,
            ],
        ),
        out_shape=(out_shape,) * n_cols,
        compiler_params=params(SERVE_VMEM),
        cost_estimate=pl.CostEstimate(
            flops=2 * rows_total * depth * n_pieces * n_cols * width,
            bytes_accessed=2 * depth * (rows_total + 2 * n_pieces * n_cols * width),
            transcendentals=0,
        ),
        name="serve",
    )(table, *operands)


def make_table(here, owner_expert, group, n_cols, two_slots):
    place_at = 0
    code_at = place_at + group * n_cols
    flag_at = code_at + group
    last = EXPERTS - 1

    def kernel(spot, hosts, out):
        me = spot[0]
        plane = lax.div(spot[1], group)
        lane = lax.rem(spot[1], group)
        for s in range(group):
            piece = lax.rem(lane + group - s, group)
            for k in range(n_cols):
                column = jnp.bitwise_xor(jnp.bitwise_and(me, n_cols - 1), k)
                out[place_at + s * n_cols + k] = piece * n_cols + column
        outer = jnp.where(plane < EXPERTS // 2, 0, last)
        inner = jnp.where(plane < EXPERTS // 2, 1, last - 1)
        near = jnp.int32(0)
        far = jnp.int32(0)
        for j in range(group):
            host = hosts[outer * group + j]
            near = jnp.where(host == inner, 1, near)
            far = jnp.where(host == last - outer, 1, far)
        at_end = jnp.where(plane == outer, 1, 0)
        for s in range(group):
            expert = hosts[plane * group + lax.rem(lane + s, group)]
            if two_slots:
                first = jnp.where(near == 1, inner, last - inner)
                code_end = jnp.where(expert == first, 2, 3)
                code_mid = jnp.where(expert == outer, 1, jnp.where(expert == last - plane, 4, 5))
                code = jnp.where(at_end == 1, code_end, code_mid)
            else:
                code = jnp.where(expert < plane, plane - expert, last + expert - plane)
            out[code_at + s] = jnp.where(expert == plane, 0, code)
        out[flag_at] = near
        out[flag_at + 1] = far
        out[flag_at + 2] = at_end
        out[flag_at + 3] = jnp.where(lane == lax.div(me, 2), 1, 0)

    table = pl.pallas_call(
        kernel,
        in_specs=[pl.BlockSpec(memory_space=pltpu.SMEM)] * 2,
        out_specs=pl.BlockSpec(memory_space=pltpu.SMEM),
        out_shape=jax.ShapeDtypeStruct((flag_at + 4,), jnp.int32),
        name="make_table",
    )(here, owner_expert)
    return table, place_at, code_at, flag_at


def body(
    grad_partials,
    master_weights,
    first_moment,
    second_moment,
    resident_weights,
    token_tiles,
    owner_expert,
    live_rows,
):
    n_dp = lax.axis_size("dp")
    n_expert = lax.axis_size("expert")
    group = n_expert // EXPERTS
    me = lax.axis_index("dp")
    own = lax.axis_index("expert")
    lane = own % group
    levels = n_dp.bit_length() - 1
    assert 1 << levels == n_dp and EXPERTS * group == n_expert

    rows, piece_cols = master_weights.shape
    owner_cols = resident_weights.shape[1]
    dp_cols = owner_cols // n_dp
    n_cols = piece_cols // dp_cols
    assert n_cols in (1, 2) and n_cols * dp_cols == piece_cols
    width = QB
    n_chunks = dp_cols // width
    parts = ROW_PARTS if rows % (ROW_PARTS * QB) == 0 else 1
    part_rows = rows // parts
    grad = grad_partials.reshape(n_dp * rows, piece_cols)
    state = (master_weights, first_moment, second_moment)

    two_slots = EXPERTS == 4 and group == 2
    here = jnp.stack([me, own]).astype(jnp.int32)
    table, place_at, code_at, flag_at = make_table(
        here, owner_expert, group, n_cols, two_slots
    )

    def flip(value, level):
        pairs = [(i, i ^ (1 << level)) for i in range(n_dp)]
        return lax.ppermute(value, "dp", pairs)

    def along(value, moves):
        pairs = [(a * group + j, b * group + j) for (a, b) in moves for j in range(group)]
        return lax.ppermute(value, "expert", pairs)

    columns = [[k * dp_cols + c * width for k in range(n_cols)] for c in range(n_chunks)]
    updated_master = None
    delta = [[None] * n_chunks for _ in range(parts)]

    def relative(level):
        return [(1 << level) + i * (2 << level) for i in range(n_dp >> (level + 1))]

    together = [[[h] for h in range(parts)] if c == 0 else [list(range(parts))] for c in range(n_chunks)]
    crossed_first = {}
    for c in range(n_chunks):
        for held in together[c]:
            held_rows = part_rows * len(held)
            first_part = held[0] // len(held)
            send = slab_sum(
                grad, here, relative(0), [], rows, held_rows, first_part, columns[c], width
            )
            crossed_first[c, held[0]] = flip(send, 0)
    for c in range(n_chunks):
        for held in together[c]:
            held_rows = part_rows * len(held)
            received = [(crossed_first[c, held[0]], 0)]
            for level in range(1, levels):
                feed = []
                for j, (array, offset) in enumerate(received):
                    feed.append(
                        (
                            array,
                            offset,
                            (1 << level) >> (j + 1),
                            (2 << level) >> (j + 1),
                        )
                    )
                send = slab_sum(
                    grad,
                    here,
                    relative(level),
                    feed,
                    rows,
                    held_rows,
                    held[0] // len(held),
                    columns[c],
                    width,
                )
                received.append((flip(send, level), 0))
            for h in held:
                updated_master, changes = adam_parts(
                    grad,
                    here,
[(array, h - held[0]) for array, _ in received],
                    state,
                    updated_master,
                    rows,
                    part_rows,
                    [h],
                    columns[c],
                    width,
                )
                delta[h][c] = changes[0]

    last = EXPERTS - 1

    def at(index):
        return lambda tab: tab[index]

    def full_line(pieces):
        found = []
        for piece in pieces:
            options = [piece]
            for side in range(2):
                value = piece
                for k in range(1, EXPERTS):
                    moves = [(p, p + 1) for p in range(k - 1, last)]
                    if side:
                        moves = [(last - a, last - b) for a, b in moves]
                    value = along(value, moves)
                    options.append(value)
            found.append(options)
        return found

    def slotted_line(pieces):
        sides = [(0, 1), (1, 0), (2, 3), (3, 2)]
        middle = [(1, 2), (2, 1)]
        count = len(pieces)
        side, center = [], []

        def odd_code(tab):
            return 1 - tab[flag_at]

        def even_code(tab):
            return jnp.where(tab[flag_at + 2] == 1, 2, tab[flag_at + 1])

        def last_code(tab):
            return tab[flag_at + 1]

        for t in range(2 * count + 1):
            c = t // 2
            if t == 0:
                value = pieces[0]
            else:
                if t % 2:
                    value = pick(table, odd_code, [[pieces[c], center[2 * c]]])
                elif c < count:
                    choices = [center[t - 2], center[t - 1], pieces[c]]
                    value = pick(table, even_code, [choices])
                else:
                    value = pick(table, last_code, [[center[t - 2], center[t - 1]]])
            side.append(along(value, sides))
            if t < 2 * count:
                center.append(along(side[t - 1] if t % 2 else pieces[c], middle))
        return [
            [pieces[c], *side[2 * c : 2 * c + 3], *center[2 * c : 2 * c + 2]] for c in range(count)
        ]

    if two_slots:
        options = [slotted_line(delta[h]) for h in range(parts)]
    else:
        options = [full_line(delta[h]) for h in range(parts)]

    moved = [[[None] * parts for _ in range(n_chunks)] for _ in range(group)]
    for c in range(n_chunks):
        groups = [[h] for h in range(parts)] if c == n_chunks - 1 else [list(range(parts))]
        for held in groups:
            for s in range(1, group):
                value = pick(table, at(code_at + s), [options[h][c] for h in held])
                pairs = [
                    (e * group + j, e * group + (j + s) % group)
                    for e in range(EXPERTS)
                    for j in range(group)
                ]
                value = lax.ppermute(value, "expert", pairs)
                for h in held:
                    moved[s][c][h] = (value, (h - held[0]) * part_rows)

    def piece_of(c, s):
        if s == 0:
            sources = [[(array, 0) for array in options[h][c]] for h in range(parts)]
            code_of = at(code_at)
        else:
            sources, code_of = [[moved[s][c][h]] for h in range(parts)], lambda tab: 0
        return sources, code_of, [place_at + s * n_cols + k for k in range(n_cols)]

    sums = []
    parity = (me % 2).astype(jnp.int32)
    for c in range(n_chunks):
        pieces = [piece_of(c, s) for s in range(group)]
        groups = [[piece] for piece in pieces]
        results = []
        for chosen in groups:
            results.append(
                serve(token_tiles, resident_weights, chosen, table, part_rows, n_chunks, c, width)
            )
        if n_dp == 4 and group == 2:
            kept = []
            for straight_sums, crossed_sums in results:
                crossed = flip(crossed_sums, 0)
                for s in range(straight_sums.shape[0]):
                    kept.append(straight_sums[s].astype(jnp.float32) + crossed[s].astype(jnp.float32))
            straight = table[flag_at + 3] == 1
            other = jnp.where(straight, kept[1], kept[0]).astype(jnp.bfloat16)
            held = jnp.where(straight, kept[0], kept[1])
            crossed = flip(other, 1)
            sums.append(held + crossed.astype(jnp.float32))
        else:
            products = [
                [result[k][s] for k in range(n_cols)]
                for result in results
                for s in range(result[0].shape[0])
            ]
            buffer = jnp.zeros((n_dp,) + products[0][0].shape, jnp.bfloat16)
            for s in range(group):
                piece = (lane - s) % group
                for k in range(n_cols):
                    column = piece * n_cols + ((k ^ parity) if n_cols == 2 else 0)
                    buffer = lax.dynamic_update_index_in_dim(
                        buffer, products[s][k], jnp.bitwise_xor(column, me), 0
                    )
            for level in range(levels):
                got = flip(buffer[1::2], level).astype(jnp.float32)
                buffer = (buffer[0::2].astype(jnp.float32) + got).astype(
                    jnp.bfloat16 if level < levels - 1 else jnp.float32
                )
            sums.append(buffer[0])
    summed = jnp.concatenate(sums, axis=1)
    row_index = lax.broadcasted_iota(jnp.int32, summed.shape, 0)
    projected = jnp.where(row_index < live_rows[0], summed, jnp.float32(0.0)).astype(jnp.bfloat16)
    return (updated_master, projected)


def solution(mesh):
    placed = (
        P("dp", None, "expert"),
        P("dp", "expert"),
        P("dp", "expert"),
        P("dp", "expert"),
        P("dp", "expert"),
        P("expert", "dp"),
        P(),
        P("expert"),
    )

    return jax.shard_map(
        body,
        mesh=mesh,
        in_specs=placed,
        out_specs=(P("dp", "expert"), P("expert", "dp")),
        check_vma=False,
    )
```

time: 330 us -> 314 us (0.952)
  Pallas kernels: 137 us -> 128 us
    ppermute x8 -> x5, waiting for transfers between devices: 0.64 us -> 10.9 us  [body(): value = lax.ppermute(value, 'expert', pairs)]
    pallas_call x16, Pallas kernels: 80 us -> 70.8 us  [the longest x8 36.5 us: serve(): pl.pallas_call(kernel, grid_spec=pltpu.PrefetchScalarGridSpec(num_scalar_...]
    ppermute x20 -> x22, waiting for transfers between devices: 31.1 us -> 23.2 us  [flip(): return lax.ppermute(value, 'dp', pairs)]
    ppermute x34, waiting for transfers between devices: 43.9 us -> 38.3 us  [along(): return lax.ppermute(value, 'expert', pairs)]
    ppermute x34, starting transfers between devices: 74.4 us -> 78.1 us  [along(): return lax.ppermute(value, 'expert', pairs)]
    ppermute x8 -> x5, starting transfers between devices: 9.77 us -> 6.42 us  [body(): value = lax.ppermute(value, 'expert', pairs)]
    pallas_call x24 -> x21, Pallas kernels: 27.9 us -> 31.2 us  [pick(): pl.pallas_call(kernel, grid_spec=pltpu.PrefetchScalarGridSpec(num_scalar_...]
    pallas_call x12 -> x10, Pallas kernels: 27.9 us -> 24.8 us  [slab_sum(): pl.pallas_call(kernel, grid_spec=pltpu.PrefetchScalarGridSpec(num_scalar_...]
  transfers between devices with their start and end apart: 62 -> 61, of which waited for: 15 -> 17; matrix products, arithmetic and copies ran while one was open for 1% -> 1% of each run, Pallas kernels for 41% -> 40%
where the time goes in v1:
time: 314 us; the launch traced here: 313 us
  Pallas kernels  128 us (41%)
  starting transfers between devices  100 us (32%)
  waiting for transfers between devices  72.4 us (23%)
  local copies, waits for them, and re-layouts  6.04 us (2%)
  other arithmetic  3.37 us (1%)
    ppermute x34, starting transfers between devices, along(): return lax.ppermute(value, 'expert', pairs)  78.1 us
    ppermute x34, waiting for transfers between devices, along(): return lax.ppermute(value, 'expert', pairs)  38.3 us
    pallas_call x8, Pallas kernels, serve(): pl.pallas_call(kernel, grid_spec=pltpu.PrefetchScalarGridSpec(num_scalar_...  36.5 us
    pallas_call x8, Pallas kernels, adam_parts(): pl.pallas_call(kernel, grid_spec=pltpu.PrefetchScalarGridSpec(num_scalar_...  34.4 us
    pallas_call x21, Pallas kernels, pick(): pl.pallas_call(kernel, grid_spec=pltpu.PrefetchScalarGridSpec(num_scalar_...  31.2 us
    pallas_call x10, Pallas kernels, slab_sum(): pl.pallas_call(kernel, grid_spec=pltpu.PrefetchScalarGridSpec(num_scalar_...  24.8 us
    ppermute x22, waiting for transfers between devices, flip(): return lax.ppermute(value, 'dp', pairs)  23.2 us
    ppermute x22, starting transfers between devices, flip(): return lax.ppermute(value, 'dp', pairs)  15.7 us
  transfers between devices with their start and end apart: 61, of which 17 were waited for; matrix products, arithmetic and copies ran while one was open for 1% of the time, Pallas kernels for 40%

profile of v1, /device:TPU:0, one launch (start us, length us, event | category | flops | bytes accessed | tf_op | source)
XLA Modules:
  0.0 312.9 jit_solution(6387147545231320657)
XLA Ops:
  0.7 3.1 %slab_sum.14 = bf16[2,1792,256]{2,1,0:T(8,128)(2,1)} custom-call(s32[2]{0:T(128)S(1)} %pad_add_fusion.tab.spot, bf16[7168,1024]{1,0:T(8,128)(2,1)} %bitcast.22, bf16[7168,1024]{1,0:T(8,128)(2,1)} %bitcast.23), custom_call_target="tpu_custom_call" | custom-call | flops 1835008 | bytes 3670016 | tf_op jit(solution)/shard_map/slab_sum/pallas_call | solution.py:80
  4.3 2.0 slab_sum.18
  6.4 2.0 slab_sum.16
  8.9 3.2 %slab_sum.12 = bf16[2,1792,256]{2,1,0:T(8,128)(2,1)} custom-call(s32[2]{0:T(128)S(1)} %pad_add_fusion.tab.spot, bf16[7168,1024]{1,0:T(8,128)(2,1)} %bitcast.28, bf16[7168,1024]{1,0:T(8,128)(2,1)} %bitcast.29), custom_call_target="tpu_custom_call" | custom-call | flops 1835008 | bytes 3670016 | tf_op jit(solution)/shard_map/slab_sum/pallas_call | solution.py:80
  12.1 1.7 slab_sum.19
  13.9 3.0 collective-permute-start.9
  16.9 1.7 slab_sum.17
  18.7 3.1 %slab_sum.10 = bf16[2,1792,256]{2,1,0:T(8,128)(2,1)} custom-call(s32[2]{0:T(128)S(1)} %pad_add_fusion.tab.spot, bf16[7168,1024]{1,0:T(8,128)(2,1)} %bitcast.35, bf16[7168,1024]{1,0:T(8,128)(2,1)} %bitcast.34), custom_call_target="tpu_custom_call" | custom-call | flops 1835008 | bytes 3670016 | tf_op jit(solution)/shard_map/slab_sum/pallas_call | solution.py:80
  21.9 6.5 %collective-permute-done.9.refs_1_ = bf16[1,896,256]{2,1,0:T(8,128)(2,1)} collective-permute-done((bf16[1,896,256]{2,1,0:T(8,128)(2,1)S(1)}, bf16[1,896,256]{2,1,0:T(8,128)(2,1)}, u32[]{:S(2)}, u32[]{:S(2)}) %collective-permute-start.9) | collective-permute-done | bytes 458784 | tf_op jit(solution)/shard_map/ppermute | solution.py:427
  28.4 4.2 %adam_parts.8 = (f32[1792,1024]{1,0:T(8,128)}, bf16[896,256]{1,0:T(8,128)(2,1)}) custom-call(s32[2]{0:T(128)} %copy-done.43, bf16[7168,1024]{1,0:T(8,128)(2,1)} %bitcast.36, bf16[2,896,256]{2,1,0:T(8,128)(2,1)} %copy-done.30, bf16[1,896,256]{2,1,0:T(8,128)(2,1)} %collective-permute-done.9.refs_1_, f32[1792,1024]{1,0:T(8,128)} %refs_2_.15, ...), custom_call_target="tpu_custom_call" | custom-call | flops 6881280 | bytes 5505024 | tf_op jit(solution)/shard_map/adam_parts/pallas_call | solution.py:149
  32.6 4.9 %collective-permute-done.7.refs_1_ = bf16[1,896,256]{2,1,0:T(8,128)(2,1)} collective-permute-done((bf16[1,896,256]{2,1,0:T(8,128)(2,1)S(1)}, bf16[1,896,256]{2,1,0:T(8,128)(2,1)}, u32[]{:S(2)}, u32[]{:S(2)}) %collective-permute-start.7) | collective-permute-done | bytes 458784 | tf_op jit(solution)/shard_map/ppermute | solution.py:427
  37.5 4.3 %adam_parts.9 = (f32[1792,1024]{1,0:T(8,128)}, bf16[896,256]{1,0:T(8,128)(2,1)}) custom-call(s32[2]{0:T(128)} %copy-done.43, bf16[7168,1024]{1,0:T(8,128)(2,1)} %bitcast.37, bf16[2,896,256]{2,1,0:T(8,128)(2,1)} %copy-done.29, bf16[1,896,256]{2,1,0:T(8,128)(2,1)} %collective-permute-done.7.refs_1_, ...), custom_call_target="tpu_custom_call", output_to_operand_aliasing={{0}: (7, {})} | custom-call | flops 6881280 | bytes 5505024 | tf_op jit(solution)/shard_map/adam_parts/pallas_call | solution.py:149
  41.9 1.9 collective-permute-start.15
  43.8 2.0 slab_sum.15
  48.1 6.0 %collective-permute-done.15.refs_7_ = bf16[896,256]{1,0:T(8,128)(2,1)} collective-permute-done((bf16[896,256]{1,0:T(8,128)(2,1)}, bf16[896,256]{1,0:T(8,128)(2,1)}, u32[]{:S(2)}, u32[]{:S(2)}) %collective-permute-start.15) | collective-permute-done | bytes 458784 | tf_op jit(solution)/shard_map/ppermute | solution.py:431
  57.1 2.9 slab_sum.13
  61.6 3.6 %collective-permute-done.10.refs_1_ = bf16[896,256]{1,0:T(8,128)(2,1)} collective-permute-done((bf16[896,256]{1,0:T(8,128)(2,1)S(1)}, bf16[896,256]{1,0:T(8,128)(2,1)}, u32[]{:S(2)}, u32[]{:S(2)}) %collective-permute-start.10) | collective-permute-done | bytes 458784 | tf_op jit(solution)/shard_map/ppermute | solution.py:431
  65.9 3.2 %collective-permute-done.5.refs_1_ = bf16[1,1792,256]{2,1,0:T(8,128)(2,1)S(1)} collective-permute-done((bf16[1,1792,256]{2,1,0:T(8,128)(2,1)S(1)}, bf16[1,1792,256]{2,1,0:T(8,128)(2,1)S(1)}, u32[]{:S(2)}, u32[]{:S(2)}) %collective-permute-start.5) | collective-permute-done | bytes 917536 | tf_op jit(solution)/shard_map/ppermute | solution.py:427
  72.7 4.2 %adam_parts.10 = (f32[1792,1024]{1,0:T(8,128)}, bf16[896,256]{1,0:T(8,128)(2,1)}) custom-call(s32[2]{0:T(128)} %copy-done.43, bf16[7168,1024]{1,0:T(8,128)(2,1)} %bitcast.42, bf16[2,1792,256]{2,1,0:T(8,128)(2,1)} %copy-done.2, bf16[1,1792,256]{2,1,0:T(8,128)(2,1)} %copy-done.46, f32[1792,1024]{1,0:T(8,128)} %refs_2_.15, ...), custom_call_target="tpu_custom_call", output_to_operand_aliasing={{0}: (7, {})} | custom-call | flops 6881280 | bytes 5505024 | tf_op jit(solution)/shard_map/adam_parts/pallas_call | solution.py:149
  77.0 4.4 %adam_parts.11 = (f32[1792,1024]{1,0:T(8,128)}, bf16[896,256]{1,0:T(8,128)(2,1)}) custom-call(s32[2]{0:T(128)} %copy-done.43, bf16[7168,1024]{1,0:T(8,128)(2,1)} %bitcast.43, bf16[2,1792,256]{2,1,0:T(8,128)(2,1)} %copy-done.2, bf16[1,1792,256]{2,1,0:T(8,128)(2,1)} %copy-done.46, f32[1792,1024]{1,0:T(8,128)} %refs_2_.15, ...), custom_call_target="tpu_custom_call", output_to_operand_aliasing={{0}: (7, {})} | custom-call | flops 6881280 | bytes 5505024 | tf_op jit(solution)/shard_map/adam_parts/pallas_call | solution.py:149
  83.0 2.9 collective-permute-start.19
  86.8 5.5 %collective-permute-start.14 = (bf16[896,256]{1,0:T(8,128)(2,1)S(1)}, bf16[896,256]{1,0:T(8,128)(2,1)S(1)}, u32[]{:S(2)}, u32[]{:S(2)}) collective-permute-start(bf16[896,256]{1,0:T(8,128)(2,1)S(1)} %pick.22), channel_id=1, source_target_pairs={{0,2},{1,3},{2,0},{3,1},{4,6},{5,7},{6,4},{7,5},{8,10},{9,11},{10,... | collective-permute-start | bytes 1376264 | tf_op jit(solution)/shard_map/ppermute | solution.py:431
  94.1 3.0 slab_sum.11
  97.1 2.3 collective-permute-start.1
  100.0 2.2 collective-permute-done.14.refs_3_.refs_1_
  103.7 5.9 %collective-permute-start.17 = (bf16[896,256]{1,0:T(8,128)(2,1)S(1)}, bf16[896,256]{1,0:T(8,128)(2,1)S(1)}, u32[]{:S(2)}, u32[]{:S(2)}) collective-permute-start(bf16[896,256]{1,0:T(8,128)(2,1)S(1)} %pick.23), channel_id=1, source_target_pairs={{0,2},{1,3},{2,0},{3,1},{4,6},{5,7},{6,4},{7,5},{8,10},{9,11},{10,... | collective-permute-start | bytes 1376264 | tf_op jit(solution)/shard_map/ppermute | solution.py:431
  109.6 1.6 pick.21
  111.3 6.5 %collective-permute-start.12 = (bf16[896,256]{1,0:T(8,128)(2,1)}, bf16[896,256]{1,0:T(8,128)(2,1)S(1)}, u32[]{:S(2)}, u32[]{:S(2)}) collective-permute-start(bf16[896,256]{1,0:T(8,128)(2,1)} %pick.21), channel_id=1, source_target_pairs={{0,2},{1,3},{2,0},{3,1},{4,6},{5,7},{6,4},{7,5},{8,10},{9,11},{10,... | collective-permute-start | bytes 1376264 | tf_op jit(solution)/shard_map/ppermute | solution.py:431
  117.7 4.2 %adam_parts.12 = (f32[1792,1024]{1,0:T(8,128)}, bf16[896,256]{1,0:T(8,128)(2,1)}) custom-call(s32[2]{0:T(128)} %copy-done.43, bf16[7168,1024]{1,0:T(8,128)(2,1)} %bitcast.46, bf16[2,1792,256]{2,1,0:T(8,128)(2,1)} %copy-done.1, bf16[1,1792,256]{2,1,0:T(8,128)(2,1)} %collective-permute-done.3.refs_1_, ...), custom_call_target="tpu_custom_call", output_to_operand_aliasing={{0}: (7, {})} | custom-call | flops 6881280 | bytes 5505024 | tf_op jit(solution)/shard_map/adam_parts/pallas_call | solution.py:149
  122.0 4.4 %adam_parts.13 = (f32[1792,1024]{1,0:T(8,128)}, bf16[896,256]{1,0:T(8,128)(2,1)}) custom-call(s32[2]{0:T(128)} %copy-done.43, bf16[7168,1024]{1,0:T(8,128)(2,1)} %bitcast.47, bf16[2,1792,256]{2,1,0:T(8,128)(2,1)} %copy-done.1, bf16[1,1792,256]{2,1,0:T(8,128)(2,1)} %collective-permute-done.3.refs_1_, ...), custom_call_target="tpu_custom_call", output_to_operand_aliasing={{0}: (7, {})} | custom-call | flops 6881280 | bytes 5505024 | tf_op jit(solution)/shard_map/adam_parts/pallas_call | solution.py:149
  129.7 6.6 %collective-permute-start.27 = (bf16[896,256]{1,0:T(8,128)(2,1)S(1)}, bf16[896,256]{1,0:T(8,128)(2,1)S(1)}, u32[]{:S(2)}, u32[]{:S(2)}) collective-permute-start(bf16[896,256]{1,0:T(8,128)(2,1)S(1)} %pick.27), channel_id=1, source_target_pairs={{0,2},{1,3},{2,0},{3,1},{4,6},{5,7},{6,4},{7,5},{8,10},{9,11},{10,... | collective-permute-start | bytes 1376264 | tf_op jit(solution)/shard_map/ppermute | solution.py:431
  140.0 4.5 %collective-permute-start.29 = (bf16[896,256]{1,0:T(8,128)(2,1)S(1)}, bf16[896,256]{1,0:T(8,128)(2,1)S(1)}, u32[]{:S(2)}, u32[]{:S(2)}) collective-permute-start(bf16[896,256]{1,0:T(8,128)(2,1)S(1)} %pick.28), channel_id=1, source_target_pairs={{0,2},{1,3},{2,0},{3,1},{4,6},{5,7},{6,4},{7,5},{8,10},{9,11},{10,... | collective-permute-start | bytes 1376264 | tf_op jit(solution)/shard_map/ppermute | solution.py:431
  145.3 3.0 collective-permute-done.27.refs_3_.refs_1_
  149.0 1.6 pick.26
  150.6 4.4 %collective-permute-start.25 = (bf16[896,256]{1,0:T(8,128)(2,1)}, bf16[896,256]{1,0:T(8,128)(2,1)}, u32[]{:S(2)}, u32[]{:S(2)}) collective-permute-start(bf16[896,256]{1,0:T(8,128)(2,1)} %pick.26), channel_id=1, source_target_pairs={{0,2},{1,3},{2,0},{3,1},{4,6},{5,7},{6,4},{7,5},{8,10},{9,11},{10,... | collective-permute-start | bytes 1376264 | tf_op jit(solution)/shard_map/ppermute | solution.py:431
  157.1 2.1 pick.25
  160.8 2.3 pick.33
  163.1 3.2 %collective-permute-start.41 = (bf16[896,256]{1,0:T(8,128)(2,1)}, bf16[896,256]{1,0:T(8,128)(2,1)S(1)}, u32[]{:S(2)}, u32[]{:S(2)}) collective-permute-start(bf16[896,256]{1,0:T(8,128)(2,1)} %pick.33), channel_id=1, source_target_pairs={{0,2},{1,3},{2,0},{3,1},{4,6},{5,7},{6,4},{7,5},{8,10},{9,11},{10,... | collective-permute-start | bytes 1376264 | tf_op jit(solution)/shard_map/ppermute | solution.py:431
  166.3 1.6 pick.31
  168.0 4.2 %collective-permute-start.37 = (bf16[896,256]{1,0:T(8,128)(2,1)}, bf16[896,256]{1,0:T(8,128)(2,1)}, u32[]{:S(2)}, u32[]{:S(2)}) collective-permute-start(bf16[896,256]{1,0:T(8,128)(2,1)} %pick.31), channel_id=1, source_target_pairs={{0,2},{1,3},{2,0},{3,1},{4,6},{5,7},{6,4},{7,5},{8,10},{9,11},{10,... | collective-permute-start | bytes 1376264 | tf_op jit(solution)/shard_map/ppermute | solution.py:431
  172.2 4.2 %adam_parts.14 = (f32[1792,1024]{1,0:T(8,128)}, bf16[896,256]{1,0:T(8,128)(2,1)}) custom-call(s32[2]{0:T(128)} %copy-done.43, bf16[7168,1024]{1,0:T(8,128)(2,1)} %bitcast.48, bf16[2,1792,256]{2,1,0:T(8,128)(2,1)} %copy-done, bf16[1,1792,256]{2,1,0:T(8,128)(2,1)} %collective-permute-done.1.refs_1_, ...), custom_call_target="tpu_custom_call", output_to_operand_aliasing={{0}: (7, {})} | custom-call | flops 6881280 | bytes 5505024 | tf_op jit(solution)/shard_map/adam_parts/pallas_call | solution.py:149
  176.4 4.4 %adam_parts.15 = (f32[1792,1024]{1,0:T(8,128)}, bf16[896,256]{1,0:T(8,128)(2,1)}) custom-call(s32[2]{0:T(128)} %copy-done.43, bf16[7168,1024]{1,0:T(8,128)(2,1)} %bitcast.49, bf16[2,1792,256]{2,1,0:T(8,128)(2,1)} %copy-done, bf16[1,1792,256]{2,1,0:T(8,128)(2,1)} %collective-permute-done.1.refs_1_, ...), custom_call_target="tpu_custom_call", output_to_operand_aliasing={{0}: (7, {})} | custom-call | flops 6881280 | bytes 5505024 | tf_op jit(solution)/shard_map/adam_parts/pallas_call | solution.py:149
  183.4 2.1 collective-permute-start.39
  188.6 2.8 pick.30
  191.4 6.2 %collective-permute-done.43.refs_9_.refs_7_.refs_1_ = bf16[896,256]{1,0:T(8,128)(2,1)S(1)} collective-permute-done((bf16[896,256]{1,0:T(8,128)(2,1)S(1)}, bf16[896,256]{1,0:T(8,128)(2,1)S(1)}, u32[]{:S(2)}, u32[]{:S(2)}) %collective-permute-start.43) | collective-permute-done | bytes 458784 | tf_op jit(solution)/shard_map/ppermute | solution.py:431
  199.0 6.3 %collective-permute-done.39.refs_3_.refs_1_ = bf16[896,256]{1,0:T(8,128)(2,1)S(1)} collective-permute-done((bf16[896,256]{1,0:T(8,128)(2,1)S(1)}, bf16[896,256]{1,0:T(8,128)(2,1)S(1)}, u32[]{:S(2)}, u32[]{:S(2)}) %collective-permute-start.39) | collective-permute-done | bytes 458784 | tf_op jit(solution)/shard_map/ppermute | solution.py:431
  205.3 2.8 pick.35
  209.4 4.5 %serve.8 = (bf16[1,1024,128]{2,1,0:T(8,128)(2,1)S(1)}, bf16[1,1024,128]{2,1,0:T(8,128)(2,1)S(1)}) custom-call(s32[10]{0:T(128)S(1)} %copy-done.42, bf16[1024,1792]{1,0:T(8,128)(2,1)} %tokens_ref.15, bf16[1792,2048]{1,0:T(8,128)(2,1)} %resident_ref.15, bf16[896,256]{1,0:T(8,128)(2,1)S(1)} %copy-done.15, bf16[896,256]{1,0:T(8,128)(2,1)} %collective-permute-done.10.refs_1_, ...), custom_call_target="tpu_custom_call" | custom-call | flops 939524096 | bytes 5505024 | tf_op jit(solution)/shard_map/serve/pallas_call | solution.py:311
  214.0 4.9 %serve.9 = (bf16[1,1024,128]{2,1,0:T(8,128)(2,1)S(1)}, bf16[1,1024,128]{2,1,0:T(8,128)(2,1)S(1)}) custom-call(s32[10]{0:T(128)S(1)} %copy-done.42, bf16[1024,1792]{1,0:T(8,128)(2,1)} %tokens_ref.15, bf16[1792,2048]{1,0:T(8,128)(2,1)} %resident_ref.15, bf16[1792,256]{1,0:T(8,128)(2,1)} %collective-permute-done.21.refs_0_.refs_1_, ...), custom_call_target="tpu_custom_call" | custom-call | flops 939524096 | bytes 5505024 | tf_op jit(solution)/shard_map/serve/pallas_call | solution.py:311
  222.5 6.2 %collective-permute-start.53 = (bf16[896,256]{1,0:T(8,128)(2,1)S(1)}, bf16[896,256]{1,0:T(8,128)(2,1)S(1)}, u32[]{:S(2)}, u32[]{:S(2)}) collective-permute-start(bf16[896,256]{1,0:T(8,128)(2,1)S(1)} %pick.38), channel_id=1, source_target_pairs={{0,2},{1,3},{2,0},{3,1},{4,6},{5,7},{6,4},{7,5},{8,10},{9,11},{10,... | collective-permute-start | bytes 1376264 | tf_op jit(solution)/shard_map/ppermute | solution.py:431
  232.5 4.4 %serve.10 = (bf16[1,1024,128]{2,1,0:T(8,128)(2,1)S(1)}, bf16[1,1024,128]{2,1,0:T(8,128)(2,1)S(1)}) custom-call(s32[10]{0:T(128)S(1)} %copy-done.42, bf16[1024,1792]{1,0:T(8,128)(2,1)} %tokens_ref.15, bf16[1792,2048]{1,0:T(8,128)(2,1)} %resident_ref.15, bf16[896,256]{1,0:T(8,128)(2,1)S(1)} %copy-done.5, ...), custom_call_target="tpu_custom_call" | custom-call | flops 939524096 | bytes 5505024 | tf_op jit(solution)/shard_map/serve/pallas_call | solution.py:311
  237.8 8.0 %collective-permute-start.49 = (bf16[896,256]{1,0:T(8,128)(2,1)S(1)}, bf16[896,256]{1,0:T(8,128)(2,1)S(1)}, u32[]{:S(2)}, u32[]{:S(2)}) collective-permute-start(bf16[896,256]{1,0:T(8,128)(2,1)S(1)} %pick.36), channel_id=1, source_target_pairs={{0,2},{1,3},{2,0},{3,1},{4,6},{5,7},{6,4},{7,5},{8,10},{9,11},{10,... | collective-permute-start | bytes 1376264 | tf_op jit(solution)/shard_map/ppermute | solution.py:431
  246.7 2.0 collective-permute-start.51
  248.7 4.6 %serve.11 = (bf16[1,1024,128]{2,1,0:T(8,128)(2,1)S(1)}, bf16[1,1024,128]{2,1,0:T(8,128)(2,1)S(1)}) custom-call(s32[10]{0:T(128)S(1)} %copy-done.42, bf16[1024,1792]{1,0:T(8,128)(2,1)} %tokens_ref.15, bf16[1792,2048]{1,0:T(8,128)(2,1)} %resident_ref.15, bf16[1792,256]{1,0:T(8,128)(2,1)S(1)} %collective-permute-done.33.refs_0_.refs_1_, ...), custom_call_target="tpu_custom_call" | custom-call | flops 939524096 | bytes 5505024 | tf_op jit(solution)/shard_map/serve/pallas_call | solution.py:311
  254.8 4.4 %serve.12 = (bf16[1,1024,128]{2,1,0:T(8,128)(2,1)S(1)}, bf16[1,1024,128]{2,1,0:T(8,128)(2,1)S(1)}) custom-call(s32[10]{0:T(128)S(1)} %copy-done.42, bf16[1024,1792]{1,0:T(8,128)(2,1)} %tokens_ref.15, bf16[1792,2048]{1,0:T(8,128)(2,1)} %resident_ref.15, bf16[896,256]{1,0:T(8,128)(2,1)S(1)} %copy-done.6, ...), custom_call_target="tpu_custom_call" | custom-call | flops 939524096 | bytes 5505024 | tf_op jit(solution)/shard_map/serve/pallas_call | solution.py:311
  259.1 4.6 %serve.13 = (bf16[1,1024,128]{2,1,0:T(8,128)(2,1)S(1)}, bf16[1,1024,128]{2,1,0:T(8,128)(2,1)S(1)}) custom-call(s32[10]{0:T(128)S(1)} %copy-done.42, bf16[1024,1792]{1,0:T(8,128)(2,1)} %tokens_ref.15, bf16[1792,2048]{1,0:T(8,128)(2,1)} %resident_ref.15, bf16[1792,256]{1,0:T(8,128)(2,1)S(1)} %collective-permute-done.45.refs_0_.refs_1_, ...), custom_call_target="tpu_custom_call" | custom-call | flops 939524096 | bytes 5505024 | tf_op jit(solution)/shard_map/serve/pallas_call | solution.py:311
  263.8 3.2 %collective-permute-done.55.refs_9_.refs_3_ = bf16[896,256]{1,0:T(8,128)(2,1)S(1)} collective-permute-done((bf16[896,256]{1,0:T(8,128)(2,1)S(1)}, bf16[896,256]{1,0:T(8,128)(2,1)S(1)}, u32[]{:S(2)}, u32[]{:S(2)}) %collective-permute-start.55) | collective-permute-done | bytes 458784 | tf_op jit(solution)/shard_map/ppermute | solution.py:431
  269.1 6.4 %collective-permute-done.51.refs_3_ = bf16[896,256]{1,0:T(8,128)(2,1)S(1)} collective-permute-done((bf16[896,256]{1,0:T(8,128)(2,1)S(1)}, bf16[896,256]{1,0:T(8,128)(2,1)S(1)}, u32[]{:S(2)}, u32[]{:S(2)}) %collective-permute-start.51) | collective-permute-done | bytes 458784 | tf_op jit(solution)/shard_map/ppermute | solution.py:431
  276.6 2.1 collective-permute-start.57
  279.9 4.5 %serve.14 = (bf16[1,1024,128]{2,1,0:T(8,128)(2,1)S(1)}, bf16[1,1024,128]{2,1,0:T(8,128)(2,1)S(1)}) custom-call(s32[10]{0:T(128)S(1)} %copy-done.42, bf16[1024,1792]{1,0:T(8,128)(2,1)} %tokens_ref.15, bf16[1792,2048]{1,0:T(8,128)(2,1)} %resident_ref.15, bf16[896,256]{1,0:T(8,128)(2,1)S(1)} %copy-done.13, ...), custom_call_target="tpu_custom_call" | custom-call | flops 939524096 | bytes 5505024 | tf_op jit(solution)/shard_map/serve/pallas_call | solution.py:311
  285.8 3.1 %collective-permute-done.58.refs_1_ = bf16[896,256]{1,0:T(8,128)(2,1)S(1)} collective-permute-done((bf16[896,256]{1,0:T(8,128)(2,1)S(1)}, bf16[896,256]{1,0:T(8,128)(2,1)S(1)}, u32[]{:S(2)}, u32[]{:S(2)}) %collective-permute-start.58) | collective-permute-done | bytes 458784 | tf_op jit(solution)/shard_map/ppermute | solution.py:562
  288.9 7.8 %collective-permute-done.57.refs_0_ = bf16[896,256]{1,0:T(8,128)(2,1)S(1)} collective-permute-done((bf16[896,256]{1,0:T(8,128)(2,1)S(1)}, bf16[896,256]{1,0:T(8,128)(2,1)S(1)}, u32[]{:S(2)}, u32[]{:S(2)}) %collective-permute-start.57) | collective-permute-done | bytes 458784 | tf_op jit(solution)/shard_map/ppermute | solution.py:562
  296.7 4.6 %serve.15 = (bf16[1,1024,128]{2,1,0:T(8,128)(2,1)S(1)}, bf16[1,1024,128]{2,1,0:T(8,128)(2,1)S(1)}) custom-call(s32[10]{0:T(128)S(1)} %copy-done.42, bf16[1024,1792]{1,0:T(8,128)(2,1)} %tokens_ref.15, bf16[1792,2048]{1,0:T(8,128)(2,1)} %resident_ref.15, bf16[896,256]{1,0:T(8,128)(2,1)S(1)} %collective-permute-done.57.refs_0_, ...), custom_call_target="tpu_custom_call" | custom-call | flops 939524096 | bytes 5505024 | tf_op jit(solution)/shard_map/serve/pallas_call | solution.py:311
  304.2 7.2 %collective-permute-done.60 = bf16[1024,128]{1,0:T(8,128)(2,1)S(1)} collective-permute-done((bf16[1024,128]{1,0:T(8,128)(2,1)S(1)}, bf16[1024,128]{1,0:T(8,128)(2,1)S(1)}, u32[]{:S(2)}, u32[]{:S(2)}) %collective-permute-start.60) | collective-permute-done | bytes 262176 | tf_op jit(solution)/shard_map/ppermute | solution.py:427
  (214 shorter events, 58.6 us)
Async XLA Ops:
  3.9 39.9 %collective-permute-start.4 = (bf16[2,1792,256]{2,1,0:T(8,128)(2,1)}, bf16[2,1792,256]{2,1,0:T(8,128)(2,1)S(1)}, u32[]{:S(2)}, u32[]{:S(2)}) collective-permute-start(bf16[2,1792,256]{2,1,0:T(8,128)(2,1)} %slab_sum.14), channel_id=1, source_target_pairs={{0,8},{8,0},{16,24},{24,16},{1,9},{9,1},{17,25},{25,17},{2,10},{10... | collective-permute-start | bytes 5505032 | tf_op jit(solution)/shard_map/ppermute | solution.py:427
  6.3 5.8 %collective-permute-start.8 = (bf16[2,896,256]{2,1,0:T(8,128)(2,1)S(1)}, bf16[2,896,256]{2,1,0:T(8,128)(2,1)S(1)}, u32[]{:S(2)}, u32[]{:S(2)}) collective-permute-start(bf16[2,896,256]{2,1,0:T(8,128)(2,1)S(1)} %slab_sum.18), channel_id=1, source_target_pairs={{0,8},{8,0},{16,24},{24,16},{1,9},{9,1},{17,25},{25,17},{2,10},{10... | collective-permute-start | bytes 2752520 | tf_op jit(solution)/shard_map/ppermute | solution.py:427
  8.4 8.5 %collective-permute-start.6 = (bf16[2,896,256]{2,1,0:T(8,128)(2,1)S(1)}, bf16[2,896,256]{2,1,0:T(8,128)(2,1)S(1)}, u32[]{:S(2)}, u32[]{:S(2)}) collective-permute-start(bf16[2,896,256]{2,1,0:T(8,128)(2,1)S(1)} %slab_sum.16), channel_id=1, source_target_pairs={{0,8},{8,0},{16,24},{24,16},{1,9},{9,1},{17,25},{25,17},{2,10},{10... | collective-permute-start | bytes 2752520 | tf_op jit(solution)/shard_map/ppermute | solution.py:427
  12.1 43.6 %collective-permute-start.2 = (bf16[2,1792,256]{2,1,0:T(8,128)(2,1)}, bf16[2,1792,256]{2,1,0:T(8,128)(2,1)S(1)}, u32[]{:S(2)}, u32[]{:S(2)}) collective-permute-start(bf16[2,1792,256]{2,1,0:T(8,128)(2,1)} %slab_sum.12), channel_id=1, source_target_pairs={{0,8},{8,0},{16,24},{24,16},{1,9},{9,1},{17,25},{25,17},{2,10},{10... | collective-permute-start | bytes 5505032 | tf_op jit(solution)/shard_map/ppermute | solution.py:427
  13.9 14.5 %collective-permute-start.9 = (bf16[1,896,256]{2,1,0:T(8,128)(2,1)S(1)}, bf16[1,896,256]{2,1,0:T(8,128)(2,1)}, u32[]{:S(2)}, u32[]{:S(2)}) collective-permute-start(bf16[1,896,256]{2,1,0:T(8,128)(2,1)S(1)} %slab_sum.19), channel_id=1, source_target_pairs={{0,16},{8,24},{16,0},{24,8},{1,17},{9,25},{17,1},{25,9},{2,18},{10... | collective-permute-start | bytes 1376264 | tf_op jit(solution)/shard_map/ppermute | solution.py:427
  18.6 18.9 %collective-permute-start.7 = (bf16[1,896,256]{2,1,0:T(8,128)(2,1)S(1)}, bf16[1,896,256]{2,1,0:T(8,128)(2,1)}, u32[]{:S(2)}, u32[]{:S(2)}) collective-permute-start(bf16[1,896,256]{2,1,0:T(8,128)(2,1)S(1)} %slab_sum.17), channel_id=1, source_target_pairs={{0,16},{8,24},{16,0},{24,8},{1,17},{9,25},{17,1},{25,9},{2,18},{10... | collective-permute-start | bytes 1376264 | tf_op jit(solution)/shard_map/ppermute | solution.py:427
  21.9 72.2 %collective-permute-start = (bf16[2,1792,256]{2,1,0:T(8,128)(2,1)}, bf16[2,1792,256]{2,1,0:T(8,128)(2,1)S(1)}, u32[]{:S(2)}, u32[]{:S(2)}) collective-permute-start(bf16[2,1792,256]{2,1,0:T(8,128)(2,1)} %slab_sum.10), channel_id=1, source_target_pairs={{0,8},{8,0},{16,24},{24,16},{1,9},{9,1},{17,25},{25,17},{2,10},{10... | collective-permute-start | bytes 5505032 | tf_op jit(solution)/shard_map/ppermute | solution.py:427
  41.9 12.2 %collective-permute-start.15 = (bf16[896,256]{1,0:T(8,128)(2,1)}, bf16[896,256]{1,0:T(8,128)(2,1)}, u32[]{:S(2)}, u32[]{:S(2)}) collective-permute-start(bf16[896,256]{1,0:T(8,128)(2,1)} %get-tuple-element.44.refs_0_.refs_6_), channel_id=1, source_target_pairs={{0,2},{1,3},{2,0},{3,1},{4,6},{5,7},{6,4},{7,5},{8,10},{9,11},{10,... | collective-permute-start | bytes 1376264 | tf_op jit(solution)/shard_map/ppermute | solution.py:431
  45.8 23.3 %collective-permute-start.5 = (bf16[1,1792,256]{2,1,0:T(8,128)(2,1)S(1)}, bf16[1,1792,256]{2,1,0:T(8,128)(2,1)S(1)}, u32[]{:S(2)}, u32[]{:S(2)}) collective-permute-start(bf16[1,1792,256]{2,1,0:T(8,128)(2,1)S(1)} %slab_sum.15), channel_id=1, source_target_pairs={{0,16},{8,24},{16,0},{24,8},{1,17},{9,25},{17,1},{25,9},{2,18},{10... | collective-permute-start | bytes 2752520 | tf_op jit(solution)/shard_map/ppermute | solution.py:427
  47.4 12.7 %collective-permute-start.16 = (bf16[896,256]{1,0:T(8,128)(2,1)S(1)}, bf16[896,256]{1,0:T(8,128)(2,1)S(1)}, u32[]{:S(2)}, u32[]{:S(2)}) collective-permute-start(bf16[896,256]{1,0:T(8,128)(2,1)S(1)} %copy-done.16), channel_id=1, source_target_pairs={{2,4},{3,5},{4,2},{5,3},{10,12},{11,13},{12,10},{13,11},{18,20},{1... | collective-permute-start | bytes 1376264 | tf_op jit(solution)/shard_map/ppermute | solution.py:431
  54.1 11.1 %collective-permute-start.10 = (bf16[896,256]{1,0:T(8,128)(2,1)S(1)}, bf16[896,256]{1,0:T(8,128)(2,1)}, u32[]{:S(2)}, u32[]{:S(2)}) collective-permute-start(bf16[896,256]{1,0:T(8,128)(2,1)S(1)} %copy-done.14), channel_id=1, source_target_pairs={{0,2},{1,3},{2,0},{3,1},{4,6},{5,7},{6,4},{7,5},{8,10},{9,11},{10,... | collective-permute-start | bytes 1376264 | tf_op jit(solution)/shard_map/ppermute | solution.py:431
  55.7 25.7 %collective-permute-start.18 = (bf16[896,256]{1,0:T(8,128)(2,1)}, bf16[896,256]{1,0:T(8,128)(2,1)}, u32[]{:S(2)}, u32[]{:S(2)}) collective-permute-start(bf16[896,256]{1,0:T(8,128)(2,1)} %collective-permute-done.15.refs_7_), channel_id=1, source_target_pairs={{2,4},{3,5},{4,2},{5,3},{10,12},{11,13},{12,10},{13,11},{18,20},{1... | collective-permute-start | bytes 1376264 | tf_op jit(solution)/shard_map/ppermute | solution.py:431
  60.1 95.0 %copy-start.7 = (bf16[896,256]{1,0:T(8,128)(2,1)}, bf16[896,256]{1,0:T(8,128)(2,1)S(1)}, u32[]{:S(2)}) copy-start(bf16[896,256]{1,0:T(8,128)(2,1)S(1)} %collective-permute-done.16.refs_1_.refs_0_.refs_10_) | copy-start | bytes 1376260
  60.1 39.2 %collective-permute-start.3 = (bf16[1,1792,256]{2,1,0:T(8,128)(2,1)}, bf16[1,1792,256]{2,1,0:T(8,128)(2,1)}, u32[]{:S(2)}, u32[]{:S(2)}) collective-permute-start(bf16[1,1792,256]{2,1,0:T(8,128)(2,1)} %slab_sum.13), channel_id=1, source_target_pairs={{0,16},{8,24},{16,0},{24,8},{1,17},{9,25},{17,1},{25,9},{2,18},{10... | collective-permute-start | bytes 2752520 | tf_op jit(solution)/shard_map/ppermute | solution.py:427
  65.3 20.6 %collective-permute-start.11 = (bf16[896,256]{1,0:T(8,128)(2,1)S(1)}, bf16[896,256]{1,0:T(8,128)(2,1)S(1)}, u32[]{:S(2)}, u32[]{:S(2)}) collective-permute-start(bf16[896,256]{1,0:T(8,128)(2,1)S(1)} %copy-done.14), channel_id=1, source_target_pairs={{2,4},{3,5},{4,2},{5,3},{10,12},{11,13},{12,10},{13,11},{18,20},{1... | collective-permute-start | bytes 1376264 | tf_op jit(solution)/shard_map/ppermute | solution.py:431
  70.1 15.8 %collective-permute-start.13 = (bf16[896,256]{1,0:T(8,128)(2,1)}, bf16[896,256]{1,0:T(8,128)(2,1)}, u32[]{:S(2)}, u32[]{:S(2)}) collective-permute-start(bf16[896,256]{1,0:T(8,128)(2,1)} %collective-permute-done.10.refs_1_), channel_id=1, source_target_pairs={{2,4},{3,5},{4,2},{5,3},{10,12},{11,13},{12,10},{13,11},{18,20},{1... | collective-permute-start | bytes 1376264 | tf_op jit(solution)/shard_map/ppermute | solution.py:431
  83.0 10.4 %collective-permute-start.19 = (bf16[896,256]{1,0:T(8,128)(2,1)S(1)}, bf16[896,256]{1,0:T(8,128)(2,1)S(1)}, u32[]{:S(2)}, u32[]{:S(2)}) collective-permute-start(bf16[896,256]{1,0:T(8,128)(2,1)S(1)} %pick.24), channel_id=1, source_target_pairs={{0,2},{1,3},{2,0},{3,1},{4,6},{5,7},{6,4},{7,5},{8,10},{9,11},{10,... | collective-permute-start | bytes 1376264 | tf_op jit(solution)/shard_map/ppermute | solution.py:431
  86.8 15.4 %collective-permute-start.14 = (bf16[896,256]{1,0:T(8,128)(2,1)S(1)}, bf16[896,256]{1,0:T(8,128)(2,1)S(1)}, u32[]{:S(2)}, u32[]{:S(2)}) collective-permute-start(bf16[896,256]{1,0:T(8,128)(2,1)S(1)} %pick.22), channel_id=1, source_target_pairs={{0,2},{1,3},{2,0},{3,1},{4,6},{5,7},{6,4},{7,5},{8,10},{9,11},{10,... | collective-permute-start | bytes 1376264 | tf_op jit(solution)/shard_map/ppermute | solution.py:431
  92.2 11.5 %collective-permute-start.28 = (bf16[896,256]{1,0:T(8,128)(2,1)}, bf16[896,256]{1,0:T(8,128)(2,1)S(1)}, u32[]{:S(2)}, u32[]{:S(2)}) collective-permute-start(bf16[896,256]{1,0:T(8,128)(2,1)} %get-tuple-element.45.refs_2_.refs_0_.refs_6_), channel_id=1, source_target_pairs={{2,4},{3,5},{4,2},{5,3},{10,12},{11,13},{12,10},{13,11},{18,20},{1... | collective-permute-start | bytes 1376264 | tf_op jit(solution)/shard_map/ppermute | solution.py:431
  93.4 95.2 %copy-start.3 = (bf16[896,256]{1,0:T(8,128)(2,1)}, bf16[896,256]{1,0:T(8,128)(2,1)S(1)}, u32[]{:S(2)}) copy-start(bf16[896,256]{1,0:T(8,128)(2,1)S(1)} %collective-permute-done.19.refs_9_.refs_7_) | copy-start | bytes 1376260
  93.4 17.9 %collective-permute-start.30 = (bf16[896,256]{1,0:T(8,128)(2,1)S(1)}, bf16[896,256]{1,0:T(8,128)(2,1)S(1)}, u32[]{:S(2)}, u32[]{:S(2)}) collective-permute-start(bf16[896,256]{1,0:T(8,128)(2,1)S(1)} %collective-permute-done.19.refs_9_.refs_7_), channel_id=1, source_target_pairs={{2,4},{3,5},{4,2},{5,3},{10,12},{11,13},{12,10},{13,11},{18,20},{1... | collective-permute-start | bytes 1376264 | tf_op jit(solution)/shard_map/ppermute | solution.py:431
  97.1 43.0 %collective-permute-start.1 = (bf16[1,1792,256]{2,1,0:T(8,128)(2,1)}, bf16[1,1792,256]{2,1,0:T(8,128)(2,1)}, u32[]{:S(2)}, u32[]{:S(2)}) collective-permute-start(bf16[1,1792,256]{2,1,0:T(8,128)(2,1)} %slab_sum.11), channel_id=1, source_target_pairs={{0,16},{8,24},{16,0},{24,8},{1,17},{9,25},{17,1},{25,9},{2,18},{10... | collective-permute-start | bytes 2752520 | tf_op jit(solution)/shard_map/ppermute | solution.py:427
  99.3 28.6 %collective-permute-start.24 = (bf16[896,256]{1,0:T(8,128)(2,1)S(1)}, bf16[896,256]{1,0:T(8,128)(2,1)S(1)}, u32[]{:S(2)}, u32[]{:S(2)}) collective-permute-start(bf16[896,256]{1,0:T(8,128)(2,1)S(1)} %copy-done.5), channel_id=1, source_target_pairs={{2,4},{3,5},{4,2},{5,3},{10,12},{11,13},{12,10},{13,11},{18,20},{1... | collective-permute-start | bytes 1376264 | tf_op jit(solution)/shard_map/ppermute | solution.py:431
  102.2 25.8 %collective-permute-start.26 = (bf16[896,256]{1,0:T(8,128)(2,1)S(1)}, bf16[896,256]{1,0:T(8,128)(2,1)S(1)}, u32[]{:S(2)}, u32[]{:S(2)}) collective-permute-start(bf16[896,256]{1,0:T(8,128)(2,1)S(1)} %collective-permute-done.14.refs_3_.refs_1_), channel_id=1, source_target_pairs={{2,4},{3,5},{4,2},{5,3},{10,12},{11,13},{12,10},{13,11},{18,20},{1... | collective-permute-start | bytes 1376264 | tf_op jit(solution)/shard_map/ppermute | solution.py:431
  103.7 84.8 %copy-start.8 = (bf16[896,256]{1,0:T(8,128)(2,1)}, bf16[896,256]{1,0:T(8,128)(2,1)S(1)}, u32[]{:S(2)}) copy-start(bf16[896,256]{1,0:T(8,128)(2,1)S(1)} %collective-permute-done.28.refs_1_.refs_0_.refs_10_) | copy-start | bytes 1376260
  103.7 32.5 %collective-permute-start.17 = (bf16[896,256]{1,0:T(8,128)(2,1)S(1)}, bf16[896,256]{1,0:T(8,128)(2,1)S(1)}, u32[]{:S(2)}, u32[]{:S(2)}) collective-permute-start(bf16[896,256]{1,0:T(8,128)(2,1)S(1)} %pick.23), channel_id=1, source_target_pairs={{0,2},{1,3},{2,0},{3,1},{4,6},{5,7},{6,4},{7,5},{8,10},{9,11},{10,... | collective-permute-start | bytes 1376264 | tf_op jit(solution)/shard_map/ppermute | solution.py:431
  111.3 26.5 %collective-permute-start.12 = (bf16[896,256]{1,0:T(8,128)(2,1)}, bf16[896,256]{1,0:T(8,128)(2,1)S(1)}, u32[]{:S(2)}, u32[]{:S(2)}) collective-permute-start(bf16[896,256]{1,0:T(8,128)(2,1)} %pick.21), channel_id=1, source_target_pairs={{0,2},{1,3},{2,0},{3,1},{4,6},{5,7},{6,4},{7,5},{8,10},{9,11},{10,... | collective-permute-start | bytes 1376264 | tf_op jit(solution)/shard_map/ppermute | solution.py:431
  127.9 16.7 %collective-permute-start.31 = (bf16[896,256]{1,0:T(8,128)(2,1)S(1)}, bf16[896,256]{1,0:T(8,128)(2,1)S(1)}, u32[]{:S(2)}, u32[]{:S(2)}) collective-permute-start(bf16[896,256]{1,0:T(8,128)(2,1)S(1)} %pick.29), channel_id=1, source_target_pairs={{0,2},{1,3},{2,0},{3,1},{4,6},{5,7},{6,4},{7,5},{8,10},{9,11},{10,... | collective-permute-start | bytes 1376264 | tf_op jit(solution)/shard_map/ppermute | solution.py:431
  129.7 18.6 %collective-permute-start.27 = (bf16[896,256]{1,0:T(8,128)(2,1)S(1)}, bf16[896,256]{1,0:T(8,128)(2,1)S(1)}, u32[]{:S(2)}, u32[]{:S(2)}) collective-permute-start(bf16[896,256]{1,0:T(8,128)(2,1)S(1)} %pick.27), channel_id=1, source_target_pairs={{0,2},{1,3},{2,0},{3,1},{4,6},{5,7},{6,4},{7,5},{8,10},{9,11},{10,... | collective-permute-start | bytes 1376264 | tf_op jit(solution)/shard_map/ppermute | solution.py:431
  137.1 13.6 %collective-permute-start.40 = (bf16[896,256]{1,0:T(8,128)(2,1)}, bf16[896,256]{1,0:T(8,128)(2,1)S(1)}, u32[]{:S(2)}, u32[]{:S(2)}) collective-permute-start(bf16[896,256]{1,0:T(8,128)(2,1)} %get-tuple-element.51.refs_2_.refs_0_.refs_6_), channel_id=1, source_target_pairs={{2,4},{3,5},{4,2},{5,3},{10,12},{11,13},{12,10},{13,11},{18,20},{1... | collective-permute-start | bytes 1376264 | tf_op jit(solution)/shard_map/ppermute | solution.py:431
  137.8 21.4 %collective-permute-start.36 = (bf16[896,256]{1,0:T(8,128)(2,1)S(1)}, bf16[896,256]{1,0:T(8,128)(2,1)S(1)}, u32[]{:S(2)}, u32[]{:S(2)}) collective-permute-start(bf16[896,256]{1,0:T(8,128)(2,1)S(1)} %copy-done.6), channel_id=1, source_target_pairs={{2,4},{3,5},{4,2},{5,3},{10,12},{11,13},{12,10},{13,11},{18,20},{1... | collective-permute-start | bytes 1376264 | tf_op jit(solution)/shard_map/ppermute | solution.py:431
  140.0 23.1 %collective-permute-start.29 = (bf16[896,256]{1,0:T(8,128)(2,1)S(1)}, bf16[896,256]{1,0:T(8,128)(2,1)S(1)}, u32[]{:S(2)}, u32[]{:S(2)}) collective-permute-start(bf16[896,256]{1,0:T(8,128)(2,1)S(1)} %pick.28), channel_id=1, source_target_pairs={{0,2},{1,3},{2,0},{3,1},{4,6},{5,7},{6,4},{7,5},{8,10},{9,11},{10,... | collective-permute-start | bytes 1376264 | tf_op jit(solution)/shard_map/ppermute | solution.py:431
  144.6 23.4 %collective-permute-start.42 = (bf16[896,256]{1,0:T(8,128)(2,1)S(1)}, bf16[896,256]{1,0:T(8,128)(2,1)S(1)}, u32[]{:S(2)}, u32[]{:S(2)}) collective-permute-start(bf16[896,256]{1,0:T(8,128)(2,1)S(1)} %collective-permute-done.31.refs_9_.refs_7_), channel_id=1, source_target_pairs={{2,4},{3,5},{4,2},{5,3},{10,12},{11,13},{12,10},{13,11},{18,20},{1... | collective-permute-start | bytes 1376264 | tf_op jit(solution)/shard_map/ppermute | solution.py:431
  148.3 34.1 %collective-permute-start.38 = (bf16[896,256]{1,0:T(8,128)(2,1)S(1)}, bf16[896,256]{1,0:T(8,128)(2,1)S(1)}, u32[]{:S(2)}, u32[]{:S(2)}) collective-permute-start(bf16[896,256]{1,0:T(8,128)(2,1)S(1)} %collective-permute-done.27.refs_3_.refs_1_), channel_id=1, source_target_pairs={{2,4},{3,5},{4,2},{5,3},{10,12},{11,13},{12,10},{13,11},{18,20},{1... | collective-permute-start | bytes 1376264 | tf_op jit(solution)/shard_map/ppermute | solution.py:431
  150.6 32.8 %collective-permute-start.25 = (bf16[896,256]{1,0:T(8,128)(2,1)}, bf16[896,256]{1,0:T(8,128)(2,1)}, u32[]{:S(2)}, u32[]{:S(2)}) collective-permute-start(bf16[896,256]{1,0:T(8,128)(2,1)} %pick.26), channel_id=1, source_target_pairs={{0,2},{1,3},{2,0},{3,1},{4,6},{5,7},{6,4},{7,5},{8,10},{9,11},{10,... | collective-permute-start | bytes 1376264 | tf_op jit(solution)/shard_map/ppermute | solution.py:431
  159.2 54.8 %collective-permute-start.21 = (bf16[1792,256]{1,0:T(8,128)(2,1)}, bf16[1792,256]{1,0:T(8,128)(2,1)}, u32[]{:S(2)}, u32[]{:S(2)}) collective-permute-start(bf16[1792,256]{1,0:T(8,128)(2,1)} %pick.25), channel_id=1, source_target_pairs={{0,1},{1,0},{2,3},{3,2},{4,5},{5,4},{6,7},{7,6},{8,9},{9,8},{10,11... | collective-permute-start | bytes 2752520 | tf_op jit(solution)/shard_map/ppermute | solution.py:562
  163.1 22.3 %collective-permute-start.41 = (bf16[896,256]{1,0:T(8,128)(2,1)}, bf16[896,256]{1,0:T(8,128)(2,1)S(1)}, u32[]{:S(2)}, u32[]{:S(2)}) collective-permute-start(bf16[896,256]{1,0:T(8,128)(2,1)} %pick.33), channel_id=1, source_target_pairs={{0,2},{1,3},{2,0},{3,1},{4,6},{5,7},{6,4},{7,5},{8,10},{9,11},{10,... | collective-permute-start | bytes 1376264 | tf_op jit(solution)/shard_map/ppermute | solution.py:431
  168.0 19.9 %collective-permute-start.37 = (bf16[896,256]{1,0:T(8,128)(2,1)}, bf16[896,256]{1,0:T(8,128)(2,1)}, u32[]{:S(2)}, u32[]{:S(2)}) collective-permute-start(bf16[896,256]{1,0:T(8,128)(2,1)} %pick.31), channel_id=1, source_target_pairs={{0,2},{1,3},{2,0},{3,1},{4,6},{5,7},{6,4},{7,5},{8,10},{9,11},{10,... | collective-permute-start | bytes 1376264 | tf_op jit(solution)/shard_map/ppermute | solution.py:431
  182.4 15.1 %collective-permute-start.43 = (bf16[896,256]{1,0:T(8,128)(2,1)S(1)}, bf16[896,256]{1,0:T(8,128)(2,1)S(1)}, u32[]{:S(2)}, u32[]{:S(2)}) collective-permute-start(bf16[896,256]{1,0:T(8,128)(2,1)S(1)} %pick.34), channel_id=1, source_target_pairs={{0,2},{1,3},{2,0},{3,1},{4,6},{5,7},{6,4},{7,5},{8,10},{9,11},{10,... | collective-permute-start | bytes 1376264 | tf_op jit(solution)/shard_map/ppermute | solution.py:431
  183.4 21.9 %collective-permute-start.39 = (bf16[896,256]{1,0:T(8,128)(2,1)S(1)}, bf16[896,256]{1,0:T(8,128)(2,1)S(1)}, u32[]{:S(2)}, u32[]{:S(2)}) collective-permute-start(bf16[896,256]{1,0:T(8,128)(2,1)S(1)} %pick.32), channel_id=1, source_target_pairs={{0,2},{1,3},{2,0},{3,1},{4,6},{5,7},{6,4},{7,5},{8,10},{9,11},{10,... | collective-permute-start | bytes 1376264 | tf_op jit(solution)/shard_map/ppermute | solution.py:431
  186.3 32.7 %collective-permute-start.52 = (bf16[896,256]{1,0:T(8,128)(2,1)}, bf16[896,256]{1,0:T(8,128)(2,1)S(1)}, u32[]{:S(2)}, u32[]{:S(2)}) collective-permute-start(bf16[896,256]{1,0:T(8,128)(2,1)} %get-tuple-element.57.refs_2_.refs_0_.refs_6_), channel_id=1, source_target_pairs={{2,4},{3,5},{4,2},{5,3},{10,12},{11,13},{12,10},{13,11},{18,20},{1... | collective-permute-start | bytes 1376264 | tf_op jit(solution)/shard_map/ppermute | solution.py:431
  187.8 31.7 %collective-permute-start.48 = (bf16[896,256]{1,0:T(8,128)(2,1)S(1)}, bf16[896,256]{1,0:T(8,128)(2,1)S(1)}, u32[]{:S(2)}, u32[]{:S(2)}) collective-permute-start(bf16[896,256]{1,0:T(8,128)(2,1)S(1)} %copy-done.13), channel_id=1, source_target_pairs={{2,4},{3,5},{4,2},{5,3},{10,12},{11,13},{12,10},{13,11},{18,20},{1... | collective-permute-start | bytes 1376264 | tf_op jit(solution)/shard_map/ppermute | solution.py:431
  197.6 49.1 %collective-permute-start.33 = (bf16[1792,256]{1,0:T(8,128)(2,1)}, bf16[1792,256]{1,0:T(8,128)(2,1)S(1)}, u32[]{:S(2)}, u32[]{:S(2)}) collective-permute-start(bf16[1792,256]{1,0:T(8,128)(2,1)} %pick.30), channel_id=1, source_target_pairs={{0,1},{1,0},{2,3},{3,2},{4,5},{5,4},{6,7},{7,6},{8,9},{9,8},{10,11... | collective-permute-start | bytes 2752520 | tf_op jit(solution)/shard_map/ppermute | solution.py:562
  208.1 45.3 %collective-permute-start.45 = (bf16[1792,256]{1,0:T(8,128)(2,1)}, bf16[1792,256]{1,0:T(8,128)(2,1)S(1)}, u32[]{:S(2)}, u32[]{:S(2)}) collective-permute-start(bf16[1792,256]{1,0:T(8,128)(2,1)} %pick.35), channel_id=1, source_target_pairs={{0,1},{1,0},{2,3},{3,2},{4,5},{5,4},{6,7},{7,6},{8,9},{9,8},{10,11... | collective-permute-start | bytes 2752520 | tf_op jit(solution)/shard_map/ppermute | solution.py:562
  214.0 6.3 %collective-permute-start.20 = (bf16[1,1024,128]{2,1,0:T(8,128)(2,1)S(1)}, bf16[1,1024,128]{2,1,0:T(8,128)(2,1)S(1)}, u32[]{:S(2)}, u32[]{:S(2)}) collective-permute-start(bf16[1,1024,128]{2,1,0:T(8,128)(2,1)S(1)} %get-tuple-element.47), channel_id=1, source_target_pairs={{0,8},{8,0},{16,24},{24,16},{1,9},{9,1},{17,25},{25,17},{2,10},{10... | collective-permute-start | bytes 786440 | tf_op jit(solution)/shard_map/ppermute | solution.py:427
  219.0 3.5 %collective-permute-start.22 = (bf16[1,1024,128]{2,1,0:T(8,128)(2,1)S(1)}, bf16[1,1024,128]{2,1,0:T(8,128)(2,1)S(1)}, u32[]{:S(2)}, u32[]{:S(2)}) collective-permute-start(bf16[1,1024,128]{2,1,0:T(8,128)(2,1)S(1)} %get-tuple-element.49), channel_id=1, source_target_pairs={{0,8},{8,0},{16,24},{24,16},{1,9},{9,1},{17,25},{25,17},{2,10},{10... | collective-permute-start | bytes 786440 | tf_op jit(solution)/shard_map/ppermute | solution.py:427
  219.6 11.1 %collective-permute-start.54 = (bf16[896,256]{1,0:T(8,128)(2,1)S(1)}, bf16[896,256]{1,0:T(8,128)(2,1)S(1)}, u32[]{:S(2)}, u32[]{:S(2)}) collective-permute-start(bf16[896,256]{1,0:T(8,128)(2,1)S(1)} %collective-permute-done.43.refs_9_.refs_7_.refs_1_), channel_id=1, source_target_pairs={{2,4},{3,5},{4,2},{5,3},{10,12},{11,13},{12,10},{13,11},{18,20},{1... | collective-permute-start | bytes 1376264 | tf_op jit(solution)/shard_map/ppermute | solution.py:431
  220.3 17.5 %collective-permute-start.50 = (bf16[896,256]{1,0:T(8,128)(2,1)S(1)}, bf16[896,256]{1,0:T(8,128)(2,1)S(1)}, u32[]{:S(2)}, u32[]{:S(2)}) collective-permute-start(bf16[896,256]{1,0:T(8,128)(2,1)S(1)} %collective-permute-done.39.refs_3_.refs_1_), channel_id=1, source_target_pairs={{2,4},{3,5},{4,2},{5,3},{10,12},{11,13},{12,10},{13,11},{18,20},{1... | collective-permute-start | bytes 1376264 | tf_op jit(solution)/shard_map/ppermute | solution.py:431
  222.5 24.0 %collective-permute-start.53 = (bf16[896,256]{1,0:T(8,128)(2,1)S(1)}, bf16[896,256]{1,0:T(8,128)(2,1)S(1)}, u32[]{:S(2)}, u32[]{:S(2)}) collective-permute-start(bf16[896,256]{1,0:T(8,128)(2,1)S(1)} %pick.38), channel_id=1, source_target_pairs={{0,2},{1,3},{2,0},{3,1},{4,6},{5,7},{6,4},{7,5},{8,10},{9,11},{10,... | collective-permute-start | bytes 1376264 | tf_op jit(solution)/shard_map/ppermute | solution.py:431
  230.7 22.6 %collective-permute-start.23 = (bf16[1024,128]{1,0:T(8,128)(2,1)S(1)}, bf16[1024,128]{1,0:T(8,128)(2,1)S(1)}, u32[]{:S(2)}, u32[]{:S(2)}) collective-permute-start(bf16[1024,128]{1,0:T(8,128)(2,1)S(1)} %fusion.1), channel_id=1, source_target_pairs={{0,16},{8,24},{16,0},{24,8},{1,17},{9,25},{17,1},{25,9},{2,18},{10... | collective-permute-start | bytes 786440 | tf_op jit(solution)/shard_map/ppermute | solution.py:427
  237.8 30.8 %collective-permute-start.49 = (bf16[896,256]{1,0:T(8,128)(2,1)S(1)}, bf16[896,256]{1,0:T(8,128)(2,1)S(1)}, u32[]{:S(2)}, u32[]{:S(2)}) collective-permute-start(bf16[896,256]{1,0:T(8,128)(2,1)S(1)} %pick.36), channel_id=1, source_target_pairs={{0,2},{1,3},{2,0},{3,1},{4,6},{5,7},{6,4},{7,5},{8,10},{9,11},{10,... | collective-permute-start | bytes 1376264 | tf_op jit(solution)/shard_map/ppermute | solution.py:431
  246.6 20.3 %collective-permute-start.55 = (bf16[896,256]{1,0:T(8,128)(2,1)S(1)}, bf16[896,256]{1,0:T(8,128)(2,1)S(1)}, u32[]{:S(2)}, u32[]{:S(2)}) collective-permute-start(bf16[896,256]{1,0:T(8,128)(2,1)S(1)} %pick.39), channel_id=1, source_target_pairs={{0,2},{1,3},{2,0},{3,1},{4,6},{5,7},{6,4},{7,5},{8,10},{9,11},{10,... | collective-permute-start | bytes 1376264 | tf_op jit(solution)/shard_map/ppermute | solution.py:431
  246.7 28.9 %collective-permute-start.51 = (bf16[896,256]{1,0:T(8,128)(2,1)S(1)}, bf16[896,256]{1,0:T(8,128)(2,1)S(1)}, u32[]{:S(2)}, u32[]{:S(2)}) collective-permute-start(bf16[896,256]{1,0:T(8,128)(2,1)S(1)} %pick.37), channel_id=1, source_target_pairs={{0,2},{1,3},{2,0},{3,1},{4,6},{5,7},{6,4},{7,5},{8,10},{9,11},{10,... | collective-permute-start | bytes 1376264 | tf_op jit(solution)/shard_map/ppermute | solution.py:431
  253.3 23.3 %collective-permute-start.32 = (bf16[1,1024,128]{2,1,0:T(8,128)(2,1)S(1)}, bf16[1,1024,128]{2,1,0:T(8,128)(2,1)S(1)}, u32[]{:S(2)}, u32[]{:S(2)}) collective-permute-start(bf16[1,1024,128]{2,1,0:T(8,128)(2,1)S(1)} %get-tuple-element.53), channel_id=1, source_target_pairs={{0,8},{8,0},{16,24},{24,16},{1,9},{9,1},{17,25},{25,17},{2,10},{10... | collective-permute-start | bytes 786440 | tf_op jit(solution)/shard_map/ppermute | solution.py:427
  253.4 25.3 %collective-permute-start.34 = (bf16[1,1024,128]{2,1,0:T(8,128)(2,1)S(1)}, bf16[1,1024,128]{2,1,0:T(8,128)(2,1)S(1)}, u32[]{:S(2)}, u32[]{:S(2)}) collective-permute-start(bf16[1,1024,128]{2,1,0:T(8,128)(2,1)S(1)} %get-tuple-element.55), channel_id=1, source_target_pairs={{0,8},{8,0},{16,24},{24,16},{1,9},{9,1},{17,25},{25,17},{2,10},{10... | collective-permute-start | bytes 786440 | tf_op jit(solution)/shard_map/ppermute | solution.py:427
  266.9 17.4 %collective-permute-start.44 = (bf16[1,1024,128]{2,1,0:T(8,128)(2,1)S(1)}, bf16[1,1024,128]{2,1,0:T(8,128)(2,1)S(1)}, u32[]{:S(2)}, u32[]{:S(2)}) collective-permute-start(bf16[1,1024,128]{2,1,0:T(8,128)(2,1)S(1)} %get-tuple-element.59), channel_id=1, source_target_pairs={{0,8},{8,0},{16,24},{24,16},{1,9},{9,1},{17,25},{25,17},{2,10},{10... | collective-permute-start | bytes 786440 | tf_op jit(solution)/shard_map/ppermute | solution.py:427
  268.5 15.9 %collective-permute-start.46 = (bf16[1,1024,128]{2,1,0:T(8,128)(2,1)S(1)}, bf16[1,1024,128]{2,1,0:T(8,128)(2,1)S(1)}, u32[]{:S(2)}, u32[]{:S(2)}) collective-permute-start(bf16[1,1024,128]{2,1,0:T(8,128)(2,1)S(1)} %get-tuple-element.61), channel_id=1, source_target_pairs={{0,8},{8,0},{16,24},{24,16},{1,9},{9,1},{17,25},{25,17},{2,10},{10... | collective-permute-start | bytes 786440 | tf_op jit(solution)/shard_map/ppermute | solution.py:427
  275.5 13.4 %collective-permute-start.58 = (bf16[896,256]{1,0:T(8,128)(2,1)S(1)}, bf16[896,256]{1,0:T(8,128)(2,1)S(1)}, u32[]{:S(2)}, u32[]{:S(2)}) collective-permute-start(bf16[896,256]{1,0:T(8,128)(2,1)S(1)} %pick.41), channel_id=1, source_target_pairs={{0,1},{1,0},{2,3},{3,2},{4,5},{5,4},{6,7},{7,6},{8,9},{9,8},{10,11... | collective-permute-start | bytes 1376264 | tf_op jit(solution)/shard_map/ppermute | solution.py:562
  276.6 20.0 %collective-permute-start.57 = (bf16[896,256]{1,0:T(8,128)(2,1)S(1)}, bf16[896,256]{1,0:T(8,128)(2,1)S(1)}, u32[]{:S(2)}, u32[]{:S(2)}) collective-permute-start(bf16[896,256]{1,0:T(8,128)(2,1)S(1)} %pick.40), channel_id=1, source_target_pairs={{0,1},{1,0},{2,3},{3,2},{4,5},{5,4},{6,7},{7,6},{8,9},{9,8},{10,11... | collective-permute-start | bytes 1376264 | tf_op jit(solution)/shard_map/ppermute | solution.py:562
  278.9 22.5 %collective-permute-start.35 = (bf16[1024,128]{1,0:T(8,128)(2,1)S(1)}, bf16[1024,128]{1,0:T(8,128)(2,1)S(1)}, u32[]{:S(2)}, u32[]{:S(2)}) collective-permute-start(bf16[1024,128]{1,0:T(8,128)(2,1)S(1)} %fusion.2), channel_id=1, source_target_pairs={{0,16},{8,24},{16,0},{24,8},{1,17},{9,25},{17,1},{25,9},{2,18},{10... | collective-permute-start | bytes 786440 | tf_op jit(solution)/shard_map/ppermute | solution.py:427
  284.4 17.2 %collective-permute-start.56 = (bf16[1,1024,128]{2,1,0:T(8,128)(2,1)S(1)}, bf16[1,1024,128]{2,1,0:T(8,128)(2,1)S(1)}, u32[]{:S(2)}, u32[]{:S(2)}) collective-permute-start(bf16[1,1024,128]{2,1,0:T(8,128)(2,1)S(1)} %get-tuple-element.63), channel_id=1, source_target_pairs={{0,8},{8,0},{16,24},{24,16},{1,9},{9,1},{17,25},{25,17},{2,10},{10... | collective-permute-start | bytes 786440 | tf_op jit(solution)/shard_map/ppermute | solution.py:427
  284.6 19.4 %collective-permute-start.47 = (bf16[1024,128]{1,0:T(8,128)(2,1)S(1)}, bf16[1024,128]{1,0:T(8,128)(2,1)S(1)}, u32[]{:S(2)}, u32[]{:S(2)}) collective-permute-start(bf16[1024,128]{1,0:T(8,128)(2,1)S(1)} %fusion.3), channel_id=1, source_target_pairs={{0,16},{8,24},{16,0},{24,8},{1,17},{9,25},{17,1},{25,9},{2,18},{10... | collective-permute-start | bytes 786440 | tf_op jit(solution)/shard_map/ppermute | solution.py:427
  301.3 1.6 collective-permute-start.59
  303.0 8.4 %collective-permute-start.60 = (bf16[1024,128]{1,0:T(8,128)(2,1)S(1)}, bf16[1024,128]{1,0:T(8,128)(2,1)S(1)}, u32[]{:S(2)}, u32[]{:S(2)}) collective-permute-start(bf16[1024,128]{1,0:T(8,128)(2,1)S(1)} %fusion.4), channel_id=1, source_target_pairs={{0,16},{8,24},{16,0},{24,8},{1,17},{9,25},{17,1},{25,9},{2,18},{10... | collective-permute-start | bytes 786440 | tf_op jit(solution)/shard_map/ppermute | solution.py:427
  (45 other events, 595.5 us)

commit v2 on v1

--- a/solution.py
+++ b/solution.py
@@ -172,9 +172,10 @@
 
 
 def pick(table, code_of, parts):
-    part_rows, cols = parts[0][0].shape
-    n_parts, n_options = len(parts), len(parts[0])
-    shape = (n_parts * part_rows, cols)
+    cols = parts[0][1][0][0].shape[1]
+    n_options = len(parts[0][1])
+    starts = [sum(rows for rows, _ in parts[:p]) for p in range(len(parts) + 1)]
+    shape = (starts[-1], cols)
 
     def kernel(tab, *refs):
         out, sems = refs[-2:]
@@ -185,41 +186,43 @@
             def _():
                 copies = [
                     pltpu.make_async_copy(
-                        refs[h * n_options + k], out.at[pl.ds(h * part_rows, part_rows)], sems.at[h]
+                        refs[p * n_options + k].at[pl.ds(options[k][1], rows)],
+                        out.at[pl.ds(starts[p], rows)],
+                        sems.at[p],
                     )
-                    for h in range(n_parts)
+                    for p, (rows, options) in enumerate(parts)
                 ]
                 for copy in copies:
                     copy.start()
                 for copy in copies:
                     copy.wait()
 
+    operands = [array for _, options in parts for array, _ in options]
     return pl.pallas_call(
         kernel,
         grid_spec=pltpu.PrefetchScalarGridSpec(
             num_scalar_prefetch=1,
             grid=(1,),
-            in_specs=[pl.BlockSpec(memory_space=pl.ANY)] * (n_parts * n_options),
+            in_specs=[pl.BlockSpec(memory_space=pl.ANY)] * len(operands),
             out_specs=pl.BlockSpec(shape, lambda i, tab: (0, 0)),
-            scratch_shapes=[pltpu.SemaphoreType.DMA((n_parts,))],
-        ),
-        out_shape=jax.ShapeDtypeStruct(shape, parts[0][0].dtype),
+            scratch_shapes=[pltpu.SemaphoreType.DMA((len(parts),))],
+        ),
+        out_shape=jax.ShapeDtypeStruct(shape, jnp.bfloat16),
         compiler_params=params(PICK_VMEM),
         cost_estimate=pl.CostEstimate(
             flops=0, bytes_accessed=4 * shape[0] * shape[1], transcendentals=0
         ),
         name="pick",
-    )(table, *[option for options in parts for option in options])
-
-
-def serve(tokens, resident, pieces, table, part_rows, stride, shift, width):
+    )(table, *operands)
+
+
+def serve(tokens, resident, pieces, table, stride, shift, width):
     rows_total, depth = tokens.shape
     n_pieces = len(pieces)
-    n_parts = len(pieces[0][0])
-    part_cols = pieces[0][0][0][0][0].shape[1]
+    n_parts = max(len(parts) for parts, _, _ in pieces)
+    part_cols = pieces[0][0][0][2][0][0].shape[1]
     n_cols = part_cols // width
     tile = TILE if rows_total % TILE == 0 else rows_total
-    counts = [len(parts[0]) for parts, _, _ in pieces]
 
     def kernel(tab, tokens_ref, resident_ref, *refs):
         outs = refs[-7 - n_cols : -7]
@@ -236,54 +239,56 @@
 
         fetch_tokens = pltpu.make_async_copy(tokens_ref, tok, tok_sem)
 
-        def fetch(s, h, ref):
-            return pltpu.make_async_copy(ref, delta.at[s, h], sems.at[s, h])
+        def fetch(s, p, ref=None):
+            first, rows, _ = pieces[s][0][p]
+            target = delta.at[s, pl.ds(first, rows)]
+            return pltpu.make_async_copy(target if ref is None else ref, target, sems.at[s, p])
 
         for s, (parts, code_of, _) in enumerate(pieces):
             code = code_of(tab)
-            for k in range(counts[s]):
+            n_options = len(parts[0][2])
+            for k in range(n_options):
                 chosen = [
-                    refs[at_ref + h * counts[s] + k].at[pl.ds(parts[h][k][1], part_rows)]
-                    for h in range(n_parts)
+                    refs[at_ref + p * n_options + k].at[pl.ds(options[k][1], rows)]
+                    for p, (_, rows, options) in enumerate(parts)
                 ]
 
                 @pl.when(code == k)
                 def _():
-                    for h in range(n_parts):
-                        fetch(s, h, chosen[h]).start()
-
-            at_ref += n_parts * counts[s]
+                    for p, ref in enumerate(chosen):
+                        fetch(s, p, ref).start()
+
+            at_ref += len(parts) * n_options
             for k in range(n_cols):
                 fetch_resident(s, k).start()
         fetch_tokens.start()
-        for s, (_, _, places) in enumerate(pieces):
+        for s, (parts, _, places) in enumerate(pieces):
             starts = [
                 pl.multiple_of(lax.rem(tab[places[k]], n_cols) * width, width)
                 for k in range(n_cols)
             ]
             for k in range(n_cols):
                 fetch_resident(s, k).wait()
-            for h in range(n_parts):
-                fetch(s, h, delta.at[s, h]).wait()
-
-                @pl.loop(0, part_rows // QB, unroll=UNROLL)
-                def _(b):
-                    at = pl.multiple_of(h * part_rows + b * QB, QB)
-                    near = pl.multiple_of(b * QB, QB)
-                    for k in range(n_cols):
-                        for c in range(width // QB):
-                            span = slice(c * QB, (c + 1) * QB)
-                            change = delta[s, h, pl.ds(near, QB), pl.ds(starts[k] + c * QB, QB)]
-                            value = held[s, k, pl.ds(at, QB), span].astype(
-                                jnp.float32
-                            ) + change.astype(jnp.float32)
-                            largest = jnp.max(jnp.abs(value), axis=(0, 1), keepdims=True)
-                            scale = (largest + scale_epsilon) / quant_range
-                            level = jnp.floor(value * (1.0 / (scale * grid_step)) + 0.5)
-                            column = (s * n_cols + k) * width + c * QB
-                            weight[pl.ds(at, QB), column : column + QB] = (
-                                level * (scale * grid_step)
-                            ).astype(jnp.bfloat16)
+            for p in range(len(parts)):
+                fetch(s, p).wait()
+
+            @pl.loop(0, depth // QB, unroll=UNROLL)
+            def _(b):
+                at = pl.multiple_of(b * QB, QB)
+                for k in range(n_cols):
+                    for c in range(width // QB):
+                        span = slice(c * QB, (c + 1) * QB)
+                        change = delta[s, pl.ds(at, QB), pl.ds(starts[k] + c * QB, QB)]
+                        value = held[s, k, pl.ds(at, QB), span].astype(
+                            jnp.float32
+                        ) + change.astype(jnp.float32)
+                        largest = jnp.max(jnp.abs(value), axis=(0, 1), keepdims=True)
+                        scale = (largest + scale_epsilon) / quant_range
+                        level = jnp.floor(value * (1.0 / (scale * grid_step)) + 0.5)
+                        column = (s * n_cols + k) * width + c * QB
+                        weight[pl.ds(at, QB), column : column + QB] = (
+                            level * (scale * grid_step)
+                        ).astype(jnp.bfloat16)
 
         fetch_tokens.wait()
 
@@ -303,7 +308,7 @@
     in_specs = [pl.BlockSpec(memory_space=pl.ANY)] * 2
     operands = [tokens, resident]
     for parts, _, _ in pieces:
-        for options in parts:
+        for _, _, options in parts:
             in_specs += [pl.BlockSpec(memory_space=pl.ANY)] * len(options)
             operands += [array for array, _ in options]
     out_spec = pl.BlockSpec((n_pieces, rows_total, width), lambda i, tab: (0, 0, 0))
@@ -319,7 +324,7 @@
                 pltpu.VMEM((rows_total, depth), jnp.bfloat16),
                 pltpu.VMEM((n_pieces, n_cols, depth, width), jnp.bfloat16),
                 pltpu.VMEM((depth, n_pieces * n_cols * width), jnp.bfloat16),
-                pltpu.VMEM((n_pieces, n_parts, part_rows, part_cols), jnp.bfloat16),
+                pltpu.VMEM((n_pieces, depth, part_cols), jnp.bfloat16),
                 pltpu.SemaphoreType.DMA((n_pieces, n_parts)),
                 pltpu.SemaphoreType.DMA((n_pieces, n_cols)),
                 pltpu.SemaphoreType.DMA,
@@ -489,6 +494,9 @@
                 )
                 delta[h][c] = changes[0]
 
+    def entire(arrays, first=0):
+        return [(array, first) for array in arrays]
+
     last = EXPERTS - 1
 
     def at(index):
@@ -506,10 +514,10 @@
                         moves = [(last - a, last - b) for a, b in moves]
                     value = along(value, moves)
                     options.append(value)
-            found.append(options)
+            found.append([(part_rows, entire(options))])
         return found
 
-    def slotted_line(pieces):
+    def slotted_line(pieces, h):
         sides = [(0, 1), (1, 0), (2, 3), (3, 2)]
         middle = [(1, 2), (2, 1)]
         count = len(pieces)
@@ -524,63 +532,88 @@
         def last_code(tab):
             return tab[flag_at + 1]
 
-        for t in range(2 * count + 1):
+        near_rows = (part_rows // QB + 1) // 2 * QB if h == parts - 1 else part_rows
+        cuts = [(0, near_rows), (near_rows, part_rows - near_rows)]
+        cuts = [cut for cut in cuts if cut[1]]
+        for t in range(2 * count):
             c = t // 2
             if t == 0:
                 value = pieces[0]
             else:
                 if t % 2:
-                    value = pick(table, odd_code, [[pieces[c], center[2 * c]]])
-                elif c < count:
+                    choices = [pieces[c], center[2 * c]]
+                    value = pick(table, odd_code, [(part_rows, entire(choices))])
+                else:
                     choices = [center[t - 2], center[t - 1], pieces[c]]
-                    value = pick(table, even_code, [choices])
-                else:
-                    value = pick(table, last_code, [[center[t - 2], center[t - 1]]])
+                    value = pick(table, even_code, [(part_rows, entire(choices))])
             side.append(along(value, sides))
-            if t < 2 * count:
-                center.append(along(side[t - 1] if t % 2 else pieces[c], middle))
-        return [
-            [pieces[c], *side[2 * c : 2 * c + 3], *center[2 * c : 2 * c + 2]] for c in range(count)
-        ]
+            center.append(along(side[t - 1] if t % 2 else pieces[c], middle))
+        ends = []
+        for first, n_rows in cuts:
+            value = pick(table, last_code, [(n_rows, entire(center[-2:], first))])
+            ends.append(along(value, sides))
+        found = []
+        for c in range(count):
+            rest = center[2 * c : 2 * c + 2]
+            if c < count - 1:
+                arrays = [pieces[c], *side[2 * c : 2 * c + 3], *rest]
+                found.append([(part_rows, entire(arrays))])
+            else:
+                found.append(
+                    [
+                        (
+                            n_rows,
+                            entire([pieces[c], *side[2 * c : 2 * c + 2]], first)
+                            + [(end, 0)]
+                            + entire(rest, first),
+                        )
+                        for (first, n_rows), end in zip(cuts, ends)
+                    ]
+                )
+        return found
 
     if two_slots:
-        options = [slotted_line(delta[h]) for h in range(parts)]
+        options = [slotted_line(delta[h], h) for h in range(parts)]
     else:
         options = [full_line(delta[h]) for h in range(parts)]
 
-    moved = [[[None] * parts for _ in range(n_chunks)] for _ in range(group)]
+    chunk_parts = [[part for h in range(parts) for part in options[h][c]] for c in range(n_chunks)]
+    moved = [[[] for _ in range(n_chunks)] for _ in range(group)]
     for c in range(n_chunks):
-        groups = [[h] for h in range(parts)] if c == n_chunks - 1 else [list(range(parts))]
+        split = c == n_chunks - 1
+        groups = [[part] for part in chunk_parts[c]] if split else [chunk_parts[c]]
         for held in groups:
             for s in range(1, group):
-                value = pick(table, at(code_at + s), [options[h][c] for h in held])
+                value = pick(table, at(code_at + s), held)
                 pairs = [
                     (e * group + j, e * group + (j + s) % group)
                     for e in range(EXPERTS)
                     for j in range(group)
                 ]
                 value = lax.ppermute(value, "expert", pairs)
-                for h in held:
-                    moved[s][c][h] = (value, (h - held[0]) * part_rows)
+                moved[s][c].append((value.shape[0], [(value, 0)]))
+
+    def placed(parts_of):
+        first, found = 0, []
+        for n_rows, choices in parts_of:
+            found.append((first, n_rows, choices))
+            first += n_rows
+        return found
 
     def piece_of(c, s):
+        places = [place_at + s * n_cols + k for k in range(n_cols)]
         if s == 0:
-            sources = [[(array, 0) for array in options[h][c]] for h in range(parts)]
-            code_of = at(code_at)
-        else:
-            sources, code_of = [[moved[s][c][h]] for h in range(parts)], lambda tab: 0
-        return sources, code_of, [place_at + s * n_cols + k for k in range(n_cols)]
+            return placed(chunk_parts[c]), at(code_at), places
+        return placed(moved[s][c]), lambda tab: 0, places
 
     sums = []
     parity = (me % 2).astype(jnp.int32)
     for c in range(n_chunks):
         pieces = [piece_of(c, s) for s in range(group)]
-        groups = [[piece] for piece in pieces]
+        groups = [pieces] if c == n_chunks - 1 else [[piece] for piece in pieces]
         results = []
         for chosen in groups:
-            results.append(
-                serve(token_tiles, resident_weights, chosen, table, part_rows, n_chunks, c, width)
-            )
+            results.append(serve(token_tiles, resident_weights, chosen, table, n_chunks, c, width))
         if n_dp == 4 and group == 2:
             kept = []
             for straight_sums, crossed_sums in results:

time: 314 us -> 307 us (0.978)
  waiting for transfers between devices: 72.4 us -> 51.2 us
  starting transfers between devices: 100 us -> 119 us
  Pallas kernels: 128 us -> 122 us
    ppermute x34 -> x35, starting transfers between devices: 78.1 us -> 97.5 us  [along(): return lax.ppermute(value, 'expert', pairs)]
    ppermute x34 -> x35, waiting for transfers between devices: 38.3 us -> 22.9 us  [along(): return lax.ppermute(value, 'expert', pairs)]
    ppermute x5 -> x6, waiting for transfers between devices: 10.9 us -> 5.25 us  [body(): value = lax.ppermute(value, 'expert', pairs)]
    pallas_call x21 -> x23, Pallas kernels: 31.2 us -> 27.8 us  [pick(): pl.pallas_call(kernel, grid_spec=pltpu.PrefetchScalarGridSpec(num_scalar_...]
    pallas_call x8 -> x7, Pallas kernels: 36.5 us -> 33.1 us  [serve(): pl.pallas_call(kernel, grid_spec=pltpu.PrefetchScalarGridSpec(num_scalar_...]
    ppermute x22 -> x21, starting transfers between devices: 15.7 us -> 13.7 us  [flip(): return lax.ppermute(value, 'dp', pairs)]
    ppermute x5 -> x6, starting transfers between devices: 6.42 us -> 7.99 us  [body(): value = lax.ppermute(value, 'expert', pairs)]
    ppermute x22 -> x21, waiting for transfers between devices: 23.2 us -> 23.1 us  [flip(): return lax.ppermute(value, 'dp', pairs)]
  transfers between devices with their start and end apart: 61 -> 62, of which waited for: 17 -> 16; matrix products, arithmetic and copies ran while one was open for 1% -> 1% of each run, Pallas kernels for 40% -> 39%
where the time goes in v2:
time: 307 us; the launch traced here: 306 us
  Pallas kernels  122 us (40%)
  starting transfers between devices  119 us (39%)
  waiting for transfers between devices  51.2 us (17%)
  local copies, waits for them, and re-layouts  7.98 us (3%)
    ppermute x35, starting transfers between devices, along(): return lax.ppermute(value, 'expert', pairs)  97.5 us
    pallas_call x8, Pallas kernels, adam_parts(): pl.pallas_call(kernel, grid_spec=pltpu.PrefetchScalarGridSpec(num_scalar_...  34.2 us
    pallas_call x7, Pallas kernels, serve(): pl.pallas_call(kernel, grid_spec=pltpu.PrefetchScalarGridSpec(num_scalar_...  33.1 us
    pallas_call x23, Pallas kernels, pick(): pl.pallas_call(kernel, grid_spec=pltpu.PrefetchScalarGridSpec(num_scalar_...  27.8 us
    pallas_call x10, Pallas kernels, slab_sum(): pl.pallas_call(kernel, grid_spec=pltpu.PrefetchScalarGridSpec(num_scalar_...  25.6 us
    ppermute x21, waiting for transfers between devices, flip(): return lax.ppermute(value, 'dp', pairs)  23.1 us
    ppermute x35, waiting for transfers between devices, along(): return lax.ppermute(value, 'expert', pairs)  22.9 us
    ppermute x21, starting transfers between devices, flip(): return lax.ppermute(value, 'dp', pairs)  13.7 us
  transfers between devices with their start and end apart: 62, of which 16 were waited for; matrix products, arithmetic and copies ran while one was open for 1% of the time, Pallas kernels for 39%

profile of v2, /device:TPU:0, one launch (start us, length us, event | category | flops | bytes accessed | tf_op | source)
XLA Modules:
  0.0 306.0 jit_solution(2149088655693779777)
XLA Ops:
  0.7 3.1 %slab_sum.14 = bf16[2,1792,256]{2,1,0:T(8,128)(2,1)} custom-call(s32[2]{0:T(128)S(1)} %pad_add_fusion.tab.spot, bf16[7168,1024]{1,0:T(8,128)(2,1)} %bitcast.22, bf16[7168,1024]{1,0:T(8,128)(2,1)} %bitcast.23), custom_call_target="tpu_custom_call" | custom-call | flops 1835008 | bytes 3670016 | tf_op jit(solution)/shard_map/slab_sum/pallas_call | solution.py:80
  4.3 2.0 slab_sum.18
  6.4 3.1 %slab_sum.12 = bf16[2,1792,256]{2,1,0:T(8,128)(2,1)} custom-call(s32[2]{0:T(128)S(1)} %pad_add_fusion.tab.spot, bf16[7168,1024]{1,0:T(8,128)(2,1)} %bitcast.26, bf16[7168,1024]{1,0:T(8,128)(2,1)} %bitcast.27), custom_call_target="tpu_custom_call" | custom-call | flops 1835008 | bytes 3670016 | tf_op jit(solution)/shard_map/slab_sum/pallas_call | solution.py:80
  10.0 2.0 slab_sum.16
  12.1 1.7 slab_sum.19
  13.8 3.0 collective-permute-start.9
  16.9 3.2 %slab_sum.10 = bf16[2,1792,256]{2,1,0:T(8,128)(2,1)} custom-call(s32[2]{0:T(128)S(1)} %pad_add_fusion.tab.spot, bf16[7168,1024]{1,0:T(8,128)(2,1)} %bitcast.32, bf16[7168,1024]{1,0:T(8,128)(2,1)} %bitcast.33), custom_call_target="tpu_custom_call" | custom-call | flops 1835008 | bytes 3670016 | tf_op jit(solution)/shard_map/slab_sum/pallas_call | solution.py:80
  20.1 1.7 slab_sum.17
  21.9 6.4 %collective-permute-done.9.refs_1_ = bf16[1,896,256]{2,1,0:T(8,128)(2,1)} collective-permute-done((bf16[1,896,256]{2,1,0:T(8,128)(2,1)S(1)}, bf16[1,896,256]{2,1,0:T(8,128)(2,1)}, u32[]{:S(2)}, u32[]{:S(2)}) %collective-permute-start.9) | collective-permute-done | bytes 458784 | tf_op jit(solution)/shard_map/ppermute | solution.py:432
  28.3 4.2 %adam_parts.8 = (f32[1792,1024]{1,0:T(8,128)}, bf16[896,256]{1,0:T(8,128)(2,1)}) custom-call(s32[2]{0:T(128)} %copy-done.40, bf16[7168,1024]{1,0:T(8,128)(2,1)} %bitcast.36, bf16[2,896,256]{2,1,0:T(8,128)(2,1)} %copy-done.31, bf16[1,896,256]{2,1,0:T(8,128)(2,1)} %collective-permute-done.9.refs_1_, f32[1792,1024]{1,0:T(8,128)} %refs_2_.15, ...), custom_call_target="tpu_custom_call" | custom-call | flops 6881280 | bytes 5505024 | tf_op jit(solution)/shard_map/adam_parts/pallas_call | solution.py:149
  32.6 2.1 collective-permute-start.10
  34.7 3.0 slab_sum.15
  39.1 4.3 %adam_parts.9 = (f32[1792,1024]{1,0:T(8,128)}, bf16[896,256]{1,0:T(8,128)(2,1)}) custom-call(s32[2]{0:T(128)} %copy-done.40, bf16[7168,1024]{1,0:T(8,128)(2,1)} %bitcast.39, bf16[2,896,256]{2,1,0:T(8,128)(2,1)} %copy-done.30, bf16[1,896,256]{2,1,0:T(8,128)(2,1)} %collective-permute-done.7.refs_1_, ...), custom_call_target="tpu_custom_call", output_to_operand_aliasing={{0}: (7, {})} | custom-call | flops 6881280 | bytes 5505024 | tf_op jit(solution)/shard_map/adam_parts/pallas_call | solution.py:149
  46.3 2.9 slab_sum.13
  49.1 4.9 %collective-permute-done.15.refs_7_ = bf16[896,256]{1,0:T(8,128)(2,1)} collective-permute-done((bf16[896,256]{1,0:T(8,128)(2,1)}, bf16[896,256]{1,0:T(8,128)(2,1)}, u32[]{:S(2)}, u32[]{:S(2)}) %collective-permute-start.15) | collective-permute-done | bytes 458784 | tf_op jit(solution)/shard_map/ppermute | solution.py:436
  54.8 1.5 collective-permute-start.3
  56.3 4.7 %collective-permute-done.5.refs_1_ = bf16[1,1792,256]{2,1,0:T(8,128)(2,1)} collective-permute-done((bf16[1,1792,256]{2,1,0:T(8,128)(2,1)}, bf16[1,1792,256]{2,1,0:T(8,128)(2,1)}, u32[]{:S(2)}, u32[]{:S(2)}) %collective-permute-start.5) | collective-permute-done | bytes 917536 | tf_op jit(solution)/shard_map/ppermute | solution.py:432
  63.7 4.2 %adam_parts.10 = (f32[1792,1024]{1,0:T(8,128)}, bf16[896,256]{1,0:T(8,128)(2,1)}) custom-call(s32[2]{0:T(128)} %copy-done.40, bf16[7168,1024]{1,0:T(8,128)(2,1)} %bitcast.42, bf16[2,1792,256]{2,1,0:T(8,128)(2,1)} %copy-done.6, bf16[1,1792,256]{2,1,0:T(8,128)(2,1)} %collective-permute-done.5.refs_1_, ...), custom_call_target="tpu_custom_call", output_to_operand_aliasing={{0}: (7, {})} | custom-call | flops 6881280 | bytes 5505024 | tf_op jit(solution)/shard_map/adam_parts/pallas_call | solution.py:149
  69.8 3.5 %collective-permute-start.14 = (bf16[896,256]{1,0:T(8,128)(2,1)S(1)}, bf16[896,256]{1,0:T(8,128)(2,1)S(1)}, u32[]{:S(2)}, u32[]{:S(2)}) collective-permute-start(bf16[896,256]{1,0:T(8,128)(2,1)S(1)} %pick.24), channel_id=1, source_target_pairs={{0,2},{1,3},{2,0},{3,1},{4,6},{5,7},{6,4},{7,5},{8,10},{9,11},{10,... | collective-permute-start | bytes 1376264 | tf_op jit(solution)/shard_map/ppermute | solution.py:436
  73.3 4.4 %adam_parts.11 = (f32[1792,1024]{1,0:T(8,128)}, bf16[896,256]{1,0:T(8,128)(2,1)}) custom-call(s32[2]{0:T(128)} %copy-done.40, bf16[7168,1024]{1,0:T(8,128)(2,1)} %bitcast.43, bf16[2,1792,256]{2,1,0:T(8,128)(2,1)} %copy-done.6, bf16[1,1792,256]{2,1,0:T(8,128)(2,1)} %collective-permute-done.5.refs_1_, ...), custom_call_target="tpu_custom_call", output_to_operand_aliasing={{0}: (7, {})} | custom-call | flops 6881280 | bytes 5505024 | tf_op jit(solution)/shard_map/adam_parts/pallas_call | solution.py:149
  79.8 10.1 %collective-permute-start.19 = (bf16[896,256]{1,0:T(8,128)(2,1)S(1)}, bf16[896,256]{1,0:T(8,128)(2,1)S(1)}, u32[]{:S(2)}, u32[]{:S(2)}) collective-permute-start(bf16[896,256]{1,0:T(8,128)(2,1)S(1)} %pick.26), channel_id=1, source_target_pairs={{0,2},{1,3},{2,0},{3,1},{4,6},{5,7},{6,4},{7,5},{8,10},{9,11},{10,... | collective-permute-start | bytes 1376264 | tf_op jit(solution)/shard_map/ppermute | solution.py:436
  89.9 3.0 slab_sum.11
  96.4 1.6 collective-permute-done.19.refs_9_.refs_7_
  98.7 4.2 %adam_parts.12 = (f32[1792,1024]{1,0:T(8,128)}, bf16[896,256]{1,0:T(8,128)(2,1)}) custom-call(s32[2]{0:T(128)} %copy-done.40, bf16[7168,1024]{1,0:T(8,128)(2,1)} %bitcast.46, bf16[2,1792,256]{2,1,0:T(8,128)(2,1)} %copy-done.5, bf16[1,1792,256]{2,1,0:T(8,128)(2,1)} %collective-permute-done.3.refs_1_, ...), custom_call_target="tpu_custom_call", output_to_operand_aliasing={{0}: (7, {})} | custom-call | flops 6881280 | bytes 5505024 | tf_op jit(solution)/shard_map/adam_parts/pallas_call | solution.py:149
  105.0 16.7 %collective-permute-start.27 = (bf16[896,256]{1,0:T(8,128)(2,1)S(1)}, bf16[896,256]{1,0:T(8,128)(2,1)S(1)}, u32[]{:S(2)}, u32[]{:S(2)}) collective-permute-start(bf16[896,256]{1,0:T(8,128)(2,1)S(1)} %pick.29), channel_id=1, source_target_pairs={{0,2},{1,3},{2,0},{3,1},{4,6},{5,7},{6,4},{7,5},{8,10},{9,11},{10,... | collective-permute-start | bytes 1376264 | tf_op jit(solution)/shard_map/ppermute | solution.py:436
  121.7 2.3 pick.25
  124.2 1.6 pick.23
  125.8 3.7 %collective-permute-start.12 = (bf16[896,256]{1,0:T(8,128)(2,1)}, bf16[896,256]{1,0:T(8,128)(2,1)}, u32[]{:S(2)}, u32[]{:S(2)}) collective-permute-start(bf16[896,256]{1,0:T(8,128)(2,1)} %pick.23), channel_id=1, source_target_pairs={{0,2},{1,3},{2,0},{3,1},{4,6},{5,7},{6,4},{7,5},{8,10},{9,11},{10,... | collective-permute-start | bytes 1376264 | tf_op jit(solution)/shard_map/ppermute | solution.py:436
  130.2 4.3 %adam_parts.13 = (f32[1792,1024]{1,0:T(8,128)}, bf16[896,256]{1,0:T(8,128)(2,1)}) custom-call(s32[2]{0:T(128)} %copy-done.40, bf16[7168,1024]{1,0:T(8,128)(2,1)} %bitcast.47, bf16[2,1792,256]{2,1,0:T(8,128)(2,1)} %copy-done.5, bf16[1,1792,256]{2,1,0:T(8,128)(2,1)} %collective-permute-done.3.refs_1_, ...), custom_call_target="tpu_custom_call", output_to_operand_aliasing={{0}: (7, {})} | custom-call | flops 6881280 | bytes 5505024 | tf_op jit(solution)/shard_map/adam_parts/pallas_call | solution.py:149
  135.5 1.7 pick.31
  137.1 9.2 %collective-permute-start.31 = (bf16[896,256]{1,0:T(8,128)(2,1)}, bf16[896,256]{1,0:T(8,128)(2,1)S(1)}, u32[]{:S(2)}, u32[]{:S(2)}) collective-permute-start(bf16[896,256]{1,0:T(8,128)(2,1)} %pick.31), channel_id=1, source_target_pairs={{0,2},{1,3},{2,0},{3,1},{4,6},{5,7},{6,4},{7,5},{8,10},{9,11},{10,... | collective-permute-start | bytes 1376264 | tf_op jit(solution)/shard_map/ppermute | solution.py:436
  147.8 4.2 %adam_parts.14 = (f32[1792,1024]{1,0:T(8,128)}, bf16[896,256]{1,0:T(8,128)(2,1)}) custom-call(s32[2]{0:T(128)} %copy-done.40, bf16[7168,1024]{1,0:T(8,128)(2,1)} %bitcast.48, bf16[2,1792,256]{2,1,0:T(8,128)(2,1)} %copy-done.4, bf16[1,1792,256]{2,1,0:T(8,128)(2,1)} %collective-permute-done.1.refs_1_, ...), custom_call_target="tpu_custom_call", output_to_operand_aliasing={{0}: (7, {})} | custom-call | flops 6881280 | bytes 5505024 | tf_op jit(solution)/shard_map/adam_parts/pallas_call | solution.py:149
  152.0 4.4 %adam_parts.15 = (f32[1792,1024]{1,0:T(8,128)}, bf16[896,256]{1,0:T(8,128)(2,1)}) custom-call(s32[2]{0:T(128)} %copy-done.40, bf16[7168,1024]{1,0:T(8,128)(2,1)} %bitcast.49, bf16[2,1792,256]{2,1,0:T(8,128)(2,1)} %copy-done.4, bf16[1,1792,256]{2,1,0:T(8,128)(2,1)} %collective-permute-done.1.refs_1_, ...), custom_call_target="tpu_custom_call", output_to_operand_aliasing={{0}: (7, {})} | custom-call | flops 6881280 | bytes 5505024 | tf_op jit(solution)/shard_map/adam_parts/pallas_call | solution.py:149
  158.8 5.3 %collective-permute-start.29 = (bf16[896,256]{1,0:T(8,128)(2,1)S(1)}, bf16[896,256]{1,0:T(8,128)(2,1)S(1)}, u32[]{:S(2)}, u32[]{:S(2)}) collective-permute-start(bf16[896,256]{1,0:T(8,128)(2,1)S(1)} %pick.30), channel_id=1, source_target_pairs={{0,2},{1,3},{2,0},{3,1},{4,6},{5,7},{6,4},{7,5},{8,10},{9,11},{10,... | collective-permute-start | bytes 1376264 | tf_op jit(solution)/shard_map/ppermute | solution.py:436
  165.7 3.1 collective-permute-start.25
  169.6 3.0 collective-permute-start.39
  175.5 10.7 %collective-permute-start.41 = (bf16[896,256]{1,0:T(8,128)(2,1)S(1)}, bf16[896,256]{1,0:T(8,128)(2,1)S(1)}, u32[]{:S(2)}, u32[]{:S(2)}) collective-permute-start(bf16[896,256]{1,0:T(8,128)(2,1)S(1)} %pick.35), channel_id=1, source_target_pairs={{0,2},{1,3},{2,0},{3,1},{4,6},{5,7},{6,4},{7,5},{8,10},{9,11},{10,... | collective-permute-start | bytes 1376264 | tf_op jit(solution)/shard_map/ppermute | solution.py:436
  186.2 1.9 pick.27
  190.4 4.3 %collective-permute-start.43 = (bf16[896,256]{1,0:T(8,128)(2,1)S(1)}, bf16[896,256]{1,0:T(8,128)(2,1)S(1)}, u32[]{:S(2)}, u32[]{:S(2)}) collective-permute-start(bf16[896,256]{1,0:T(8,128)(2,1)S(1)} %pick.36), channel_id=1, source_target_pairs={{0,2},{1,3},{2,0},{3,1},{4,6},{5,7},{6,4},{7,5},{8,10},{9,11},{10,... | collective-permute-start | bytes 1376264 | tf_op jit(solution)/shard_map/ppermute | solution.py:436
  196.7 2.3 pick.32
  199.0 1.6 collective-permute-start.33
  200.6 4.4 %collective-permute-done.41.refs_8_ = bf16[896,256]{1,0:T(8,128)(2,1)S(1)} collective-permute-done((bf16[896,256]{1,0:T(8,128)(2,1)S(1)}, bf16[896,256]{1,0:T(8,128)(2,1)S(1)}, u32[]{:S(2)}, u32[]{:S(2)}) %collective-permute-start.41) | collective-permute-done | bytes 458784 | tf_op jit(solution)/shard_map/ppermute | solution.py:436
  205.0 2.0 collective-permute-start.37
  207.0 7.8 %collective-permute-done.43.refs_9_.refs_1_.refs_7_.refs_13_ = bf16[896,256]{1,0:T(8,128)(2,1)S(1)} collective-permute-done((bf16[896,256]{1,0:T(8,128)(2,1)S(1)}, bf16[896,256]{1,0:T(8,128)(2,1)S(1)}, u32[]{:S(2)}, u32[]{:S(2)}) %collective-permute-start.43) | collective-permute-done | bytes 458784 | tf_op jit(solution)/shard_map/ppermute | solution.py:436
  215.5 1.6 pick.38
  217.1 5.0 %collective-permute-start.49 = (bf16[896,256]{1,0:T(8,128)(2,1)}, bf16[896,256]{1,0:T(8,128)(2,1)}, u32[]{:S(2)}, u32[]{:S(2)}) collective-permute-start(bf16[896,256]{1,0:T(8,128)(2,1)} %pick.38), channel_id=1, source_target_pairs={{0,2},{1,3},{2,0},{3,1},{4,6},{5,7},{6,4},{7,5},{8,10},{9,11},{10,... | collective-permute-start | bytes 1376264 | tf_op jit(solution)/shard_map/ppermute | solution.py:436
  222.2 1.6 pick.39
  224.7 2.0 collective-permute-start.51
  227.3 1.6 pick.40
  229.9 4.4 %serve.7 = (bf16[1,1024,128]{2,1,0:T(8,128)(2,1)S(1)}, bf16[1,1024,128]{2,1,0:T(8,128)(2,1)S(1)}) custom-call(s32[10]{0:T(128)S(1)} %copy-done.39, bf16[1024,1792]{1,0:T(8,128)(2,1)} %tokens_ref.13, bf16[1792,2048]{1,0:T(8,128)(2,1)} %resident_ref.13, bf16[896,256]{1,0:T(8,128)(2,1)S(1)} %copy-done.24, bf16[896,256]{1,0:T(8,128)(2,1)} %collective-permute-done.10.refs_1_, ...), custom_call_target="tpu_custom_call" | custom-call | flops 939524096 | bytes 5505024 | tf_op jit(solution)/shard_map/serve/pallas_call | solution.py:316
  234.3 2.1 pick.37
  236.4 1.7 collective-permute-start.45
  239.3 4.3 %serve.8 = (bf16[1,1024,128]{2,1,0:T(8,128)(2,1)S(1)}, bf16[1,1024,128]{2,1,0:T(8,128)(2,1)S(1)}) custom-call(s32[10]{0:T(128)S(1)} %copy-done.39, bf16[1024,1792]{1,0:T(8,128)(2,1)} %tokens_ref.13, bf16[1792,2048]{1,0:T(8,128)(2,1)} %resident_ref.13, bf16[1792,256]{1,0:T(8,128)(2,1)S(1)} %copy-done.38), custom_call_target="tpu_custom_call" | custom-call | flops 939524096 | bytes 5505024 | tf_op jit(solution)/shard_map/serve/pallas_call | solution.py:316
  245.0 2.5 collective-permute-start.56
  248.7 4.5 %serve.9 = (bf16[1,1024,128]{2,1,0:T(8,128)(2,1)S(1)}, bf16[1,1024,128]{2,1,0:T(8,128)(2,1)S(1)}) custom-call(s32[10]{0:T(128)S(1)} %copy-done.39, bf16[1024,1792]{1,0:T(8,128)(2,1)} %tokens_ref.13, bf16[1792,2048]{1,0:T(8,128)(2,1)} %resident_ref.13, bf16[896,256]{1,0:T(8,128)(2,1)S(1)} %copy-done.11, ...), custom_call_target="tpu_custom_call" | custom-call | flops 939524096 | bytes 5505024 | tf_op jit(solution)/shard_map/serve/pallas_call | solution.py:316
  253.2 4.3 %serve.10 = (bf16[1,1024,128]{2,1,0:T(8,128)(2,1)S(1)}, bf16[1,1024,128]{2,1,0:T(8,128)(2,1)S(1)}) custom-call(s32[10]{0:T(128)S(1)} %copy-done.39, bf16[1024,1792]{1,0:T(8,128)(2,1)} %tokens_ref.13, bf16[1792,2048]{1,0:T(8,128)(2,1)} %resident_ref.13, bf16[1792,256]{1,0:T(8,128)(2,1)} %collective-permute-done.33.refs_0_), custom_call_target="tpu_custom_call" | custom-call | flops 939524096 | bytes 5505024 | tf_op jit(solution)/shard_map/serve/pallas_call | solution.py:316
  260.9 4.5 %serve.11 = (bf16[1,1024,128]{2,1,0:T(8,128)(2,1)S(1)}, bf16[1,1024,128]{2,1,0:T(8,128)(2,1)S(1)}) custom-call(s32[10]{0:T(128)S(1)} %copy-done.39, bf16[1024,1792]{1,0:T(8,128)(2,1)} %tokens_ref.13, bf16[1792,2048]{1,0:T(8,128)(2,1)} %resident_ref.13, bf16[896,256]{1,0:T(8,128)(2,1)S(1)} %copy-done.15, ...), custom_call_target="tpu_custom_call" | custom-call | flops 939524096 | bytes 5505024 | tf_op jit(solution)/shard_map/serve/pallas_call | solution.py:316
  266.3 1.6 collective-permute-done.55.refs_3_.refs_9_
  271.4 4.3 %serve.12 = (bf16[1,1024,128]{2,1,0:T(8,128)(2,1)S(1)}, bf16[1,1024,128]{2,1,0:T(8,128)(2,1)S(1)}) custom-call(s32[10]{0:T(128)S(1)} %copy-done.39, bf16[1024,1792]{1,0:T(8,128)(2,1)} %tokens_ref.13, bf16[1792,2048]{1,0:T(8,128)(2,1)} %resident_ref.13, bf16[1792,256]{1,0:T(8,128)(2,1)S(1)} %collective-permute-done.45.refs_0_), custom_call_target="tpu_custom_call" | custom-call | flops 939524096 | bytes 5505024 | tf_op jit(solution)/shard_map/serve/pallas_call | solution.py:316
  275.7 1.6 collective-permute-done.59.refs_20_
  278.4 3.6 %collective-permute-done.58.refs_19_ = bf16[512,256]{1,0:T(8,128)(2,1)S(1)} collective-permute-done((bf16[512,256]{1,0:T(8,128)(2,1)S(1)}, bf16[512,256]{1,0:T(8,128)(2,1)S(1)}, u32[]{:S(2)}, u32[]{:S(2)}) %collective-permute-start.58) | collective-permute-done | bytes 262176 | tf_op jit(solution)/shard_map/ppermute | solution.py:593
  282.8 6.9 %serve.13 = (bf16[2,1024,128]{2,1,0:T(8,128)(2,1)}, bf16[2,1024,128]{2,1,0:T(8,128)(2,1)}) custom-call(s32[10]{0:T(128)S(1)} %copy-done.39, bf16[1024,1792]{1,0:T(8,128)(2,1)} %tokens_ref.13, bf16[1792,2048]{1,0:T(8,128)(2,1)} %resident_ref.13, bf16[896,256]{1,0:T(8,128)(2,1)S(1)} %copy-done.21, ...), custom_call_target="tpu_custom_call" | custom-call | flops 1879048192 | bytes 7340032 | tf_op jit(solution)/shard_map/serve/pallas_call | solution.py:316
  293.1 6.7 %collective-permute-done.47 = bf16[1024,128]{1,0:T(8,128)(2,1)S(1)} collective-permute-done((bf16[1024,128]{1,0:T(8,128)(2,1)S(1)}, bf16[1024,128]{1,0:T(8,128)(2,1)S(1)}, u32[]{:S(2)}, u32[]{:S(2)}) %collective-permute-start.47) | collective-permute-done | bytes 262176 | tf_op jit(solution)/shard_map/ppermute | solution.py:432
  300.0 4.5 %collective-permute-done.61 = bf16[1024,128]{1,0:T(8,128)(2,1)S(1)} collective-permute-done((bf16[1024,128]{1,0:T(8,128)(2,1)S(1)}, bf16[1024,128]{1,0:T(8,128)(2,1)S(1)}, u32[]{:S(2)}, u32[]{:S(2)}) %collective-permute-start.61) | collective-permute-done | bytes 262176 | tf_op jit(solution)/shard_map/ppermute | solution.py:432
  (217 shorter events, 54.2 us)
Async XLA Ops:
  3.9 30.8 %collective-permute-start.4 = (bf16[2,1792,256]{2,1,0:T(8,128)(2,1)}, bf16[2,1792,256]{2,1,0:T(8,128)(2,1)S(1)}, u32[]{:S(2)}, u32[]{:S(2)}) collective-permute-start(bf16[2,1792,256]{2,1,0:T(8,128)(2,1)} %slab_sum.14), channel_id=1, source_target_pairs={{0,8},{8,0},{16,24},{24,16},{1,9},{9,1},{17,25},{25,17},{2,10},{10... | collective-permute-start | bytes 5505032 | tf_op jit(solution)/shard_map/ppermute | solution.py:432
  6.3 5.8 %collective-permute-start.8 = (bf16[2,896,256]{2,1,0:T(8,128)(2,1)S(1)}, bf16[2,896,256]{2,1,0:T(8,128)(2,1)S(1)}, u32[]{:S(2)}, u32[]{:S(2)}) collective-permute-start(bf16[2,896,256]{2,1,0:T(8,128)(2,1)S(1)} %slab_sum.18), channel_id=1, source_target_pairs={{0,8},{8,0},{16,24},{24,16},{1,9},{9,1},{17,25},{25,17},{2,10},{10... | collective-permute-start | bytes 2752520 | tf_op jit(solution)/shard_map/ppermute | solution.py:432
  9.5 35.3 %collective-permute-start.2 = (bf16[2,1792,256]{2,1,0:T(8,128)(2,1)}, bf16[2,1792,256]{2,1,0:T(8,128)(2,1)S(1)}, u32[]{:S(2)}, u32[]{:S(2)}) collective-permute-start(bf16[2,1792,256]{2,1,0:T(8,128)(2,1)} %slab_sum.12), channel_id=1, source_target_pairs={{0,8},{8,0},{16,24},{24,16},{1,9},{9,1},{17,25},{25,17},{2,10},{10... | collective-permute-start | bytes 5505032 | tf_op jit(solution)/shard_map/ppermute | solution.py:432
  12.0 8.0 %collective-permute-start.6 = (bf16[2,896,256]{2,1,0:T(8,128)(2,1)S(1)}, bf16[2,896,256]{2,1,0:T(8,128)(2,1)S(1)}, u32[]{:S(2)}, u32[]{:S(2)}) collective-permute-start(bf16[2,896,256]{2,1,0:T(8,128)(2,1)S(1)} %slab_sum.16), channel_id=1, source_target_pairs={{0,8},{8,0},{16,24},{24,16},{1,9},{9,1},{17,25},{25,17},{2,10},{10... | collective-permute-start | bytes 2752520 | tf_op jit(solution)/shard_map/ppermute | solution.py:432
  13.8 14.5 %collective-permute-start.9 = (bf16[1,896,256]{2,1,0:T(8,128)(2,1)S(1)}, bf16[1,896,256]{2,1,0:T(8,128)(2,1)}, u32[]{:S(2)}, u32[]{:S(2)}) collective-permute-start(bf16[1,896,256]{2,1,0:T(8,128)(2,1)S(1)} %slab_sum.19), channel_id=1, source_target_pairs={{0,16},{8,24},{16,0},{24,8},{1,17},{9,25},{17,1},{25,9},{2,18},{10... | collective-permute-start | bytes 1376264 | tf_op jit(solution)/shard_map/ppermute | solution.py:432
  20.0 69.8 %collective-permute-start = (bf16[2,1792,256]{2,1,0:T(8,128)(2,1)}, bf16[2,1792,256]{2,1,0:T(8,128)(2,1)S(1)}, u32[]{:S(2)}, u32[]{:S(2)}) collective-permute-start(bf16[2,1792,256]{2,1,0:T(8,128)(2,1)} %slab_sum.10), channel_id=1, source_target_pairs={{0,8},{8,0},{16,24},{24,16},{1,9},{9,1},{17,25},{25,17},{2,10},{10... | collective-permute-start | bytes 5505032 | tf_op jit(solution)/shard_map/ppermute | solution.py:432
  21.8 17.3 %collective-permute-start.7 = (bf16[1,896,256]{2,1,0:T(8,128)(2,1)S(1)}, bf16[1,896,256]{2,1,0:T(8,128)(2,1)}, u32[]{:S(2)}, u32[]{:S(2)}) collective-permute-start(bf16[1,896,256]{2,1,0:T(8,128)(2,1)S(1)} %slab_sum.17), channel_id=1, source_target_pairs={{0,16},{8,24},{16,0},{24,8},{1,17},{9,25},{17,1},{25,9},{2,18},{10... | collective-permute-start | bytes 1376264 | tf_op jit(solution)/shard_map/ppermute | solution.py:432
  32.6 11.5 %collective-permute-start.10 = (bf16[896,256]{1,0:T(8,128)(2,1)}, bf16[896,256]{1,0:T(8,128)(2,1)}, u32[]{:S(2)}, u32[]{:S(2)}) collective-permute-start(bf16[896,256]{1,0:T(8,128)(2,1)} %get-tuple-element.40.refs_0_), channel_id=1, source_target_pairs={{0,2},{1,3},{2,0},{3,1},{4,6},{5,7},{6,4},{7,5},{8,10},{9,11},{10,... | collective-permute-start | bytes 1376264 | tf_op jit(solution)/shard_map/ppermute | solution.py:436
  37.6 23.4 %collective-permute-start.5 = (bf16[1,1792,256]{2,1,0:T(8,128)(2,1)}, bf16[1,1792,256]{2,1,0:T(8,128)(2,1)}, u32[]{:S(2)}, u32[]{:S(2)}) collective-permute-start(bf16[1,1792,256]{2,1,0:T(8,128)(2,1)} %slab_sum.15), channel_id=1, source_target_pairs={{0,16},{8,24},{16,0},{24,8},{1,17},{9,25},{17,1},{25,9},{2,18},{10... | collective-permute-start | bytes 2752520 | tf_op jit(solution)/shard_map/ppermute | solution.py:432
  43.5 10.6 %collective-permute-start.15 = (bf16[896,256]{1,0:T(8,128)(2,1)}, bf16[896,256]{1,0:T(8,128)(2,1)}, u32[]{:S(2)}, u32[]{:S(2)}) collective-permute-start(bf16[896,256]{1,0:T(8,128)(2,1)} %get-tuple-element.42.refs_0_.refs_6_), channel_id=1, source_target_pairs={{0,2},{1,3},{2,0},{3,1},{4,6},{5,7},{6,4},{7,5},{8,10},{9,11},{10,... | collective-permute-start | bytes 1376264 | tf_op jit(solution)/shard_map/ppermute | solution.py:436
  44.1 10.6 %collective-permute-start.11 = (bf16[896,256]{1,0:T(8,128)(2,1)S(1)}, bf16[896,256]{1,0:T(8,128)(2,1)S(1)}, u32[]{:S(2)}, u32[]{:S(2)}) collective-permute-start(bf16[896,256]{1,0:T(8,128)(2,1)S(1)} %copy-done.23), channel_id=1, source_target_pairs={{2,4},{3,5},{4,2},{5,3},{10,12},{11,13},{12,10},{13,11},{18,20},{1... | collective-permute-start | bytes 1376264 | tf_op jit(solution)/shard_map/ppermute | solution.py:436
  44.8 23.1 %collective-permute-start.13 = (bf16[896,256]{1,0:T(8,128)(2,1)}, bf16[896,256]{1,0:T(8,128)(2,1)}, u32[]{:S(2)}, u32[]{:S(2)}) collective-permute-start(bf16[896,256]{1,0:T(8,128)(2,1)} %collective-permute-done.10.refs_1_), channel_id=1, source_target_pairs={{2,4},{3,5},{4,2},{5,3},{10,12},{11,13},{12,10},{13,11},{18,20},{1... | collective-permute-start | bytes 1376264 | tf_op jit(solution)/shard_map/ppermute | solution.py:436
  54.1 23.6 %collective-permute-start.16 = (bf16[896,256]{1,0:T(8,128)(2,1)}, bf16[896,256]{1,0:T(8,128)(2,1)S(1)}, u32[]{:S(2)}, u32[]{:S(2)}) collective-permute-start(bf16[896,256]{1,0:T(8,128)(2,1)} %get-tuple-element.42.refs_0_.refs_6_), channel_id=1, source_target_pairs={{2,4},{3,5},{4,2},{5,3},{10,12},{11,13},{12,10},{13,11},{18,20},{1... | collective-permute-start | bytes 1376264 | tf_op jit(solution)/shard_map/ppermute | solution.py:436
  54.8 41.0 %collective-permute-start.3 = (bf16[1,1792,256]{2,1,0:T(8,128)(2,1)}, bf16[1,1792,256]{2,1,0:T(8,128)(2,1)}, u32[]{:S(2)}, u32[]{:S(2)}) collective-permute-start(bf16[1,1792,256]{2,1,0:T(8,128)(2,1)} %slab_sum.13), channel_id=1, source_target_pairs={{0,16},{8,24},{16,0},{24,8},{1,17},{9,25},{17,1},{25,9},{2,18},{10... | collective-permute-start | bytes 2752520 | tf_op jit(solution)/shard_map/ppermute | solution.py:432
  61.0 16.7 %collective-permute-start.18 = (bf16[896,256]{1,0:T(8,128)(2,1)}, bf16[896,256]{1,0:T(8,128)(2,1)}, u32[]{:S(2)}, u32[]{:S(2)}) collective-permute-start(bf16[896,256]{1,0:T(8,128)(2,1)} %collective-permute-done.15.refs_7_), channel_id=1, source_target_pairs={{2,4},{3,5},{4,2},{5,3},{10,12},{11,13},{12,10},{13,11},{18,20},{1... | collective-permute-start | bytes 1376264 | tf_op jit(solution)/shard_map/ppermute | solution.py:436
  69.8 25.2 %collective-permute-start.14 = (bf16[896,256]{1,0:T(8,128)(2,1)S(1)}, bf16[896,256]{1,0:T(8,128)(2,1)S(1)}, u32[]{:S(2)}, u32[]{:S(2)}) collective-permute-start(bf16[896,256]{1,0:T(8,128)(2,1)S(1)} %pick.24), channel_id=1, source_target_pairs={{0,2},{1,3},{2,0},{3,1},{4,6},{5,7},{6,4},{7,5},{8,10},{9,11},{10,... | collective-permute-start | bytes 1376264 | tf_op jit(solution)/shard_map/ppermute | solution.py:436
  77.7 108.5 %copy-start.16 = (bf16[896,256]{1,0:T(8,128)(2,1)}, bf16[896,256]{1,0:T(8,128)(2,1)S(1)}, u32[]{:S(2)}) copy-start(bf16[896,256]{1,0:T(8,128)(2,1)S(1)} %collective-permute-done.16.refs_1_.refs_0_.refs_10_) | copy-start | bytes 1376260
  79.8 18.3 %collective-permute-start.19 = (bf16[896,256]{1,0:T(8,128)(2,1)S(1)}, bf16[896,256]{1,0:T(8,128)(2,1)S(1)}, u32[]{:S(2)}, u32[]{:S(2)}) collective-permute-start(bf16[896,256]{1,0:T(8,128)(2,1)S(1)} %pick.26), channel_id=1, source_target_pairs={{0,2},{1,3},{2,0},{3,1},{4,6},{5,7},{6,4},{7,5},{8,10},{9,11},{10,... | collective-permute-start | bytes 1376264 | tf_op jit(solution)/shard_map/ppermute | solution.py:436
  92.8 44.3 %collective-permute-start.1 = (bf16[1,1792,256]{2,1,0:T(8,128)(2,1)}, bf16[1,1792,256]{2,1,0:T(8,128)(2,1)}, u32[]{:S(2)}, u32[]{:S(2)}) collective-permute-start(bf16[1,1792,256]{2,1,0:T(8,128)(2,1)} %slab_sum.11), channel_id=1, source_target_pairs={{0,16},{8,24},{16,0},{24,8},{1,17},{9,25},{17,1},{25,9},{2,18},{10... | collective-permute-start | bytes 2752520 | tf_op jit(solution)/shard_map/ppermute | solution.py:432
  94.3 8.6 %collective-permute-start.24 = (bf16[896,256]{1,0:T(8,128)(2,1)S(1)}, bf16[896,256]{1,0:T(8,128)(2,1)S(1)}, u32[]{:S(2)}, u32[]{:S(2)}) collective-permute-start(bf16[896,256]{1,0:T(8,128)(2,1)S(1)} %copy-done.11), channel_id=1, source_target_pairs={{2,4},{3,5},{4,2},{5,3},{10,12},{11,13},{12,10},{13,11},{18,20},{1... | collective-permute-start | bytes 1376264 | tf_op jit(solution)/shard_map/ppermute | solution.py:436
  95.0 7.9 %collective-permute-start.26 = (bf16[896,256]{1,0:T(8,128)(2,1)S(1)}, bf16[896,256]{1,0:T(8,128)(2,1)S(1)}, u32[]{:S(2)}, u32[]{:S(2)}) collective-permute-start(bf16[896,256]{1,0:T(8,128)(2,1)S(1)} %collective-permute-done.14.refs_3_.refs_1_), channel_id=1, source_target_pairs={{2,4},{3,5},{4,2},{5,3},{10,12},{11,13},{12,10},{13,11},{18,20},{1... | collective-permute-start | bytes 1376264 | tf_op jit(solution)/shard_map/ppermute | solution.py:436
  95.7 30.0 %collective-permute-start.28 = (bf16[896,256]{1,0:T(8,128)(2,1)S(1)}, bf16[896,256]{1,0:T(8,128)(2,1)S(1)}, u32[]{:S(2)}, u32[]{:S(2)}) collective-permute-start(bf16[896,256]{1,0:T(8,128)(2,1)S(1)} %copy-done.13), channel_id=1, source_target_pairs={{2,4},{3,5},{4,2},{5,3},{10,12},{11,13},{12,10},{13,11},{18,20},{1... | collective-permute-start | bytes 1376264 | tf_op jit(solution)/shard_map/ppermute | solution.py:436
  98.0 98.7 %copy-start.8 = (bf16[896,256]{1,0:T(8,128)(2,1)}, bf16[896,256]{1,0:T(8,128)(2,1)S(1)}, u32[]{:S(2)}) copy-start(bf16[896,256]{1,0:T(8,128)(2,1)S(1)} %collective-permute-done.19.refs_9_.refs_7_) | copy-start | bytes 1376260
  98.0 31.4 %collective-permute-start.30 = (bf16[896,256]{1,0:T(8,128)(2,1)S(1)}, bf16[896,256]{1,0:T(8,128)(2,1)S(1)}, u32[]{:S(2)}, u32[]{:S(2)}) collective-permute-start(bf16[896,256]{1,0:T(8,128)(2,1)S(1)} %collective-permute-done.19.refs_9_.refs_7_), channel_id=1, source_target_pairs={{2,4},{3,5},{4,2},{5,3},{10,12},{11,13},{12,10},{13,11},{18,20},{1... | collective-permute-start | bytes 1376264 | tf_op jit(solution)/shard_map/ppermute | solution.py:436
  105.0 41.4 %collective-permute-start.27 = (bf16[896,256]{1,0:T(8,128)(2,1)S(1)}, bf16[896,256]{1,0:T(8,128)(2,1)S(1)}, u32[]{:S(2)}, u32[]{:S(2)}) collective-permute-start(bf16[896,256]{1,0:T(8,128)(2,1)S(1)} %pick.29), channel_id=1, source_target_pairs={{0,2},{1,3},{2,0},{3,1},{4,6},{5,7},{6,4},{7,5},{8,10},{9,11},{10,... | collective-permute-start | bytes 1376264 | tf_op jit(solution)/shard_map/ppermute | solution.py:436
  124.1 32.3 %collective-permute-start.17 = (bf16[896,256]{1,0:T(8,128)(2,1)}, bf16[896,256]{1,0:T(8,128)(2,1)}, u32[]{:S(2)}, u32[]{:S(2)}) collective-permute-start(bf16[896,256]{1,0:T(8,128)(2,1)} %pick.25), channel_id=1, source_target_pairs={{0,2},{1,3},{2,0},{3,1},{4,6},{5,7},{6,4},{7,5},{8,10},{9,11},{10,... | collective-permute-start | bytes 1376264 | tf_op jit(solution)/shard_map/ppermute | solution.py:436
  125.8 32.3 %collective-permute-start.12 = (bf16[896,256]{1,0:T(8,128)(2,1)}, bf16[896,256]{1,0:T(8,128)(2,1)}, u32[]{:S(2)}, u32[]{:S(2)}) collective-permute-start(bf16[896,256]{1,0:T(8,128)(2,1)} %pick.23), channel_id=1, source_target_pairs={{0,2},{1,3},{2,0},{3,1},{4,6},{5,7},{6,4},{7,5},{8,10},{9,11},{10,... | collective-permute-start | bytes 1376264 | tf_op jit(solution)/shard_map/ppermute | solution.py:436
  129.5 29.3 %collective-permute-start.36 = (bf16[896,256]{1,0:T(8,128)(2,1)S(1)}, bf16[896,256]{1,0:T(8,128)(2,1)S(1)}, u32[]{:S(2)}, u32[]{:S(2)}) collective-permute-start(bf16[896,256]{1,0:T(8,128)(2,1)S(1)} %copy-done.15), channel_id=1, source_target_pairs={{2,4},{3,5},{4,2},{5,3},{10,12},{11,13},{12,10},{13,11},{18,20},{1... | collective-permute-start | bytes 1376264 | tf_op jit(solution)/shard_map/ppermute | solution.py:436
  137.1 27.0 %collective-permute-start.31 = (bf16[896,256]{1,0:T(8,128)(2,1)}, bf16[896,256]{1,0:T(8,128)(2,1)S(1)}, u32[]{:S(2)}, u32[]{:S(2)}) collective-permute-start(bf16[896,256]{1,0:T(8,128)(2,1)} %pick.31), channel_id=1, source_target_pairs={{0,2},{1,3},{2,0},{3,1},{4,6},{5,7},{6,4},{7,5},{8,10},{9,11},{10,... | collective-permute-start | bytes 1376264 | tf_op jit(solution)/shard_map/ppermute | solution.py:436
  146.4 19.3 %collective-permute-start.38 = (bf16[896,256]{1,0:T(8,128)(2,1)S(1)}, bf16[896,256]{1,0:T(8,128)(2,1)}, u32[]{:S(2)}, u32[]{:S(2)}) collective-permute-start(bf16[896,256]{1,0:T(8,128)(2,1)S(1)} %collective-permute-done.27.refs_3_.refs_1_), channel_id=1, source_target_pairs={{2,4},{3,5},{4,2},{5,3},{10,12},{11,13},{12,10},{13,11},{18,20},{1... | collective-permute-start | bytes 1376264 | tf_op jit(solution)/shard_map/ppermute | solution.py:436
  156.4 13.2 %collective-permute-start.40 = (bf16[896,256]{1,0:T(8,128)(2,1)S(1)}, bf16[896,256]{1,0:T(8,128)(2,1)S(1)}, u32[]{:S(2)}, u32[]{:S(2)}) collective-permute-start(bf16[896,256]{1,0:T(8,128)(2,1)S(1)} %copy-done.18), channel_id=1, source_target_pairs={{2,4},{3,5},{4,2},{5,3},{10,12},{11,13},{12,10},{13,11},{18,20},{1... | collective-permute-start | bytes 1376264 | tf_op jit(solution)/shard_map/ppermute | solution.py:436
  158.1 15.4 %collective-permute-start.52 = (bf16[896,256]{1,0:T(8,128)(2,1)}, bf16[896,256]{1,0:T(8,128)(2,1)S(1)}, u32[]{:S(2)}, u32[]{:S(2)}) collective-permute-start(bf16[896,256]{1,0:T(8,128)(2,1)} %get-tuple-element.55.refs_2_.refs_0_.refs_6_.refs_12_), channel_id=1, source_target_pairs={{2,4},{3,5},{4,2},{5,3},{10,12},{11,13},{12,10},{13,11},{18,20},{1... | collective-permute-start | bytes 1376264 | tf_op jit(solution)/shard_map/ppermute | solution.py:436
  158.8 16.7 %collective-permute-start.29 = (bf16[896,256]{1,0:T(8,128)(2,1)S(1)}, bf16[896,256]{1,0:T(8,128)(2,1)S(1)}, u32[]{:S(2)}, u32[]{:S(2)}) collective-permute-start(bf16[896,256]{1,0:T(8,128)(2,1)S(1)} %pick.30), channel_id=1, source_target_pairs={{0,2},{1,3},{2,0},{3,1},{4,6},{5,7},{6,4},{7,5},{8,10},{9,11},{10,... | collective-permute-start | bytes 1376264 | tf_op jit(solution)/shard_map/ppermute | solution.py:436
  164.1 23.9 %collective-permute-start.42 = (bf16[896,256]{1,0:T(8,128)(2,1)S(1)}, bf16[896,256]{1,0:T(8,128)(2,1)S(1)}, u32[]{:S(2)}, u32[]{:S(2)}) collective-permute-start(bf16[896,256]{1,0:T(8,128)(2,1)S(1)} %collective-permute-done.31.refs_9_.refs_7_), channel_id=1, source_target_pairs={{2,4},{3,5},{4,2},{5,3},{10,12},{11,13},{12,10},{13,11},{18,20},{1... | collective-permute-start | bytes 1376264 | tf_op jit(solution)/shard_map/ppermute | solution.py:436
  165.7 24.7 %collective-permute-start.25 = (bf16[896,256]{1,0:T(8,128)(2,1)S(1)}, bf16[896,256]{1,0:T(8,128)(2,1)S(1)}, u32[]{:S(2)}, u32[]{:S(2)}) collective-permute-start(bf16[896,256]{1,0:T(8,128)(2,1)S(1)} %pick.28), channel_id=1, source_target_pairs={{0,2},{1,3},{2,0},{3,1},{4,6},{5,7},{6,4},{7,5},{8,10},{9,11},{10,... | collective-permute-start | bytes 1376264 | tf_op jit(solution)/shard_map/ppermute | solution.py:436
  169.6 25.6 %collective-permute-start.39 = (bf16[896,256]{1,0:T(8,128)(2,1)S(1)}, bf16[896,256]{1,0:T(8,128)(2,1)S(1)}, u32[]{:S(2)}, u32[]{:S(2)}) collective-permute-start(bf16[896,256]{1,0:T(8,128)(2,1)S(1)} %pick.34), channel_id=1, source_target_pairs={{0,2},{1,3},{2,0},{3,1},{4,6},{5,7},{6,4},{7,5},{8,10},{9,11},{10,... | collective-permute-start | bytes 1376264 | tf_op jit(solution)/shard_map/ppermute | solution.py:436
  173.5 25.5 %collective-permute-start.48 = (bf16[896,256]{1,0:T(8,128)(2,1)S(1)}, bf16[896,256]{1,0:T(8,128)(2,1)S(1)}, u32[]{:S(2)}, u32[]{:S(2)}) collective-permute-start(bf16[896,256]{1,0:T(8,128)(2,1)S(1)} %copy-done.21), channel_id=1, source_target_pairs={{2,4},{3,5},{4,2},{5,3},{10,12},{11,13},{12,10},{13,11},{18,20},{1... | collective-permute-start | bytes 1376264 | tf_op jit(solution)/shard_map/ppermute | solution.py:436
  175.5 29.5 %collective-permute-start.41 = (bf16[896,256]{1,0:T(8,128)(2,1)S(1)}, bf16[896,256]{1,0:T(8,128)(2,1)S(1)}, u32[]{:S(2)}, u32[]{:S(2)}) collective-permute-start(bf16[896,256]{1,0:T(8,128)(2,1)S(1)} %pick.35), channel_id=1, source_target_pairs={{0,2},{1,3},{2,0},{3,1},{4,6},{5,7},{6,4},{7,5},{8,10},{9,11},{10,... | collective-permute-start | bytes 1376264 | tf_op jit(solution)/shard_map/ppermute | solution.py:436
  188.1 40.9 %collective-permute-start.21 = (bf16[1792,256]{1,0:T(8,128)(2,1)S(1)}, bf16[1792,256]{1,0:T(8,128)(2,1)S(1)}, u32[]{:S(2)}, u32[]{:S(2)}) collective-permute-start(bf16[1792,256]{1,0:T(8,128)(2,1)S(1)} %pick.27), channel_id=1, source_target_pairs={{0,1},{1,0},{2,3},{3,2},{4,5},{5,4},{6,7},{7,6},{8,9},{9,8},{10,11... | collective-permute-start | bytes 2752520 | tf_op jit(solution)/shard_map/ppermute | solution.py:593
  190.4 24.4 %collective-permute-start.43 = (bf16[896,256]{1,0:T(8,128)(2,1)S(1)}, bf16[896,256]{1,0:T(8,128)(2,1)S(1)}, u32[]{:S(2)}, u32[]{:S(2)}) collective-permute-start(bf16[896,256]{1,0:T(8,128)(2,1)S(1)} %pick.36), channel_id=1, source_target_pairs={{0,2},{1,3},{2,0},{3,1},{4,6},{5,7},{6,4},{7,5},{8,10},{9,11},{10,... | collective-permute-start | bytes 1376264 | tf_op jit(solution)/shard_map/ppermute | solution.py:436
  195.2 22.0 %collective-permute-start.50 = (bf16[896,256]{1,0:T(8,128)(2,1)S(1)}, bf16[896,256]{1,0:T(8,128)(2,1)S(1)}, u32[]{:S(2)}, u32[]{:S(2)}) collective-permute-start(bf16[896,256]{1,0:T(8,128)(2,1)S(1)} %collective-permute-done.39.refs_3_.refs_1_), channel_id=1, source_target_pairs={{2,4},{3,5},{4,2},{5,3},{10,12},{11,13},{12,10},{13,11},{18,20},{1... | collective-permute-start | bytes 1376264 | tf_op jit(solution)/shard_map/ppermute | solution.py:436
  199.0 45.5 %collective-permute-start.33 = (bf16[1792,256]{1,0:T(8,128)(2,1)}, bf16[1792,256]{1,0:T(8,128)(2,1)}, u32[]{:S(2)}, u32[]{:S(2)}) collective-permute-start(bf16[1792,256]{1,0:T(8,128)(2,1)} %pick.32), channel_id=1, source_target_pairs={{0,1},{1,0},{2,3},{3,2},{4,5},{5,4},{6,7},{7,6},{8,9},{9,8},{10,11... | collective-permute-start | bytes 2752520 | tf_op jit(solution)/shard_map/ppermute | solution.py:593
  205.0 19.7 %collective-permute-start.37 = (bf16[896,256]{1,0:T(8,128)(2,1)S(1)}, bf16[896,256]{1,0:T(8,128)(2,1)S(1)}, u32[]{:S(2)}, u32[]{:S(2)}) collective-permute-start(bf16[896,256]{1,0:T(8,128)(2,1)S(1)} %pick.33), channel_id=1, source_target_pairs={{0,2},{1,3},{2,0},{3,1},{4,6},{5,7},{6,4},{7,5},{8,10},{9,11},{10,... | collective-permute-start | bytes 1376264 | tf_op jit(solution)/shard_map/ppermute | solution.py:436
  214.8 21.6 %collective-permute-start.54 = (bf16[896,256]{1,0:T(8,128)(2,1)S(1)}, bf16[896,256]{1,0:T(8,128)(2,1)S(1)}, u32[]{:S(2)}, u32[]{:S(2)}) collective-permute-start(bf16[896,256]{1,0:T(8,128)(2,1)S(1)} %collective-permute-done.43.refs_9_.refs_1_.refs_7_.refs_13_), channel_id=1, source_target_pairs={{2,4},{3,5},{4,2},{5,3},{10,12},{11,13},{12,10},{13,11},{18,20},{1... | collective-permute-start | bytes 1376264 | tf_op jit(solution)/shard_map/ppermute | solution.py:436
  217.1 27.3 %collective-permute-start.49 = (bf16[896,256]{1,0:T(8,128)(2,1)}, bf16[896,256]{1,0:T(8,128)(2,1)}, u32[]{:S(2)}, u32[]{:S(2)}) collective-permute-start(bf16[896,256]{1,0:T(8,128)(2,1)} %pick.38), channel_id=1, source_target_pairs={{0,2},{1,3},{2,0},{3,1},{4,6},{5,7},{6,4},{7,5},{8,10},{9,11},{10,... | collective-permute-start | bytes 1376264 | tf_op jit(solution)/shard_map/ppermute | solution.py:436
  224.7 20.4 %collective-permute-start.51 = (bf16[896,256]{1,0:T(8,128)(2,1)}, bf16[896,256]{1,0:T(8,128)(2,1)}, u32[]{:S(2)}, u32[]{:S(2)}) collective-permute-start(bf16[896,256]{1,0:T(8,128)(2,1)} %pick.39), channel_id=1, source_target_pairs={{0,2},{1,3},{2,0},{3,1},{4,6},{5,7},{6,4},{7,5},{8,10},{9,11},{10,... | collective-permute-start | bytes 1376264 | tf_op jit(solution)/shard_map/ppermute | solution.py:436
  229.9 29.2 %collective-permute-start.53 = (bf16[896,256]{1,0:T(8,128)(2,1)}, bf16[896,256]{1,0:T(8,128)(2,1)S(1)}, u32[]{:S(2)}, u32[]{:S(2)}) collective-permute-start(bf16[896,256]{1,0:T(8,128)(2,1)} %pick.40), channel_id=1, source_target_pairs={{0,2},{1,3},{2,0},{3,1},{4,6},{5,7},{6,4},{7,5},{8,10},{9,11},{10,... | collective-permute-start | bytes 1376264 | tf_op jit(solution)/shard_map/ppermute | solution.py:436
  236.4 34.9 %collective-permute-start.45 = (bf16[1792,256]{1,0:T(8,128)(2,1)}, bf16[1792,256]{1,0:T(8,128)(2,1)S(1)}, u32[]{:S(2)}, u32[]{:S(2)}) collective-permute-start(bf16[1792,256]{1,0:T(8,128)(2,1)} %pick.37), channel_id=1, source_target_pairs={{0,1},{1,0},{2,3},{3,2},{4,5},{5,4},{6,7},{7,6},{8,9},{9,8},{10,11... | collective-permute-start | bytes 2752520 | tf_op jit(solution)/shard_map/ppermute | solution.py:593
  244.4 14.6 %collective-permute-start.20 = (bf16[1,1024,128]{2,1,0:T(8,128)(2,1)S(1)}, bf16[1,1024,128]{2,1,0:T(8,128)(2,1)S(1)}, u32[]{:S(2)}, u32[]{:S(2)}) collective-permute-start(bf16[1,1024,128]{2,1,0:T(8,128)(2,1)S(1)} %get-tuple-element.45), channel_id=1, source_target_pairs={{0,8},{8,0},{16,24},{24,16},{1,9},{9,1},{17,25},{25,17},{2,10},{10... | collective-permute-start | bytes 786440 | tf_op jit(solution)/shard_map/ppermute | solution.py:432
  244.5 15.1 %collective-permute-start.22 = (bf16[1,1024,128]{2,1,0:T(8,128)(2,1)S(1)}, bf16[1,1024,128]{2,1,0:T(8,128)(2,1)S(1)}, u32[]{:S(2)}, u32[]{:S(2)}) collective-permute-start(bf16[1,1024,128]{2,1,0:T(8,128)(2,1)S(1)} %get-tuple-element.47), channel_id=1, source_target_pairs={{0,8},{8,0},{16,24},{24,16},{1,9},{9,1},{17,25},{25,17},{2,10},{10... | collective-permute-start | bytes 786440 | tf_op jit(solution)/shard_map/ppermute | solution.py:432
  245.0 14.6 %collective-permute-start.56 = (bf16[384,256]{1,0:T(8,128)(2,1)S(1)}, bf16[384,256]{1,0:T(8,128)(2,1)S(1)}, u32[]{:S(2)}, u32[]{:S(2)}) collective-permute-start(bf16[384,256]{1,0:T(8,128)(2,1)S(1)} %pick.42), channel_id=1, source_target_pairs={{0,2},{1,3},{2,0},{3,1},{4,6},{5,7},{6,4},{7,5},{8,10},{9,11},{10,... | collective-permute-start | bytes 589832 | tf_op jit(solution)/shard_map/ppermute | solution.py:436
  259.0 10.0 %collective-permute-start.32 = (bf16[1,1024,128]{2,1,0:T(8,128)(2,1)S(1)}, bf16[1,1024,128]{2,1,0:T(8,128)(2,1)S(1)}, u32[]{:S(2)}, u32[]{:S(2)}) collective-permute-start(bf16[1,1024,128]{2,1,0:T(8,128)(2,1)S(1)} %get-tuple-element.51), channel_id=1, source_target_pairs={{0,8},{8,0},{16,24},{24,16},{1,9},{9,1},{17,25},{25,17},{2,10},{10... | collective-permute-start | bytes 786440 | tf_op jit(solution)/shard_map/ppermute | solution.py:432
  259.1 11.1 %collective-permute-start.34 = (bf16[1,1024,128]{2,1,0:T(8,128)(2,1)S(1)}, bf16[1,1024,128]{2,1,0:T(8,128)(2,1)S(1)}, u32[]{:S(2)}, u32[]{:S(2)}) collective-permute-start(bf16[1,1024,128]{2,1,0:T(8,128)(2,1)S(1)} %get-tuple-element.53), channel_id=1, source_target_pairs={{0,8},{8,0},{16,24},{24,16},{1,9},{9,1},{17,25},{25,17},{2,10},{10... | collective-permute-start | bytes 786440 | tf_op jit(solution)/shard_map/ppermute | solution.py:432
  259.6 8.3 %collective-permute-start.55 = (bf16[512,256]{1,0:T(8,128)(2,1)S(1)}, bf16[512,256]{1,0:T(8,128)(2,1)S(1)}, u32[]{:S(2)}, u32[]{:S(2)}) collective-permute-start(bf16[512,256]{1,0:T(8,128)(2,1)S(1)} %pick.41), channel_id=1, source_target_pairs={{0,2},{1,3},{2,0},{3,1},{4,6},{5,7},{6,4},{7,5},{8,10},{9,11},{10,... | collective-permute-start | bytes 786440 | tf_op jit(solution)/shard_map/ppermute | solution.py:436
  259.6 22.4 %collective-permute-start.57 = (bf16[896,256]{1,0:T(8,128)(2,1)S(1)}, bf16[896,256]{1,0:T(8,128)(2,1)S(1)}, u32[]{:S(2)}, u32[]{:S(2)}) collective-permute-start(bf16[896,256]{1,0:T(8,128)(2,1)S(1)} %pick.43), channel_id=1, source_target_pairs={{0,1},{1,0},{2,3},{3,2},{4,5},{5,4},{6,7},{7,6},{8,9},{9,8},{10,11... | collective-permute-start | bytes 1376264 | tf_op jit(solution)/shard_map/ppermute | solution.py:593
  267.9 22.4 %collective-permute-start.23 = (bf16[1024,128]{1,0:T(8,128)(2,1)S(1)}, bf16[1024,128]{1,0:T(8,128)(2,1)S(1)}, u32[]{:S(2)}, u32[]{:S(2)}) collective-permute-start(bf16[1024,128]{1,0:T(8,128)(2,1)S(1)} %fusion.1), channel_id=1, source_target_pairs={{0,16},{8,24},{16,0},{24,8},{1,17},{9,25},{17,1},{25,9},{2,18},{10... | collective-permute-start | bytes 786440 | tf_op jit(solution)/shard_map/ppermute | solution.py:432
  269.0 8.2 %collective-permute-start.59 = (bf16[384,256]{1,0:T(8,128)(2,1)S(1)}, bf16[384,256]{1,0:T(8,128)(2,1)S(1)}, u32[]{:S(2)}, u32[]{:S(2)}) collective-permute-start(bf16[384,256]{1,0:T(8,128)(2,1)S(1)} %pick.45), channel_id=1, source_target_pairs={{0,1},{1,0},{2,3},{3,2},{4,5},{5,4},{6,7},{7,6},{8,9},{9,8},{10,11... | collective-permute-start | bytes 589832 | tf_op jit(solution)/shard_map/ppermute | solution.py:593
  270.2 11.8 %collective-permute-start.58 = (bf16[512,256]{1,0:T(8,128)(2,1)S(1)}, bf16[512,256]{1,0:T(8,128)(2,1)S(1)}, u32[]{:S(2)}, u32[]{:S(2)}) collective-permute-start(bf16[512,256]{1,0:T(8,128)(2,1)S(1)} %pick.44), channel_id=1, source_target_pairs={{0,1},{1,0},{2,3},{3,2},{4,5},{5,4},{6,7},{7,6},{8,9},{9,8},{10,11... | collective-permute-start | bytes 786440 | tf_op jit(solution)/shard_map/ppermute | solution.py:593
  271.3 19.1 %collective-permute-start.44 = (bf16[1,1024,128]{2,1,0:T(8,128)(2,1)S(1)}, bf16[1,1024,128]{2,1,0:T(8,128)(2,1)S(1)}, u32[]{:S(2)}, u32[]{:S(2)}) collective-permute-start(bf16[1,1024,128]{2,1,0:T(8,128)(2,1)S(1)} %get-tuple-element.57), channel_id=1, source_target_pairs={{0,8},{8,0},{16,24},{24,16},{1,9},{9,1},{17,25},{25,17},{2,10},{10... | collective-permute-start | bytes 786440 | tf_op jit(solution)/shard_map/ppermute | solution.py:432
  277.3 13.9 %collective-permute-start.35 = (bf16[1024,128]{1,0:T(8,128)(2,1)S(1)}, bf16[1024,128]{1,0:T(8,128)(2,1)S(1)}, u32[]{:S(2)}, u32[]{:S(2)}) collective-permute-start(bf16[1024,128]{1,0:T(8,128)(2,1)S(1)} %fusion.2), channel_id=1, source_target_pairs={{0,16},{8,24},{16,0},{24,8},{1,17},{9,25},{17,1},{25,9},{2,18},{10... | collective-permute-start | bytes 786440 | tf_op jit(solution)/shard_map/ppermute | solution.py:432
  282.0 8.4 %collective-permute-start.46 = (bf16[1,1024,128]{2,1,0:T(8,128)(2,1)S(1)}, bf16[1,1024,128]{2,1,0:T(8,128)(2,1)S(1)}, u32[]{:S(2)}, u32[]{:S(2)}) collective-permute-start(bf16[1,1024,128]{2,1,0:T(8,128)(2,1)S(1)} %get-tuple-element.59), channel_id=1, source_target_pairs={{0,8},{8,0},{16,24},{24,16},{1,9},{9,1},{17,25},{25,17},{2,10},{10... | collective-permute-start | bytes 786440 | tf_op jit(solution)/shard_map/ppermute | solution.py:432
  289.7 2.3 collective-permute-start.60
  290.6 9.2 %collective-permute-start.47 = (bf16[1024,128]{1,0:T(8,128)(2,1)S(1)}, bf16[1024,128]{1,0:T(8,128)(2,1)S(1)}, u32[]{:S(2)}, u32[]{:S(2)}) collective-permute-start(bf16[1024,128]{1,0:T(8,128)(2,1)S(1)} %fusion.3), channel_id=1, source_target_pairs={{0,16},{8,24},{16,0},{24,8},{1,17},{9,25},{17,1},{25,9},{2,18},{10... | collective-permute-start | bytes 786440 | tf_op jit(solution)/shard_map/ppermute | solution.py:432
  292.1 12.4 %collective-permute-start.61 = (bf16[1024,128]{1,0:T(8,128)(2,1)S(1)}, bf16[1024,128]{1,0:T(8,128)(2,1)S(1)}, u32[]{:S(2)}, u32[]{:S(2)}) collective-permute-start(bf16[1024,128]{1,0:T(8,128)(2,1)S(1)} %fusion.4), channel_id=1, source_target_pairs={{0,16},{8,24},{16,0},{24,8},{1,17},{9,25},{17,1},{25,9},{2,18},{10... | collective-permute-start | bytes 786440 | tf_op jit(solution)/shard_map/ppermute | solution.py:432
  (46 other events, 779.4 us)
